TPU v7x, 256 devices: a whole 4x4x8 slice. The times are simulated.
256 devices in a mesh: gx: 16 (over x_hi, z), gy: 16 (over y, x_lo, core).
Axes of the slice: x: 4 (x_hi: 2, x_lo: 2; x = x_hi * 2 + x_lo), y: 4, z: 8, core: 2. Of those that a mesh axis runs over, the one named last changes fastest.
Arguments:
- positions: float32 [16, 16, 3, 3, 128], P('gx', 'gy'), may hold values from 0 to 10
- velocities: float32 [16, 16, 3, 3, 128], P('gx', 'gy'), may hold values from -6 to 6
- forces: float32 [16, 16, 3, 3, 128], P('gx', 'gy'), may hold values from -6 to 6
- noise: float32 [16, 16, 3, 3, 128], P('gx', 'gy'), may hold values from -6 to 6
- species: int32 [16, 16, 3, 128], P('gx', 'gy'), may hold values from 0 to 5
- counts: int32 [16, 16, 3], P('gx', 'gy'), may hold values from 64 to 128
- pair_list: int32 [16, 16, 3, 13], P('gx', 'gy'), may hold values 0 or 1
- masses: float32 [6], replicated, may hold values from 1 to 4
- embedding: bfloat16 [6, 128], replicated, may hold values from -6 to 6
- radial_one: float32 [8, 128], replicated, may hold values from -0.625 to 0.625
- mix_one: bfloat16 [128, 128], replicated, may hold values from -0.5 to 0.5
- radial_two: bfloat16 [8, 128], replicated, may hold values from -0.75 to 0.75
- mix_two: bfloat16 [128, 128], replicated, may hold values from -0.5 to 0.5
- readout: float32 [128], replicated, may hold values from -1.5 to 1.5
Outputs:
- new_positions: float32 [16, 16, 3, 3, 128], P('gx', 'gy')
- new_velocities: float32 [16, 16, 3, 3, 128], P('gx', 'gy')
- new_forces: float32 [16, 16, 3, 3, 128], P('gx', 'gy')
Inputs may be any that keep to these rules, and one draw needn't show every extreme that they name: `species` holds a species index 0 to 5 for every slot, padding slots included. The first counts[b] slots of block b hold atoms, the others are padding. `pair_list`: entry h of a block flags its pair with the neighbour block at the h-th of the 13 offsets (ox, oy, oz) with entries -1, 0, 1 that follow (0, 0, 0) in lexicographic order.
All inputs are finite; a program needn't handle non-finite values.
Results may differ from a plain program's by a relative error of at most 0.01065.
Values may be sent and summed in bfloat16 or wider, within the bound.
No kernel may reach another device: no remote copies, remote signals or barrier semaphores. Data moves between devices by JAX's collectives and lax.ppermute only.
A program may use at most 128 MiB of HBM per device.

v0:
```python
import math

import jax
import jax.numpy as jnp
from jax import lax
from jax.sharding import PartitionSpec as P

SIDE = 10.0
REACH = 5.0
HALF_STEP = 0.25
DECAY = math.exp(-0.5)


def with_halo(cells, sides, width):
    for axis, dim in sides:
        count = lax.axis_size(axis)
        head = lax.slice_in_dim(cells, 0, width, axis=dim)
        tail = lax.slice_in_dim(cells, cells.shape[dim] - width, cells.shape[dim], axis=dim)
        cells = jnp.concatenate(
            [
                lax.ppermute(tail, axis, [(i, (i + 1) % count) for i in range(count)]),
                cells,
                lax.ppermute(head, axis, [((i + 1) % count, i) for i in range(count)]),
            ],
            axis=dim,
        )
    return cells


def offsets(stencil):
    return (stencil // 9 - 1, stencil // 3 % 3 - 1, stencil % 3 - 1)


def stencil_views(padded):
    width_x = padded.shape[0] - 2
    width_y = padded.shape[1] - 2
    stacked_views = []
    for stencil in range(27):
        step_x, step_y, step_z = offsets(stencil)
        window_view = padded[1 + step_x : 1 + step_x + width_x, 1 + step_y : 1 + step_y + width_y]
        stacked_views.append(jnp.roll(window_view, -step_z, axis=2))
    return jnp.stack(stacked_views)


def pair_frame(stencil, own_pos, near_pos, own_count, near_count, own_list, near_list):
    step_x, step_y, step_z = offsets(stencil)
    displacement = jnp.stack([step_x, step_y, step_z]).astype(jnp.float32) * SIDE
    separation = near_pos[..., :, None, :] + displacement[:, None, None] - own_pos[..., :, :, None]
    scaled = jnp.minimum(jnp.sum(separation * separation, axis=-3) / (REACH * REACH), 1.0)
    slot_ids = jnp.arange(own_pos.shape[-1], dtype=jnp.int32)
    own_live = (slot_ids < own_count[..., None]).astype(jnp.float32)
    near_live = (slot_ids < near_count[..., None]).astype(jnp.float32)
    ahead = jnp.take(own_list, jnp.clip(stencil - 14, 0, 12), axis=-1)
    behind = jnp.take(near_list, jnp.clip(12 - stencil, 0, 12), axis=-1)
    listed = jnp.where(stencil == 13, 1, jnp.where(stencil > 13, ahead, behind)).astype(jnp.float32)
    diagonal_pair = jnp.logical_and(stencil == 13, slot_ids[:, None] == slot_ids[None, :])
    weight = listed[..., None, None] * own_live[..., :, None] * near_live[..., None, :]
    weight = weight * jnp.where(diagonal_pair, 0.0, 1.0).astype(jnp.float32)
    return (separation, scaled, weight)


def radial_terms(scaled, weight, orders):
    wavenumbers = math.pi * jnp.arange(orders, dtype=jnp.int32).astype(jnp.float32)[:, None, None]
    angles = wavenumbers * scaled[..., None, :, :]
    leftover = (1.0 - scaled)[..., None, :, :]
    return weight[..., None, :, :] * leftover * leftover * jnp.cos(angles)


def radial_slope(scaled, weight, orders):
    wavenumbers = math.pi * jnp.arange(orders, dtype=jnp.int32).astype(jnp.float32)[:, None, None]
    angles = wavenumbers * scaled[..., None, :, :]
    leftover = (1.0 - scaled)[..., None, :, :]
    return weight[..., None, :, :] * (
        -2.0 * leftover * jnp.cos(angles) - wavenumbers * leftover * leftover * jnp.sin(angles)
    )


def silu_slope(values):
    sigmoid = jax.nn.sigmoid(values)
    return sigmoid * (1.0 + values * (1.0 - sigmoid))


def force_field(
    positions,
    species,
    counts,
    pair_list,
    embedding,
    radial_one,
    mix_one,
    radial_two,
    mix_two,
    readout,
):
    species_total = embedding.shape[0]
    orders = radial_one.shape[0]
    slot_total = positions.shape[-1]
    highest = lax.Precision.HIGHEST
    species_ids = jnp.arange(species_total, dtype=jnp.int32)
    padded_species, padded_counts, padded_lists = (
        with_halo(species, (("gx", 0), ("gy", 1)), 1),
        with_halo(counts, (("gx", 0), ("gy", 1)), 1),
        with_halo(pair_list, (("gx", 0), ("gy", 1)), 1),
    )
    padded_positions = with_halo(positions, (("gx", 0), ("gy", 1)), 1)
    own_kinds = (species[..., None] == species_ids).astype(jnp.bfloat16)
    near_kinds = (stencil_views(padded_species)[..., None] == species_ids).astype(jnp.bfloat16)
    near_positions = stencil_views(padded_positions)
    near_counts = stencil_views(padded_counts)
    near_lists = stencil_views(padded_lists)
    stencils = jnp.arange(27, dtype=jnp.int32)
    slot_ids = jnp.arange(slot_total, dtype=jnp.int32)
    own_live = (slot_ids < counts[..., None]).astype(jnp.float32)
    base_features = jnp.einsum(
        "xyzas,sc->xyzac", own_kinds, embedding, preferred_element_type=jnp.float32
    ).astype(jnp.bfloat16)
    table_one = radial_one[:, None, :] * embedding.astype(jnp.float32)[None, :, :]
    radial_wide = radial_two.astype(jnp.float32)[:, None, :]

    def build(running, inputs):
        stencil, near_pos, near_count, near_list, near_kind = inputs
        separation, scaled, weight = pair_frame(
            stencil, positions, near_pos, counts, near_count, pair_list, near_list
        )
        radial_basis = radial_terms(scaled, weight, orders).astype(jnp.bfloat16)
        running = running + jnp.einsum(
            "xyzkij,xyzjs->xyzkis", radial_basis, near_kind, preferred_element_type=jnp.float32
        )
        return (running, radial_basis)

    tally_init = jnp.zeros(species.shape[:3] + (orders, slot_total, species_total), jnp.float32)
    tally, basis_stack = lax.scan(
        build, tally_init, (stencils, near_positions, near_counts, near_lists, near_kinds)
    )
    first_message = jnp.einsum("xyzkis,ksc->xyzic", tally, table_one, precision=highest)
    first_gate = jnp.einsum(
        "xyzic,cd->xyzid",
        first_message.astype(jnp.bfloat16),
        mix_one,
        preferred_element_type=jnp.float32,
    )
    hidden = (base_features.astype(jnp.float32) + jax.nn.silu(first_gate)).astype(jnp.bfloat16)
    near_hidden = stencil_views(with_halo(hidden, (("gx", 0), ("gy", 1)), 1))

    def stencil_sum(near_field):
        gathered = jnp.einsum(
            "qxyzkij,qxyzjc->xyzkic", basis_stack, near_field, preferred_element_type=jnp.float32
        )
        return jnp.sum(gathered * radial_wide, axis=-3)

    second_message = stencil_sum(near_hidden)
    second_gate = jnp.einsum(
        "xyzic,cd->xyzid",
        second_message.astype(jnp.bfloat16),
        mix_two,
        preferred_element_type=jnp.float32,
    )
    upstream = own_live[..., None] * readout
    second_grad = (upstream * silu_slope(second_gate)).astype(jnp.bfloat16)
    message_grad = jnp.einsum(
        "xyzid,cd->xyzic", second_grad, mix_two, preferred_element_type=jnp.float32
    ).astype(jnp.bfloat16)
    weighted_grad = (radial_wide * message_grad.astype(jnp.float32)[..., None, :, :]).astype(
        jnp.bfloat16
    )

    def full_pair(
        stencil,
        near_pos,
        near_count,
        near_list,
        near_kind,
        near_feature,
        near_gradient,
        near_project,
        left_side,
        projected,
    ):
        separation, scaled, weight = pair_frame(
            stencil, positions, near_pos, counts, near_count, pair_list, near_list
        )
        right_side = jnp.concatenate([near_feature, near_gradient], axis=-1)
        pair_grad = jnp.einsum(
            "xyzkic,xyzjc->xyzkij", left_side, right_side, preferred_element_type=jnp.float32
        )
        pair_grad = pair_grad + jnp.einsum(
            "xyzksi,xyzjs->xyzkij", projected, near_kind, preferred_element_type=jnp.float32
        )
        pair_grad = pair_grad + jnp.einsum(
            "xyzksj,xyzis->xyzkij", near_project, own_kinds, preferred_element_type=jnp.float32
        )
        strength = jnp.sum(pair_grad * radial_slope(scaled, weight, orders), axis=-3)
        return (strength, separation)

    near_grad = stencil_views(with_halo(message_grad, (("gx", 0), ("gy", 1)), 1))
    first_grad = ((upstream + stencil_sum(near_grad)) * silu_slope(first_gate)).astype(jnp.bfloat16)
    first_message_grad = jnp.einsum(
        "xyzid,cd->xyzic", first_grad, mix_one, preferred_element_type=jnp.float32
    )
    projected = jnp.einsum(
        "xyzic,ksc->xyzksi", first_message_grad, table_one, precision=highest
    ).astype(jnp.bfloat16)
    near_projected = stencil_views(with_halo(projected, (("gx", 0), ("gy", 1)), 1))
    weighted_hidden = (radial_wide * hidden.astype(jnp.float32)[..., None, :, :]).astype(
        jnp.bfloat16
    )
    left_side = jnp.concatenate([weighted_grad, weighted_hidden], axis=-1)

    def gradient_pass(running, inputs):
        (
            stencil,
            near_pos,
            near_count,
            near_list,
            near_kind,
            near_feature,
            near_gradient,
            near_project,
        ) = inputs
        strength, separation = full_pair(
            stencil,
            near_pos,
            near_count,
            near_list,
            near_kind,
            near_feature,
            near_gradient,
            near_project,
            left_side,
            projected,
        )
        return (
            running + jnp.einsum("xyzij,xyzdij->xyzdi", strength, separation, precision=highest),
            None,
        )

    summed, _ = lax.scan(
        gradient_pass,
        jnp.zeros(positions.shape, jnp.float32),
        (
            stencils,
            near_positions,
            near_counts,
            near_lists,
            near_kinds,
            near_hidden,
            near_grad,
            near_projected,
        ),
    )
    return 2.0 / (REACH * REACH) * summed


def on_device(
    positions,
    velocities,
    forces,
    noise,
    species,
    counts,
    pair_list,
    masses,
    embedding,
    radial_one,
    mix_one,
    radial_two,
    mix_two,
    readout,
):
    species_total = masses.shape[0]
    kinds_float = (species[..., None] == jnp.arange(species_total, dtype=jnp.int32)).astype(
        jnp.float32
    )
    atom_mass = jnp.einsum("xyzas,s->xyza", kinds_float, masses, precision=lax.Precision.HIGHEST)[
        ..., None, :
    ]
    half_velocity = velocities + HALF_STEP * forces / atom_mass
    half_position = positions + HALF_STEP * half_velocity
    mixed_velocity = DECAY * half_velocity + jnp.sqrt((1.0 - DECAY * DECAY) / atom_mass) * noise
    new_positions = half_position + HALF_STEP * mixed_velocity
    new_forces = force_field(
        new_positions,
        species,
        counts,
        pair_list,
        embedding,
        radial_one,
        mix_one,
        radial_two,
        mix_two,
        readout,
    )
    new_velocities = mixed_velocity + HALF_STEP * new_forces / atom_mass
    return (new_positions, new_velocities, new_forces)


def solution(mesh):
    in_specs = (
        P("gx", "gy", None, None, None),
        P("gx", "gy", None, None, None),
        P("gx", "gy", None, None, None),
        P("gx", "gy", None, None, None),
        P("gx", "gy", None, None),
        P("gx", "gy", None),
        P("gx", "gy", None, None),
        P(),
        P(),
        P(),
        P(),
        P(),
        P(),
        P(),
    )
    out_specs = (
        P("gx", "gy", None, None, None),
        P("gx", "gy", None, None, None),
        P("gx", "gy", None, None, None),
    )
    return jax.shard_map(
        on_device, mesh=mesh, in_specs=in_specs, out_specs=out_specs, check_vma=False
    )
```

profile of v0, /device:TPU:1, one launch (start us, length us, event | category | flops | bytes accessed | tf_op | source)
XLA Modules:
  0.0 1161.5 jit_solution(77777973173032524)
XLA Ops:
  5.5 6.5 collective-permute-start.1
  54.5 6.3 collective-permute-start.13
  81.0 507.5 %while.31 = (s32[]{:T(128)}, f32[1,1,3,8,128,6]{4,5,3,2,1,0:T(8,128)S(1)}, bf16[27,1,1,3,8,128,128]{6,5,4,3,2,1,0:T(8,128)(2,1)}, s32[1,1,3]{2,1,0:T(1,128)S(1)}...) while((s32[]{:T(128)}, ...), condition=%wide.region_2.4_spmd.clone, body=%wide.region_0.3_spmd.clone.sunk | while | flops 7903965 | bytes 2695410 | solution.py:132
  88.4 6.2 fusion.205
  163.6 6.2 fusion.205
  220.0 6.2 fusion.205
  238.8 6.2 fusion.205
  276.4 6.2 fusion.205
  332.8 6.2 fusion.205
  426.8 6.2 fusion.205
  483.1 6.2 fusion.205
  520.7 6.2 fusion.205
  577.1 6.2 fusion.205
  589.6 13.8 %collective-permute-start.17 = (bf16[1,1,3,128,128]{4,3,2,1,0:T(8,128)(2,1)S(1)}, bf16[1,1,3,128,128]{4,3,2,1,0:T(8,128)(2,1)S(1)}, u32[]{:S(2)}, u32[]{:S(2)}) collective-permute-start(bf16[1,1,3,128,128]{4,3,2,1,0:T(8,128)(2,1)S(1)} %bitcast.889), channel_id=1, source_target_pairs={{16,0},{32,16},{48,32},{64,48},{80,64},{96,80},{112,96},{128,112},... | collective-permute-start | bytes 294920 | tf_op jit(solution)/shard_map/ppermute | solution.py:23
  615.6 11.0 fusion.53
  627.2 6.2 collective-permute-start.21
  636.1 6.5 collective-permute-start.23
  646.6 10.0 fusion.51
  658.0 6.4 collective-permute-start.25
  665.9 6.7 collective-permute-start.27
  675.0 485.6 %while.32 = (s32[]{:T(128)}, f32[1,1,3,3,128]{4,3,2,1,0:T(4,128)S(1)}, f32[27,1,1,3,3,128]{5,4,3,2,1,0:T(4,128)S(1)}, s32[27]{0:T(128)S(1)}, f32[1,1,3,3,128]{4,...) while((s32[]{:T(128)}, ...), condition=%wide.region_8.10_spmd.clone, body=%wide.region_5.9_spmd.clone.sunk | while | flops 216621360 | bytes 12738338 | solution.py:237
  685.7 6.6 fusion.220
  703.7 6.6 fusion.220
  721.7 6.6 fusion.220
  739.7 6.6 fusion.220
  757.7 6.6 fusion.220
  775.7 6.6 fusion.220
  793.6 6.6 fusion.220
  811.6 6.6 fusion.220
  829.6 6.6 fusion.220
  847.6 6.6 fusion.220
  865.6 6.6 fusion.220
  883.6 6.6 fusion.220
  901.6 6.6 fusion.220
  919.6 6.6 fusion.220
  937.5 6.6 fusion.220
  955.5 6.6 fusion.220
  973.5 6.6 fusion.220
  991.5 6.6 fusion.220
  1009.5 6.6 fusion.220
  1027.5 6.6 fusion.220
  1045.5 6.6 fusion.220
  1063.5 6.6 fusion.220
  1081.4 6.6 fusion.220
  1099.4 6.6 fusion.220
  1117.4 6.6 fusion.220
  1135.4 6.6 fusion.220
  1153.4 6.6 fusion.220
  (1426 shorter events, 524.4 us)
Async XLA Ops:
  0.6 626.2 %copy-start = (bf16[128,128]{1,0:T(8,128)(2,1)S(1)}, bf16[128,128]{1,0:T(8,128)(2,1)}, u32[]{:S(2)}) copy-start(bf16[128,128]{1,0:T(8,128)(2,1)} %param.32) | copy-start | bytes 98308
  0.6 80.3 %copy-start.4 = (s32[1,1,3]{2,1,0:T(1,128)S(1)}, s32[1,1,3]{2,1,0:T(1,128)}, u32[]{:S(2)}) copy-start(s32[1,1,3]{2,1,0:T(1,128)} %param.25) | copy-start | bytes 40
  2.9 78.1 %copy-start.1 = (f32[1,1,3,3,128]{4,1,3,2,0:T(1,128)}, f32[1,1,3,3,128]{4,1,3,2,0:T(1,128)S(1)}, u32[]{:S(2)}) copy-start(f32[1,1,3,3,128]{4,1,3,2,0:T(1,128)S(1)} %get-tuple-element.707) | copy-start | bytes 13828
  2.9 72.4 %collective-permute-start = (f32[1,1,3,3,128]{4,1,3,2,0:T(1,128)S(1)}, f32[1,1,3,3,128]{4,1,3,2,0:T(1,128)S(1)}, u32[]{:S(2)}, u32[]{:S(2)}) collective-permute-start(f32[1,1,3,3,128]{4,1,3,2,0:T(1,128)S(1)} %get-tuple-element.707), channel_id=1, source_target_pairs={{0,16},{16,32},{32,48},{48,64},{64,80},{80,96},{96,112},{112,128},... | collective-permute-start | bytes 13832 | tf_op jit(solution)/shard_map/ppermute | solution.py:21
  5.5 69.8 %collective-permute-start.1 = (f32[1,1,3,3,128]{4,1,3,2,0:T(1,128)S(1)}, f32[1,1,3,3,128]{4,1,3,2,0:T(1,128)S(1)}, u32[]{:S(2)}, u32[]{:S(2)}) collective-permute-start(f32[1,1,3,3,128]{4,1,3,2,0:T(1,128)S(1)} %get-tuple-element.707), channel_id=1, source_target_pairs={{16,0},{32,16},{48,32},{64,48},{80,64},{96,80},{112,96},{128,112},... | collective-permute-start | bytes 13832 | tf_op jit(solution)/shard_map/ppermute | solution.py:23
  11.9 42.6 %collective-permute-start.4 = (s32[1,1,3,13]{3,1,2,0:T(1,128)}, s32[1,1,3,13]{3,1,2,0:T(1,128)S(1)}, u32[]{:S(2)}, u32[]{:S(2)}) collective-permute-start(s32[1,1,3,13]{3,1,2,0:T(1,128)} %param.26), channel_id=1, source_target_pairs={{0,16},{16,32},{32,48},{48,64},{64,80},{80,96},{96,112},{112,128},... | collective-permute-start | bytes 476 | tf_op jit(solution)/shard_map/ppermute | solution.py:21
  12.0 49.5 %collective-permute-start.5 = (s32[1,1,3,13]{3,1,2,0:T(1,128)}, s32[1,1,3,13]{3,1,2,0:T(1,128)S(1)}, u32[]{:S(2)}, u32[]{:S(2)}) collective-permute-start(s32[1,1,3,13]{3,1,2,0:T(1,128)} %param.26), channel_id=1, source_target_pairs={{16,0},{32,16},{48,32},{64,48},{80,64},{96,80},{112,96},{128,112},... | collective-permute-start | bytes 476 | tf_op jit(solution)/shard_map/ppermute | solution.py:23
  17.0 11.8 %collective-permute-start.8 = (s32[1,1,3]{2,1,0:T(1,128)}, s32[1,1,3]{2,1,0:T(1,128)S(1)}, u32[]{:S(2)}, u32[]{:S(2)}) collective-permute-start(s32[1,1,3]{2,1,0:T(1,128)} %param.25), channel_id=1, source_target_pairs={{0,16},{16,32},{32,48},{48,64},{64,80},{80,96},{96,112},{112,128},... | collective-permute-start | bytes 44 | tf_op jit(solution)/shard_map/ppermute | solution.py:21
  28.9 6.0 collective-permute-start.9
  34.9 7.4 collective-permute-start.10
  42.3 3.0 collective-permute-start.11
  45.3 28.2 %collective-permute-start.12 = (s32[1,1,3,128]{3,0,2,1:T(1,128)}, s32[1,1,3,128]{3,0,2,1:T(1,128)S(1)}, u32[]{:S(2)}, u32[]{:S(2)}) collective-permute-start(s32[1,1,3,128]{3,0,2,1:T(1,128)} %bitcast.907), channel_id=1, source_target_pairs={{0,16},{16,32},{32,48},{48,64},{64,80},{80,96},{96,112},{112,128},... | collective-permute-start | bytes 4616 | tf_op jit(solution)/shard_map/ppermute | solution.py:21
  54.5 19.1 %collective-permute-start.13 = (s32[1,1,3,128]{3,0,2,1:T(1,128)}, s32[1,1,3,128]{3,0,2,1:T(1,128)S(1)}, u32[]{:S(2)}, u32[]{:S(2)}) collective-permute-start(s32[1,1,3,128]{3,0,2,1:T(1,128)} %bitcast.908), channel_id=1, source_target_pairs={{16,0},{32,16},{48,32},{64,48},{80,64},{96,80},{112,96},{128,112},... | collective-permute-start | bytes 4616 | tf_op jit(solution)/shard_map/ppermute | solution.py:23
  61.5 3.4 collective-permute-start.6
  64.9 5.3 collective-permute-start.7
  74.3 5.0 collective-permute-start.14
  74.6 4.8 collective-permute-start.15
  75.3 5.1 collective-permute-start.2
  76.6 3.9 collective-permute-start.3
  81.0 508.1 %copy-start.6 = (bf16[128,128]{1,0:T(8,128)(2,1)S(1)}, bf16[128,128]{1,0:T(8,128)(2,1)}, u32[]{:S(2)}) copy-start(bf16[128,128]{1,0:T(8,128)(2,1)} %param.30) | copy-start | bytes 98308
  81.0 508.3 %copy-start.9 = (bf16[6,128]{1,0:T(8,128)(2,1)S(1)}, bf16[6,128]{1,0:T(8,128)(2,1)}, u32[]{:S(2)}) copy-start(bf16[6,128]{1,0:T(8,128)(2,1)} %param.28) | copy-start | bytes 4612
  589.5 13.9 %collective-permute-start.16 = (bf16[1,1,3,128,128]{4,3,2,1,0:T(8,128)(2,1)S(1)}, bf16[1,1,3,128,128]{4,3,2,1,0:T(8,128)(2,1)S(1)}, u32[]{:S(2)}, u32[]{:S(2)}) collective-permute-start(bf16[1,1,3,128,128]{4,3,2,1,0:T(8,128)(2,1)S(1)} %bitcast.888), channel_id=1, source_target_pairs={{0,16},{16,32},{32,48},{48,64},{64,80},{80,96},{96,112},{112,128},... | collective-permute-start | bytes 294920 | tf_op jit(solution)/shard_map/ppermute | solution.py:21
  589.6 15.4 %collective-permute-start.17 = (bf16[1,1,3,128,128]{4,3,2,1,0:T(8,128)(2,1)S(1)}, bf16[1,1,3,128,128]{4,3,2,1,0:T(8,128)(2,1)S(1)}, u32[]{:S(2)}, u32[]{:S(2)}) collective-permute-start(bf16[1,1,3,128,128]{4,3,2,1,0:T(8,128)(2,1)S(1)} %bitcast.889), channel_id=1, source_target_pairs={{16,0},{32,16},{48,32},{64,48},{80,64},{96,80},{112,96},{128,112},... | collective-permute-start | bytes 294920 | tf_op jit(solution)/shard_map/ppermute | solution.py:23
  605.1 6.3 collective-permute-start.18
  605.6 9.4 collective-permute-start.19
  615.6 11.0 copy-start.2
  615.6 11.2 copy-start.10
  627.1 8.2 collective-permute-start.20
  627.2 8.1 collective-permute-start.21
  635.4 8.3 collective-permute-start.22
  636.1 8.5 collective-permute-start.23
  645.2 1.5 copy-start.3
  656.7 0.7 copy-start.8
  657.7 8.0 collective-permute-start.24
  658.0 7.7 collective-permute-start.25
  665.8 7.5 collective-permute-start.26
  665.9 7.7 collective-permute-start.27
  674.0 1.0 copy-start.5
  675.0 485.7 %copy-start.7 = (f32[1,1,3,3,128]{4,1,3,2,0:T(1,128)S(1)}, f32[1,1,3,3,128]{4,1,3,2,0:T(1,128)}, u32[]{:S(2)}) copy-start(f32[1,1,3,3,128]{4,1,3,2,0:T(1,128)} %param.23) | copy-start | bytes 13828
where the time goes:
time: 1180 us; the launch traced here: 1160 us
  matrix products  374 us (32%)
  loops' own time  320 us (27%)
  other arithmetic  247 us (21%)
  local copies, waits for them, and re-layouts  119 us (10%)
  starting transfers between devices  85.2 us (7%)
  waiting for transfers between devices  14 us (1%)
    dot_general x27, matrix products, full_pair(): jnp.einsum('xyzksj,xyzis->xyzkij', near_project, own_kinds, preferred_ele...  179 us
    dynamic_update_slice x27, other arithmetic, force_field(): lax.scan(build, tally_init, (stencils, near_positions, near_counts, near_...  166 us
    another operation x1, loops' own time, force_field(): lax.scan(gradient_pass, jnp.zeros(positions.shape, jnp.float32), (stencil...  163 us
    another operation x1, loops' own time, force_field(): lax.scan(build, tally_init, (stencils, near_positions, near_counts, near_...  158 us
    dot_general x27, matrix products, build(): jnp.einsum('xyzkij,xyzjs->xyzkis', radial_basis, near_kind, preferred_ele...  142 us
    ppermute x14, starting transfers between devices, with_halo(): lax.ppermute(head, axis, [((i + 1) % count, i) for i in range(count)])  75.4 us
    dynamic_slice x54, local copies, waits for them, and re-layouts, force_field(): lax.scan(build, tally_init, (stencils, near_positions, near_counts, near_...  32.4 us
    squeeze x27, local copies, waits for them, and re-layouts, force_field(): lax.scan(gradient_pass, jnp.zeros(positions.shape, jnp.float32), (stencil...  25.9 us
  transfers between devices with their start and end apart: 28, of which 13 were waited for; matrix products, arithmetic and copies ran while one was open for 3% of the time, Pallas kernels for 0%

commit v1 on v0

v1 whole, which is shorter than its diff:
```python
import functools
import math

import jax
import jax.numpy as jnp
from jax import lax
from jax.experimental import pallas as pl
from jax.experimental.pallas import tpu as pltpu
from jax.sharding import PartitionSpec as P

SIDE = 10.0
REACH = 5.0
HALF_STEP = 0.25
DECAY = math.exp(-0.5)
FAR = 1.0e4

ORDERS = 8
KINDS = 8
SLOTS = 128
COLUMN = 3
ATOMS = COLUMN * SLOTS
CHANNELS = 128
PARTS = 7
CHUNK = 32

F32 = jnp.float32
BF16 = jnp.bfloat16
HIGHEST = lax.Precision.HIGHEST
ODD = (3.14159265160, -5.16771249, 2.55012026, -0.59890223, 0.07772681)
EVEN = (1.0, -4.93480219, 4.05869615, -1.33500654, 0.23347127, -0.02380946)


def fit_terms():
    import numpy as np

    nodes = 0.5 * np.cos(np.pi * (np.arange(400) + 0.5) / 800)
    odd = np.polynomial.polynomial.polyfit(nodes * nodes, np.sin(np.pi * nodes) / nodes, 4)
    even = np.polynomial.polynomial.polyfit(nodes * nodes, np.cos(np.pi * nodes), 4)
    return tuple(float(value) for value in odd), tuple(float(value) for value in even)


ODD, EVEN = fit_terms()


def horner(terms, square):
    total = terms[-1]
    for term in terms[-2::-1]:
        total = total * square + term
    return total


def turned(row):
    return jnp.broadcast_to(row, (SLOTS, SLOTS)).T


def dot(left, right, contract=((1,), (0,)), precision=None):
    return lax.dot_general(
        left, right, (contract, ((), ())), precision=precision, preferred_element_type=F32
    )


def spread_own(own_ref, own_cols):
    for block in range(COLUMN):
        for axis in range(3):
            own_cols[axis, pl.ds(block * SLOTS, SLOTS), :] = turned(
                own_ref[0, block, axis : axis + 1, :] * (1.0 / REACH)
            )


def mark_diagonal(column, diagonal):
    rows = lax.broadcasted_iota(jnp.int32, (SLOTS, SLOTS), 0)
    lanes = lax.broadcasted_iota(jnp.int32, (SLOTS, SLOTS), 1)
    hit = jnp.logical_and(rows == lanes, column == 4)
    diagonal[...] = jnp.where(hit, FAR * FAR, 0.0)


def offset_z(block, near):
    return (near - block + 1) % 3 - 1


def near_rows(lists_ref, near_ref, column, block, near):
    step_x = column // 3 - 1
    step_y = column % 3 - 1
    step_z = offset_z(block, near)
    stencil = column * 3 + step_z + 1
    ahead = lists_ref[4, block, jnp.clip(stencil - 14, 0, 12)]
    behind = lists_ref[column, near, jnp.clip(12 - stencil, 0, 12)]
    listed = jnp.where(stencil == 13, 1.0, jnp.where(stencil > 13, ahead, behind))
    slots = lax.broadcasted_iota(jnp.int32, (1, SLOTS), 1).astype(F32)
    live = slots < near_ref[0, near, 4:5, :]
    x = (near_ref[0, near, 0:1, :] + SIDE * step_x.astype(F32)) * (1.0 / REACH)
    y = (near_ref[0, near, 1:2, :] + SIDE * step_y.astype(F32)) * (1.0 / REACH)
    z = (near_ref[0, near, 2:3, :] + SIDE * step_z) * (1.0 / REACH)
    x = jnp.where(jnp.logical_and(live, listed > 0.5), x, FAR)
    return x, y, z


def left_over(rows, own_cols, diagonal, block, near, start):
    span = pl.ds(block * SLOTS + start, CHUNK)
    dx = rows[0] - own_cols[0, span, :]
    dy = rows[1] - own_cols[1, span, :]
    dz = rows[2] - own_cols[2, span, :]
    square = dx * dx + dy * dy + dz * dz
    if near == block:
        square = square + diagonal[pl.ds(start, CHUNK), :]
    return jnp.maximum(1.0 - square, 0.0), (dx, dy, dz)


def species_features(near_ref, embedding, near):
    kinds = turned(near_ref[0, near, 3:4, :])
    lanes = lax.broadcasted_iota(jnp.int32, (SLOTS, SLOTS), 1).astype(F32)
    one_hot = jnp.where(kinds == lanes, 1.0, 0.0).astype(BF16)
    return dot(one_hot, embedding).astype(BF16)


def basis_kernel(
    lists_ref, own_ref, near_ref, embedding_ref, radial_ref, mix_ref,
    basis_ref, hidden_ref, gate_ref,
    own_cols, diagonal, message, base, features,
):
    column = pl.program_id(0)

    @pl.when(column == 0)
    def _():
        spread_own(own_ref, own_cols)
        message[...] = jnp.zeros_like(message)
        for block in range(COLUMN):
            base[pl.ds(block * SLOTS, SLOTS), :] = species_features(
                own_ref, embedding_ref[...], block
            )

    mark_diagonal(column, diagonal)
    for block in range(COLUMN):
        for near in range(COLUMN):
            rows = near_rows(lists_ref, near_ref, column, block, near)
            for start in range(0, SLOTS, CHUNK):
                left, _ = left_over(rows, own_cols, diagonal, block, near, start)
                middle = left - 0.5
                cosine = middle * horner(ODD, middle * middle)
                twice = cosine + cosine
                last = left * left
                now = last * cosine
                span = (pl.ds(block * SLOTS + start, CHUNK), pl.ds(near * SLOTS, SLOTS))
                basis_ref[0, 0, span[0], span[1]] = last.astype(BF16)
                basis_ref[0, 1, span[0], span[1]] = now.astype(BF16)
                for order in range(2, ORDERS):
                    last, now = now, twice * now - last
                    basis_ref[0, order, span[0], span[1]] = now.astype(BF16)
    for near in range(COLUMN):
        features[pl.ds(near * SLOTS, SLOTS), :] = species_features(
            near_ref, embedding_ref[...], near
        )
    total = message[...]
    for order in range(ORDERS):
        total = total + radial_ref[order : order + 1, :] * dot(basis_ref[0, order], features[...])
    message[...] = total

    @pl.when(column == 8)
    def _():
        gate = dot(message[...].astype(BF16), mix_ref[...])
        gate_ref[...] = gate
        hidden_ref[...] = (base[...].astype(F32) + gate * jax.nn.sigmoid(gate)).astype(BF16)


def silu_slope(values):
    sigmoid = jax.nn.sigmoid(values)
    return sigmoid * (1.0 + values * (1.0 - sigmoid))


def upstream_of(counts_ref, readout_ref):
    slots = lax.broadcasted_iota(jnp.int32, (SLOTS, CHANNELS), 0)
    readout = jnp.broadcast_to(readout_ref[...], (SLOTS, CHANNELS))
    return jnp.concatenate(
        [jnp.where(slots < counts_ref[block], readout, 0.0) for block in range(COLUMN)], axis=0
    )


def gather_message(basis_ref, field_ref, radial_ref, message):
    @pl.when(pl.program_id(0) == 0)
    def _():
        message[...] = jnp.zeros_like(message)

    total = message[...]
    for order in range(ORDERS):
        total = total + radial_ref[order : order + 1, :] * dot(basis_ref[0, order], field_ref[0])
    message[...] = total


def second_kernel(
    counts_ref, basis_ref, hidden_ref, radial_ref, mix_ref, readout_ref, grad_ref, message
):
    gather_message(basis_ref, hidden_ref, radial_ref, message)

    @pl.when(pl.program_id(0) == 8)
    def _():
        gate = dot(message[...].astype(BF16), mix_ref[...])
        second = (upstream_of(counts_ref, readout_ref) * silu_slope(gate)).astype(BF16)
        grad_ref[...] = dot(second, mix_ref[...], ((1,), (1,))).astype(BF16)


def first_kernel(
    counts_ref, basis_ref, grad_ref, radial_ref, mix_ref, readout_ref, gate_ref, table_ref,
    projected_ref, message,
):
    gather_message(basis_ref, grad_ref, radial_ref, message)

    @pl.when(pl.program_id(0) == 8)
    def _():
        hidden_grad = upstream_of(counts_ref, readout_ref) + message[...]
        first = (hidden_grad * silu_slope(gate_ref[...])).astype(BF16)
        message_grad = dot(first, mix_ref[...], ((1,), (1,)))
        projected_ref[...] = dot(
            table_ref[...], message_grad, ((1,), (1,)), HIGHEST
        ).astype(BF16)


def split(values):
    high = values.astype(BF16)
    return high, (values - high.astype(F32)).astype(BF16)


def slope_kernel(
    lists_ref, own_ref, near_ref, slope_ref, kind_ref, own_cols, diagonal, table
):
    column = pl.program_id(0)

    @pl.when(column == 0)
    def _():
        spread_own(own_ref, own_cols)
        kind_ref[...] = jnp.zeros_like(kind_ref)

    mark_diagonal(column, diagonal)
    for block in range(COLUMN):
        for near in range(COLUMN):
            rows = near_rows(lists_ref, near_ref, column, block, near)
            for start in range(0, SLOTS, CHUNK):
                left, _ = left_over(rows, own_cols, diagonal, block, near, start)
                middle = left - 0.5
                square = middle * middle
                cosine = middle * horner(ODD, square)
                sine = horner(EVEN, square)
                twice = cosine + cosine
                last_a = -2.0 * left
                now_a = last_a * cosine
                now_b = (left * left) * (sine * -math.pi)
                last_b = None
                span = (pl.ds(block * SLOTS + start, CHUNK), pl.ds(near * SLOTS, SLOTS))
                slope_ref[0, 0, span[0], span[1]] = last_a.astype(BF16)
                slope_ref[0, 1, span[0], span[1]] = (now_a + now_b).astype(BF16)
                for order in range(2, ORDERS):
                    last_a, now_a = now_a, twice * now_a - last_a
                    if last_b is None:
                        last_b, now_b = now_b, twice * now_b
                    else:
                        last_b, now_b = now_b, twice * now_b - last_b
                    slope_ref[0, order, span[0], span[1]] = (
                        now_a + float(order) * now_b
                    ).astype(BF16)
    for block in range(COLUMN):
        for near in range(COLUMN):
            coordinates = true_rows(near_ref, column, block, near)
            one_hot = kind_rows(near_ref, near)
            fill_table(table, one_hot, coordinates, near)
        for order in range(ORDERS):
            kind_ref[order, pl.ds(block * SLOTS, SLOTS), :] += dot(
                slope_ref[0, order, pl.ds(block * SLOTS, SLOTS), :], table[...], ((1,), (1,))
            )


def true_rows(near_ref, column, block, near):
    steps = (
        (column // 3 - 1).astype(F32),
        (column % 3 - 1).astype(F32),
        float(offset_z(block, near)),
    )
    return [
        (near_ref[0, near, axis : axis + 1, :] + SIDE * steps[axis]) * (1.0 / REACH)
        for axis in range(3)
    ]


def kind_rows(near_ref, near):
    kinds = lax.broadcasted_iota(jnp.int32, (KINDS, SLOTS), 0).astype(F32)
    return jnp.where(near_ref[0, near, 3:4, :] == kinds, 1.0, 0.0)


def fill_table(table, values, coordinates, near):
    pieces = [values.astype(BF16)]
    for axis in range(3):
        pieces.extend(split(values * coordinates[axis]))
    pieces.append(jnp.zeros((SLOTS - KINDS * PARTS, SLOTS), BF16))
    pieces = [piece.astype(F32) for piece in pieces]
    table[:, pl.ds(near * SLOTS, SLOTS)] = jnp.concatenate(pieces, axis=0).astype(BF16)


def pair_kernel(
    lists_ref, own_ref, near_ref, slope_ref, near_hidden_ref, near_grad_ref, hidden_ref, grad_ref,
    radial_ref, force_ref, own_cols, left_side, right_side,
):
    column = pl.program_id(0)

    @pl.when(column == 0)
    def _():
        spread_own(own_ref, own_cols)
        force_ref[...] = jnp.zeros_like(force_ref)
        for order in range(ORDERS):
            radial = radial_ref[order : order + 1, :]
            left_side[order, :, 0:CHANNELS] = (radial * grad_ref[0].astype(F32)).astype(BF16)
            left_side[order, :, CHANNELS : 2 * CHANNELS] = (
                radial * hidden_ref[0].astype(F32)
            ).astype(BF16)

    right_side[:, 0:CHANNELS] = near_hidden_ref[0]
    right_side[:, CHANNELS : 2 * CHANNELS] = near_grad_ref[0]
    for block in range(COLUMN):
        span = pl.ds(block * SLOTS, SLOTS)
        strength = jnp.zeros((SLOTS, ATOMS), F32)
        for order in range(ORDERS):
            pair = dot(left_side[order, span, :], right_side[...], ((1,), (1,)))
            strength = strength + pair * slope_ref[0, order, span, :].astype(F32)
        for near in range(COLUMN):
            rows = true_rows(near_ref, column, block, near)
            part = strength[:, near * SLOTS : (near + 1) * SLOTS]
            for axis in range(3):
                force_ref[axis, span, :] += part * (rows[axis] - own_cols[axis, span, :])


def last_kernel(
    counts_ref, slope_ref, projected_ref, own_projected_ref, own_ref, near_ref, force_ref,
    kind_ref, mixed_ref, mass_ref, new_force_ref, new_velocity_ref, own_cols, table, near_kind,
):
    column = pl.program_id(0)

    @pl.when(column == 0)
    def _():
        spread_own(own_ref, own_cols)
        near_kind[...] = jnp.zeros_like(near_kind)

    for block in range(COLUMN):
        span = pl.ds(block * SLOTS, SLOTS)
        total = near_kind[span, :]
        for order in range(ORDERS):
            for near in range(COLUMN):
                values = projected_ref[
                    0, order * KINDS : (order + 1) * KINDS, near * SLOTS : (near + 1) * SLOTS
                ].astype(F32)
                fill_table(table, values, true_rows(near_ref, column, block, near), near)
            total = total + dot(slope_ref[0, order, span, :], table[...], ((1,), (1,)))
        near_kind[span, :] = total

    @pl.when(column == 8)
    def _():
        lanes = lax.broadcasted_iota(jnp.int32, (SLOTS, SLOTS), 1)
        lane_kind = (lanes % KINDS).astype(F32)
        part = lanes // KINDS
        inner = lax.broadcasted_iota(jnp.int32, (ORDERS * KINDS, SLOTS), 0)
        outer = lax.broadcasted_iota(jnp.int32, (ORDERS * KINDS, SLOTS), 1) % KINDS
        slots = lax.broadcasted_iota(jnp.int32, (1, SLOTS), 1)
        for block in range(COLUMN):
            span = pl.ds(block * SLOTS, SLOTS)
            kinds = turned(own_ref[0, block, 3:4, :])
            total = jnp.where(kinds == lane_kind, near_kind[span, :], 0.0)
            own = own_projected_ref[0, :, span]
            for order in range(ORDERS):
                pick = jnp.where(inner == outer + order * KINDS, 1.0, 0.0).astype(BF16)
                spread = dot(own, pick, ((0,), (0,)))
                total = total + spread * kind_ref[order, span, :]
            for axis in range(3):
                here = jnp.logical_or(part == 1 + 2 * axis, part == 2 + 2 * axis)
                factor = jnp.where(here, 1.0, jnp.where(part == 0, -own_cols[axis, span, :], 0.0))
                lanes_force = force_ref[axis, span, :] + total * factor
                summed = jnp.sum(lanes_force.T, axis=0, keepdims=True)
                live = slots < counts_ref[block]
                force = jnp.where(live, summed * (2.0 / REACH), 0.0)
                new_force_ref[block, axis : axis + 1, :] = force
                new_velocity_ref[block, axis : axis + 1, :] = (
                    mixed_ref[block, axis : axis + 1, :]
                    + HALF_STEP * force / mass_ref[block : block + 1, :]
                )


def neighbours(cell):
    count_x, count_y = lax.axis_size("gx"), lax.axis_size("gy")
    row = jnp.stack(
        [
            lax.ppermute(cell, "gy", [(i, (i + 1) % count_y) for i in range(count_y)]),
            cell,
            lax.ppermute(cell, "gy", [((i + 1) % count_y, i) for i in range(count_y)]),
        ]
    )
    return jnp.concatenate(
        [
            lax.ppermute(row, "gx", [(i, (i + 1) % count_x) for i in range(count_x)]),
            row,
            lax.ppermute(row, "gx", [((i + 1) % count_x, i) for i in range(count_x)]),
        ]
    )


SMEM = pl.BlockSpec(memory_space=pltpu.SMEM)


def whole(*shape):
    return pl.BlockSpec(shape, lambda column: (0,) * len(shape))


def at_column(*shape):
    return pl.BlockSpec((1,) + shape, lambda column: (column,) + (0,) * len(shape))


def at_centre(*shape):
    return pl.BlockSpec((1,) + shape, lambda column: (4,) + (0,) * len(shape))


def call(kernel, name, out_shape, in_specs, out_specs, scratch, flops, bytes_accessed):
    return pl.pallas_call(
        kernel,
        name=name,
        out_shape=out_shape,
        grid=(9,),
        in_specs=in_specs,
        out_specs=out_specs,
        scratch_shapes=scratch,
        cost_estimate=pl.CostEstimate(
            flops=flops, bytes_accessed=bytes_accessed, transcendentals=0
        ),
        compiler_params=pltpu.CompilerParams(dimension_semantics=("arbitrary",)),
    )


def shape_of(*shape, kind=F32):
    return jax.ShapeDtypeStruct(shape, kind)


PAIR_BYTES = 9 * ORDERS * ATOMS * ATOMS * 2
PAIR_FLOPS = 9 * ORDERS * ATOMS * ATOMS * CHANNELS * 2


def force_field(
    positions, species, counts, pair_list, embedding, radial_one, mix_one, radial_two, mix_two,
    readout, mixed_velocity, atom_mass,
):
    geometry = jnp.concatenate(
        [
            positions,
            species.astype(F32)[:, None, :],
            jnp.broadcast_to(counts.astype(F32)[:, None, None], (COLUMN, 1, SLOTS)),
            jnp.pad(pair_list.astype(F32)[:, None, :], ((0, 0), (0, 0), (0, SLOTS - 13))),
            jnp.zeros((COLUMN, 2, SLOTS), F32),
        ],
        axis=1,
    )
    near_geometry = neighbours(geometry)
    lists = near_geometry[:, :, 5, :13]
    kinds = embedding.shape[0]
    wide_embedding = jnp.pad(embedding, ((0, SLOTS - kinds), (0, 0)))
    table = (
        radial_one[:, None, :]
        * jnp.pad(embedding.astype(F32), ((0, KINDS - kinds), (0, 0)))[None, :, :]
    ).reshape(ORDERS * KINDS, CHANNELS)
    radial_wide = radial_two.astype(F32)
    readout_row = readout[None, :]

    cols = pltpu.VMEM((3, ATOMS, SLOTS), F32)
    message = pltpu.VMEM((ATOMS, CHANNELS), F32)
    square = pltpu.VMEM((SLOTS, SLOTS), F32)
    pairs = (ORDERS, ATOMS, ATOMS)
    geometry_specs = [SMEM, at_centre(COLUMN, 8, SLOTS), at_column(COLUMN, 8, SLOTS)]

    basis, hidden, first_gate = call(
        basis_kernel,
        "basis",
        (
            shape_of(9, *pairs, kind=BF16),
            shape_of(ATOMS, CHANNELS, kind=BF16),
            shape_of(ATOMS, CHANNELS),
        ),
        geometry_specs + [whole(SLOTS, CHANNELS), whole(ORDERS, CHANNELS), whole(CHANNELS, CHANNELS)],
        (at_column(*pairs), whole(ATOMS, CHANNELS), whole(ATOMS, CHANNELS)),
        [
            cols, square, message, pltpu.VMEM((ATOMS, CHANNELS), BF16),
            pltpu.VMEM((ATOMS, CHANNELS), BF16),
        ],
        PAIR_FLOPS,
        PAIR_BYTES,
    )(lists, near_geometry, near_geometry, wide_embedding, radial_one, mix_one)
    near_hidden = neighbours(hidden)

    slope, kind_sums = call(
        slope_kernel,
        "slope",
        (shape_of(9, *pairs, kind=BF16), shape_of(ORDERS, ATOMS, SLOTS)),
        geometry_specs,
        (at_column(*pairs), whole(ORDERS, ATOMS, SLOTS)),
        [cols, square, pltpu.VMEM((SLOTS, ATOMS), BF16)],
        PAIR_FLOPS,
        PAIR_BYTES,
    )(lists, near_geometry, near_geometry)

    message_grad = call(
        second_kernel,
        "second",
        shape_of(ATOMS, CHANNELS, kind=BF16),
        [
            SMEM, at_column(*pairs), at_column(ATOMS, CHANNELS), whole(ORDERS, CHANNELS),
            whole(CHANNELS, CHANNELS), whole(1, CHANNELS),
        ],
        whole(ATOMS, CHANNELS),
        [message],
        PAIR_FLOPS,
        PAIR_BYTES,
    )(counts, basis, near_hidden, radial_wide, mix_two, readout_row)
    near_grad = neighbours(message_grad)

    projected = call(
        first_kernel,
        "first",
        shape_of(ORDERS * KINDS, ATOMS, kind=BF16),
        [
            SMEM, at_column(*pairs), at_column(ATOMS, CHANNELS), whole(ORDERS, CHANNELS),
            whole(CHANNELS, CHANNELS), whole(1, CHANNELS), whole(ATOMS, CHANNELS),
            whole(ORDERS * KINDS, CHANNELS),
        ],
        whole(ORDERS * KINDS, ATOMS),
        [message],
        PAIR_FLOPS,
        PAIR_BYTES,
    )(counts, basis, near_grad, radial_wide, mix_one, readout_row, first_gate, table)
    near_projected = neighbours(projected)

    partial_force = call(
        pair_kernel,
        "pair",
        shape_of(3, ATOMS, SLOTS),
        geometry_specs
        + [
            at_column(*pairs), at_column(ATOMS, CHANNELS), at_column(ATOMS, CHANNELS),
            at_centre(ATOMS, CHANNELS), at_centre(ATOMS, CHANNELS), whole(ORDERS, CHANNELS),
        ],
        whole(3, ATOMS, SLOTS),
        [
            cols, pltpu.VMEM((ORDERS, ATOMS, 2 * CHANNELS), BF16),
            pltpu.VMEM((ATOMS, 2 * CHANNELS), BF16),
        ],
        2 * PAIR_FLOPS,
        PAIR_BYTES,
    )(
        lists, near_geometry, near_geometry, slope, near_hidden, near_grad, near_hidden, near_grad,
        radial_wide,
    )

    return call(
        last_kernel,
        "last",
        (shape_of(COLUMN, 3, SLOTS), shape_of(COLUMN, 3, SLOTS)),
        [
            SMEM, at_column(*pairs), at_column(ORDERS * KINDS, ATOMS),
            at_centre(ORDERS * KINDS, ATOMS), at_centre(COLUMN, 8, SLOTS),
            at_column(COLUMN, 8, SLOTS), whole(3, ATOMS, SLOTS), whole(ORDERS, ATOMS, SLOTS),
            whole(COLUMN, 3, SLOTS), whole(COLUMN, SLOTS),
        ],
        (whole(COLUMN, 3, SLOTS), whole(COLUMN, 3, SLOTS)),
        [cols, pltpu.VMEM((SLOTS, ATOMS), BF16), pltpu.VMEM((ATOMS, SLOTS), F32)],
        PAIR_FLOPS,
        PAIR_BYTES,
    )(
        counts, slope, near_projected, near_projected, near_geometry, near_geometry, partial_force,
        kind_sums, mixed_velocity, atom_mass,
    )


def on_device(
    positions, velocities, forces, noise, species, counts, pair_list, masses, embedding,
    radial_one, mix_one, radial_two, mix_two, readout,
):
    positions, velocities, forces, noise, species, counts, pair_list = (
        value[0, 0]
        for value in (positions, velocities, forces, noise, species, counts, pair_list)
    )
    atom_mass = jnp.zeros(species.shape, F32)
    for kind in range(masses.shape[0]):
        atom_mass = jnp.where(species == kind, masses[kind], atom_mass)
    wide_mass = atom_mass[:, None, :]
    half_velocity = velocities + HALF_STEP * forces / wide_mass
    half_position = positions + HALF_STEP * half_velocity
    mixed_velocity = DECAY * half_velocity + jnp.sqrt((1.0 - DECAY * DECAY) / wide_mass) * noise
    new_positions = half_position + HALF_STEP * mixed_velocity
    new_forces, new_velocities = force_field(
        new_positions, species, counts, pair_list, embedding, radial_one, mix_one, radial_two,
        mix_two, readout, mixed_velocity, atom_mass,
    )
    return tuple(value[None, None] for value in (new_positions, new_velocities, new_forces))


def solution(mesh):
    split_spec = P("gx", "gy")
    return jax.shard_map(
        on_device,
        mesh=mesh,
        in_specs=(split_spec,) * 7 + (P(),) * 7,
        out_specs=(split_spec,) * 3,
        check_vma=False,
    )
```

time: 1180 us -> 194 us (0.16); the launches traced: 1160 us -> 192 us
  matrix products: 374 us -> 0 us
  loops' own time: 320 us -> 0 us
  other arithmetic: 247 us -> 12.4 us
  local copies, waits for them, and re-layouts: 119 us -> 11.5 us
  Pallas kernels: 0 us -> 107 us
  starting transfers between devices: 85.2 us -> 43.6 us
    dot_general x117 -> x0, matrix products: 374 us -> none  [the longest x27 179 us: full_pair(): jnp.einsum('xyzksj,xyzis->xyzkij', near_project, own_kinds, preferred_ele...]
    another operation x2 -> x0, loops' own time: 320 us -> none  [the longest x1 163 us: force_field(): lax.scan(gradient_pass, jnp.zeros(positions.shape, jnp.float32), (stencil...]
    dynamic_update_slice x27 -> x0, other arithmetic: 166 us -> none  [force_field(): lax.scan(build, tally_init, (stencils, near_positions, near_counts, near_...]
    pallas_call x0 -> x6, Pallas kernels: none -> 107 us  [the longest x1 25.7 us: force_field(): call(slope_kernel, 'slope', (shape_of(9, *pairs, kind=BF16), shape_of(ORD...]
    dynamic_slice x81 -> x0, local copies, waits for them, and re-layouts: 53.4 us -> none  [the longest x54 32.4 us: force_field(): lax.scan(build, tally_init, (stencils, near_positions, near_counts, near_...]
    ppermute x28 -> x16, starting transfers between devices: 85.2 us -> 43.6 us  [the longest x4 22.5 us: neighbours(): lax.ppermute(row, 'gx', [((i + 1) % count_x, i) for i in range(count_x)])]
    squeeze x81 -> x0, local copies, waits for them, and re-layouts: 26.5 us -> none  [the longest x27 25.9 us: force_field(): lax.scan(gradient_pass, jnp.zeros(positions.shape, jnp.float32), (stencil...]
    mul x299 -> x1, other arithmetic: 17.8 us -> 0.61 us  [force_field(): radial_one[:, None, :]]
  transfers between devices with their start and end apart: 28 -> 16, of which waited for: 13 -> 11; matrix products, arithmetic and copies ran while one was open for 3% -> 3% of each run, Pallas kernels for 0% -> 23%
where the time goes in v1:
time: 194 us; the launch traced here: 192 us
  Pallas kernels  107 us (55%)
  starting transfers between devices  43.6 us (22%)
  waiting for transfers between devices  16.4 us (8%)
  other arithmetic  12.4 us (6%)
  local copies, waits for them, and re-layouts  11.5 us (6%)
    pallas_call x1, Pallas kernels, force_field(): call(slope_kernel, 'slope', (shape_of(9, *pairs, kind=BF16), shape_of(ORD...  25.7 us
    ppermute x4, starting transfers between devices, neighbours(): lax.ppermute(row, 'gx', [((i + 1) % count_x, i) for i in range(count_x)])  22.5 us
    pallas_call x1, Pallas kernels, force_field(): call(basis_kernel, 'basis', (shape_of(9, *pairs, kind=BF16), shape_of(ATO...  19.4 us
    ppermute x4, starting transfers between devices, neighbours(): lax.ppermute(cell, 'gy', [((i + 1) % count_y, i) for i in range(count_y)])  19.2 us
    pallas_call x1, Pallas kernels, force_field(): call(pair_kernel, 'pair', shape_of(3, ATOMS, SLOTS), geometry_specs + [at...  18.3 us
    pallas_call x1, Pallas kernels, force_field(): call(last_kernel, 'last', (shape_of(COLUMN, 3, SLOTS), shape_of(COLUMN, 3...  16.8 us
    pallas_call x1, Pallas kernels, force_field(): call(first_kernel, 'first', shape_of(ORDERS * KINDS, ATOMS, kind=BF16), [...  13.8 us
    pallas_call x1, Pallas kernels, force_field(): call(second_kernel, 'second', shape_of(ATOMS, CHANNELS, kind=BF16), [SMEM...  13.5 us
  transfers between devices with their start and end apart: 16, of which 11 were waited for; matrix products, arithmetic and copies ran while one was open for 3% of the time, Pallas kernels for 23%

profile of v1, /device:TPU:1, one launch (start us, length us, event | category | flops | bytes accessed | tf_op | source)
XLA Modules:
  0.0 192.3 jit_solution(6227809438079822774)
XLA Ops:
  0.7 0.7 bitcast_convert_fusion.1
  1.4 0.7 convert_bitcast_fusion
  2.1 0.7 fusion.5
  2.8 1.5 fusion.7
  4.3 4.4 %divide_sqrt_fusion = (f32[3,128]{1,0:T(4,128)S(1)}, f32[3,128]{1,0:T(4,128)S(1)}) fusion(f32[]{:T(128)} %bitcast.5, f32[]{:T(128)} %bitcast.4, f32[]{:T(128)} %bitcast.3, f32[]{:T(128)} %bitcast.2, f32[]{:T(128)} %bitcast.1, f32[]{:T(128)} %bitcast, s32[1,1,3,128]{3,1,2,0:T(1,128)} %param.18), kind=kLoop, calls=%fused_computation.46 | loop fusion | flops 4992 | bytes 4632 | tf_op jit(solution)/shard_map/sqrt | solution.py:586
  8.7 1.3 fusion.1
  10.2 3.3 %collective-permute-start.1 = (f32[3,8,128]{2,1,0:T(8,128)S(1)}, f32[3,8,128]{2,1,0:T(8,128)S(1)}, u32[]{:S(2)}, u32[]{:S(2)}) collective-permute-start(f32[3,8,128]{2,1,0:T(8,128)S(1)} %concatenate.19), channel_id=1, source_target_pairs={{1,0},{2,1},{3,2},{4,3},{5,4},{6,5},{7,6},{8,7},{9,8},{10,9},{11,1... | collective-permute-start | bytes 36872 | tf_op jit(solution)/shard_map/ppermute | solution.py:388
  13.5 0.8 collective-permute-done.1
  14.3 1.5 collective-permute-done
  15.8 1.6 collective-permute-start.2
  17.4 1.3 pad.16.embedding_ref
  18.7 6.1 %collective-permute-start.3 = (f32[3,3,8,128]{3,2,1,0:T(8,128)S(1)}, f32[3,3,8,128]{3,2,1,0:T(8,128)S(1)}, u32[]{:S(2)}, u32[]{:S(2)}) collective-permute-start(f32[3,3,8,128]{3,2,1,0:T(8,128)S(1)} %pad_maximum_fusion.3), channel_id=1, source_target_pairs={{16,0},{32,16},{48,32},{64,48},{80,64},{96,80},{112,96},{128,112},... | collective-permute-start | bytes 110600 | tf_op jit(solution)/shard_map/ppermute | solution.py:395
  24.9 1.0 collective-permute-done.3
  25.9 0.6 copy.87
  26.6 19.4 %basis.1 = (bf16[9,8,384,384]{3,2,1,0:T(8,128)(2,1)}, bf16[384,128]{1,0:T(8,128)(2,1)}, f32[384,128]{1,0:T(8,128)}) custom-call(f32[9,3,13]{2,1,0:T(4,128)} %bitcast.84, f32[9,3,8,128]{3,2,1,0:T(8,128)} %copy-done.3, f32[9,3,8,128]{3,2,1,0:T(8,128)} %copy-done.3, bf16[128,128]{1,0:T(8,128)(2,1)} %pad.16.embedding_ref, f32[8,128]{1,0:T(8,128)} %radial_ref.1, ...), custom_call_target="tpu_custom_call" | custom-call | flops 2717908992 | bytes 21233664 | tf_op jit(solution)/shard_map/basis/pallas_call | solution.py:470
  45.9 5.4 %collective-permute-start.5 = (bf16[384,128]{1,0:T(8,128)(2,1)}, bf16[384,128]{1,0:T(8,128)(2,1)S(1)}, u32[]{:S(2)}, u32[]{:S(2)}) collective-permute-start(bf16[384,128]{1,0:T(8,128)(2,1)} %get-tuple-element.12), channel_id=1, source_target_pairs={{1,0},{2,1},{3,2},{4,3},{5,4},{6,5},{7,6},{8,7},{9,8},{10,9},{11,1... | collective-permute-start | bytes 294920 | tf_op jit(solution)/shard_map/ppermute | solution.py:388
  51.4 1.2 collective-permute-done.5
  52.5 1.6 collective-permute-done.4
  54.1 0.9 pad_maximum_fusion
  55.0 0.1 collective-permute-start.6
  55.1 1.3 convert_element_type.48.radial_ref
  56.4 5.7 %collective-permute-start.7 = (bf16[3,384,128]{2,1,0:T(8,128)(2,1)S(1)}, bf16[3,384,128]{2,1,0:T(8,128)(2,1)S(1)}, u32[]{:S(2)}, u32[]{:S(2)}) collective-permute-start(bf16[3,384,128]{2,1,0:T(8,128)(2,1)S(1)} %pad_maximum_fusion), channel_id=1, source_target_pairs={{16,0},{32,16},{48,32},{64,48},{80,64},{96,80},{112,96},{128,112},... | collective-permute-start | bytes 884744 | tf_op jit(solution)/shard_map/ppermute | solution.py:395
  62.1 2.8 %collective-permute-done.6 = bf16[3,384,128]{2,1,0:T(8,128)(2,1)S(1)} collective-permute-done((bf16[3,384,128]{2,1,0:T(8,128)(2,1)S(1)}, bf16[3,384,128]{2,1,0:T(8,128)(2,1)S(1)}, u32[]{:S(2)}, u32[]{:S(2)}) %collective-permute-start.6) | collective-permute-done | bytes 294944 | tf_op jit(solution)/shard_map/ppermute | solution.py:393
  64.9 0.9 constant_dynamic-update-slice_fusion.7
  65.9 0.9 copy-done
  66.9 13.5 %second.1 = bf16[384,128]{1,0:T(8,128)(2,1)} custom-call(s32[3]{0:T(128)} %bitcast.91, bf16[9,8,384,384]{3,2,1,0:T(8,128)(2,1)} %get-tuple-element.11.basis_ref, bf16[9,384,128]{2,1,0:T(8,128)(2,1)} %copy-done, f32[8,128]{1,0:T(8,128)} %convert_element_type.48.radial_ref, bf16[128,128]{1,0:T(8,128)(2,1)} %mix_ref.4, f32[1,128]{1,0:T(1,128)} %bitcast.94), custom_call_target="tpu_custom_call" | custom-call | flops 2717908992 | bytes 21233664 | tf_op jit(solution)/shard_map/second/pallas_call | solution.py:500
  80.4 4.6 %collective-permute-start.9 = (bf16[384,128]{1,0:T(8,128)(2,1)}, bf16[384,128]{1,0:T(8,128)(2,1)S(1)}, u32[]{:S(2)}, u32[]{:S(2)}) collective-permute-start(bf16[384,128]{1,0:T(8,128)(2,1)} %second.1), channel_id=1, source_target_pairs={{1,0},{2,1},{3,2},{4,3},{5,4},{6,5},{7,6},{8,7},{9,8},{10,9},{11,1... | collective-permute-start | bytes 294920 | tf_op jit(solution)/shard_map/ppermute | solution.py:388
  85.0 0.6 copy.28
  85.6 1.1 collective-permute-done.9
  86.7 0.6 collective-permute-done.8
  87.3 0.9 pad_maximum_fusion.1
  88.2 0.1 collective-permute-start.10
  88.3 0.6 multiply_bitcast_fusion.table_ref
  89.0 5.7 %collective-permute-start.11 = (bf16[3,384,128]{2,1,0:T(8,128)(2,1)S(1)}, bf16[3,384,128]{2,1,0:T(8,128)(2,1)S(1)}, u32[]{:S(2)}, u32[]{:S(2)}) collective-permute-start(bf16[3,384,128]{2,1,0:T(8,128)(2,1)S(1)} %pad_maximum_fusion.1), channel_id=1, source_target_pairs={{16,0},{32,16},{48,32},{64,48},{80,64},{96,80},{112,96},{128,112},... | collective-permute-start | bytes 884744 | tf_op jit(solution)/shard_map/ppermute | solution.py:395
  94.6 3.5 %collective-permute-done.10 = bf16[3,384,128]{2,1,0:T(8,128)(2,1)S(1)} collective-permute-done((bf16[3,384,128]{2,1,0:T(8,128)(2,1)S(1)}, bf16[3,384,128]{2,1,0:T(8,128)(2,1)S(1)}, u32[]{:S(2)}, u32[]{:S(2)}) %collective-permute-start.10) | collective-permute-done | bytes 294944 | tf_op jit(solution)/shard_map/ppermute | solution.py:393
  98.1 0.9 constant_dynamic-update-slice_fusion.12
  99.2 0.9 copy-done.1
  100.1 13.8 %first.1 = bf16[64,384]{1,0:T(8,128)(2,1)} custom-call(s32[3]{0:T(128)} %bitcast.92, bf16[9,8,384,384]{3,2,1,0:T(8,128)(2,1)} %get-tuple-element.11.basis_ref, bf16[9,384,128]{2,1,0:T(8,128)(2,1)} %copy-done.1, f32[8,128]{1,0:T(8,128)} %convert_element_type.48.radial_ref, bf16[128,128]{1,0:T(8,128)(2,1)} %mix_ref.5, f32[1,128]{1,0:T(1,128)} %bitcast.95, ...), custom_call_target="tpu_custom_call" | custom-call | flops 2717908992 | bytes 21233664 | tf_op jit(solution)/shard_map/first/pallas_call | solution.py:515
  113.8 5.9 %collective-permute-start.13 = (bf16[64,384]{1,0:T(8,128)(2,1)}, bf16[64,384]{1,0:T(8,128)(2,1)S(1)}, u32[]{:S(2)}, u32[]{:S(2)}) collective-permute-start(bf16[64,384]{1,0:T(8,128)(2,1)} %first.1), channel_id=1, source_target_pairs={{1,0},{2,1},{3,2},{4,3},{5,4},{6,5},{7,6},{8,7},{9,8},{10,9},{11,1... | collective-permute-start | bytes 147464 | tf_op jit(solution)/shard_map/ppermute | solution.py:388
  119.7 25.7 %slope.1 = (bf16[9,8,384,384]{3,2,1,0:T(8,128)(2,1)}, f32[8,384,128]{2,1,0:T(8,128)}) custom-call(f32[9,3,13]{2,1,0:T(4,128)} %bitcast.85, f32[9,3,8,128]{3,2,1,0:T(8,128)} %copy-done.3, f32[9,3,8,128]{3,2,1,0:T(8,128)} %copy-done.3), custom_call_target="tpu_custom_call" | custom-call | flops 2717908992 | bytes 21233664 | tf_op jit(solution)/shard_map/slope/pallas_call | solution.py:489
  145.4 0.8 pad_maximum_fusion.2
  146.3 18.3 %pair.1.force_ref = f32[3,384,128]{2,1,0:T(8,128)} custom-call(f32[9,3,13]{2,1,0:T(4,128)} %bitcast.86, f32[9,3,8,128]{3,2,1,0:T(8,128)} %copy-done.3, f32[9,3,8,128]{3,2,1,0:T(8,128)} %copy-done.3, bf16[9,8,384,384]{3,2,1,0:T(8,128)(2,1)} %get-tuple-element.10.slope_ref, bf16[9,384,128]{2,1,0:T(8,128)(2,1)} %copy-done, bf16[9,384,128]{2,1,0:T(8,128)(2,1)} %copy-done.1, ...), custom_call_target="tpu_custom_call" | custom-call | flops 5435817984 | bytes 21233664 | tf_op jit(solution)/shard_map/pair/pallas_call | solution.py:531
  164.6 5.0 %collective-permute-start.15 = (bf16[3,64,384]{2,1,0:T(8,128)(2,1)S(1)}, bf16[3,64,384]{2,1,0:T(8,128)(2,1)S(1)}, u32[]{:S(2)}, u32[]{:S(2)}) collective-permute-start(bf16[3,64,384]{2,1,0:T(8,128)(2,1)S(1)} %pad_maximum_fusion.2), channel_id=1, source_target_pairs={{16,0},{32,16},{48,32},{64,48},{80,64},{96,80},{112,96},{128,112},... | collective-permute-start | bytes 442376 | tf_op jit(solution)/shard_map/ppermute | solution.py:395
  169.8 2.3 %collective-permute-done.15 = bf16[3,64,384]{2,1,0:T(8,128)(2,1)S(1)} collective-permute-done((bf16[3,64,384]{2,1,0:T(8,128)(2,1)S(1)}, bf16[3,64,384]{2,1,0:T(8,128)(2,1)S(1)}, u32[]{:S(2)}, u32[]{:S(2)}) %collective-permute-start.15) | collective-permute-done | bytes 147488 | tf_op jit(solution)/shard_map/ppermute | solution.py:395
  172.1 0.8 copy-done.2
  172.9 16.8 %last.1 = (f32[3,3,128]{2,1,0:T(4,128)}, f32[3,3,128]{2,1,0:T(4,128)}) custom-call(s32[3]{0:T(128)} %bitcast.93, bf16[9,8,384,384]{3,2,1,0:T(8,128)(2,1)} %get-tuple-element.10.slope_ref, bf16[9,64,384]{2,1,0:T(8,128)(2,1)} %copy-done.2, bf16[9,64,384]{2,1,0:T(8,128)(2,1)} %copy-done.2, f32[9,3,8,128]{3,2,1,0:T(8,128)} %copy-done.3, ...), custom_call_target="tpu_custom_call" | custom-call | flops 2717908992 | bytes 21233664 | tf_op jit(solution)/shard_map/last/pallas_call | solution.py:552
  189.7 1.3 copy.29
  191.0 1.3 copy.30
  (58 shorter events, 0.6 us)
Async XLA Ops:
  0.6 84.4 %copy-start.6 = (f32[1,1,3,3,128]{4,1,3,2,0:T(1,128)S(1)}, f32[1,1,3,3,128]{4,1,3,2,0:T(1,128)}, u32[]{:S(2)}) copy-start(f32[1,1,3,3,128]{4,1,3,2,0:T(1,128)} %param.17) | copy-start | bytes 13828
  0.6 84.3 %copy-start.9 = (f32[1,1,3,3,128]{4,1,3,2,0:T(1,128)S(1)}, f32[1,1,3,3,128]{4,1,3,2,0:T(1,128)}, u32[]{:S(2)}) copy-start(f32[1,1,3,3,128]{4,1,3,2,0:T(1,128)} %param.16) | copy-start | bytes 13828
  0.7 84.3 %copy-start.8 = (f32[1,1,3,3,128]{4,1,3,2,0:T(1,128)S(1)}, f32[1,1,3,3,128]{4,1,3,2,0:T(1,128)}, u32[]{:S(2)}) copy-start(f32[1,1,3,3,128]{4,1,3,2,0:T(1,128)} %param.15) | copy-start | bytes 13828
  0.7 84.3 %copy-start.7 = (f32[1,1,3,3,128]{4,1,3,2,0:T(1,128)S(1)}, f32[1,1,3,3,128]{4,1,3,2,0:T(1,128)}, u32[]{:S(2)}) copy-start(f32[1,1,3,3,128]{4,1,3,2,0:T(1,128)} %param.14) | copy-start | bytes 13828
  0.7 87.6 %copy-start.10 = (bf16[6,128]{1,0:T(8,128)(2,1)S(1)}, bf16[6,128]{1,0:T(8,128)(2,1)}, u32[]{:S(2)}) copy-start(bf16[6,128]{1,0:T(8,128)(2,1)} %param.22) | copy-start | bytes 4612
  0.7 87.6 %copy-start.11 = (f32[8,128]{1,0:T(8,128)S(1)}, f32[8,128]{1,0:T(8,128)}, u32[]{:S(2)}) copy-start(f32[8,128]{1,0:T(8,128)} %radial_ref.1) | copy-start | bytes 12292
  8.7 105.1 %copy-start.5 = (f32[3,128]{1,0:T(4,128)}, f32[3,128]{1,0:T(4,128)S(1)}, u32[]{:S(2)}) copy-start(f32[3,128]{1,0:T(4,128)S(1)} %get-tuple-element.23.mass_ref) | copy-start | bytes 4612
  10.2 4.1 %collective-permute-start.1 = (f32[3,8,128]{2,1,0:T(8,128)S(1)}, f32[3,8,128]{2,1,0:T(8,128)S(1)}, u32[]{:S(2)}, u32[]{:S(2)}) collective-permute-start(f32[3,8,128]{2,1,0:T(8,128)S(1)} %concatenate.19), channel_id=1, source_target_pairs={{1,0},{2,1},{3,2},{4,3},{5,4},{6,5},{7,6},{8,7},{9,8},{10,9},{11,1... | collective-permute-start | bytes 36872 | tf_op jit(solution)/shard_map/ppermute | solution.py:388
  13.5 2.3 %collective-permute-start = (f32[3,8,128]{2,1,0:T(8,128)S(1)}, f32[3,8,128]{2,1,0:T(8,128)S(1)}, u32[]{:S(2)}, u32[]{:S(2)}) collective-permute-start(f32[3,8,128]{2,1,0:T(8,128)S(1)} %concatenate.19), channel_id=1, source_target_pairs={{0,1},{1,2},{2,3},{3,4},{4,5},{5,6},{6,7},{7,8},{8,9},{9,10},{10,1... | collective-permute-start | bytes 36872 | tf_op jit(solution)/shard_map/ppermute | solution.py:386
  15.8 9.1 %collective-permute-start.2 = (f32[3,3,8,128]{3,2,1,0:T(8,128)S(1)}, f32[3,3,8,128]{3,2,1,0:T(8,128)S(1)}, u32[]{:S(2)}, u32[]{:S(2)}) collective-permute-start(f32[3,3,8,128]{3,2,1,0:T(8,128)S(1)} %pad_maximum_fusion.3), channel_id=1, source_target_pairs={{0,16},{16,32},{32,48},{48,64},{64,80},{80,96},{96,112},{112,128},... | collective-permute-start | bytes 110600 | tf_op jit(solution)/shard_map/ppermute | solution.py:393
  18.7 7.2 %collective-permute-start.3 = (f32[3,3,8,128]{3,2,1,0:T(8,128)S(1)}, f32[3,3,8,128]{3,2,1,0:T(8,128)S(1)}, u32[]{:S(2)}, u32[]{:S(2)}) collective-permute-start(f32[3,3,8,128]{3,2,1,0:T(8,128)S(1)} %pad_maximum_fusion.3), channel_id=1, source_target_pairs={{16,0},{32,16},{48,32},{64,48},{80,64},{96,80},{112,96},{128,112},... | collective-permute-start | bytes 110600 | tf_op jit(solution)/shard_map/ppermute | solution.py:395
  25.9 0.7 copy-start.3
  45.9 6.6 %collective-permute-start.5 = (bf16[384,128]{1,0:T(8,128)(2,1)}, bf16[384,128]{1,0:T(8,128)(2,1)S(1)}, u32[]{:S(2)}, u32[]{:S(2)}) collective-permute-start(bf16[384,128]{1,0:T(8,128)(2,1)} %get-tuple-element.12), channel_id=1, source_target_pairs={{1,0},{2,1},{3,2},{4,3},{5,4},{6,5},{7,6},{8,7},{9,8},{10,9},{11,1... | collective-permute-start | bytes 294920 | tf_op jit(solution)/shard_map/ppermute | solution.py:388
  51.4 2.7 %collective-permute-start.4 = (bf16[384,128]{1,0:T(8,128)(2,1)}, bf16[384,128]{1,0:T(8,128)(2,1)S(1)}, u32[]{:S(2)}, u32[]{:S(2)}) collective-permute-start(bf16[384,128]{1,0:T(8,128)(2,1)} %get-tuple-element.12), channel_id=1, source_target_pairs={{0,1},{1,2},{2,3},{3,4},{4,5},{5,6},{6,7},{7,8},{8,9},{9,10},{10,1... | collective-permute-start | bytes 294920 | tf_op jit(solution)/shard_map/ppermute | solution.py:386
  55.0 9.8 %collective-permute-start.6 = (bf16[3,384,128]{2,1,0:T(8,128)(2,1)S(1)}, bf16[3,384,128]{2,1,0:T(8,128)(2,1)S(1)}, u32[]{:S(2)}, u32[]{:S(2)}) collective-permute-start(bf16[3,384,128]{2,1,0:T(8,128)(2,1)S(1)} %pad_maximum_fusion), channel_id=1, source_target_pairs={{0,16},{16,32},{32,48},{48,64},{64,80},{80,96},{96,112},{112,128},... | collective-permute-start | bytes 884744 | tf_op jit(solution)/shard_map/ppermute | solution.py:393
  56.4 9.5 %collective-permute-start.7 = (bf16[3,384,128]{2,1,0:T(8,128)(2,1)S(1)}, bf16[3,384,128]{2,1,0:T(8,128)(2,1)S(1)}, u32[]{:S(2)}, u32[]{:S(2)}) collective-permute-start(bf16[3,384,128]{2,1,0:T(8,128)(2,1)S(1)} %pad_maximum_fusion), channel_id=1, source_target_pairs={{16,0},{32,16},{48,32},{64,48},{80,64},{96,80},{112,96},{128,112},... | collective-permute-start | bytes 884744 | tf_op jit(solution)/shard_map/ppermute | solution.py:395
  65.9 0.9 copy-start
  80.4 6.3 %collective-permute-start.9 = (bf16[384,128]{1,0:T(8,128)(2,1)}, bf16[384,128]{1,0:T(8,128)(2,1)S(1)}, u32[]{:S(2)}, u32[]{:S(2)}) collective-permute-start(bf16[384,128]{1,0:T(8,128)(2,1)} %second.1), channel_id=1, source_target_pairs={{1,0},{2,1},{3,2},{4,3},{5,4},{6,5},{7,6},{8,7},{9,8},{10,9},{11,1... | collective-permute-start | bytes 294920 | tf_op jit(solution)/shard_map/ppermute | solution.py:388
  85.0 2.3 %collective-permute-start.8 = (bf16[384,128]{1,0:T(8,128)(2,1)}, bf16[384,128]{1,0:T(8,128)(2,1)S(1)}, u32[]{:S(2)}, u32[]{:S(2)}) collective-permute-start(bf16[384,128]{1,0:T(8,128)(2,1)} %second.1), channel_id=1, source_target_pairs={{0,1},{1,2},{2,3},{3,4},{4,5},{5,6},{6,7},{7,8},{8,9},{9,10},{10,1... | collective-permute-start | bytes 294920 | tf_op jit(solution)/shard_map/ppermute | solution.py:386
  88.2 9.9 %collective-permute-start.10 = (bf16[3,384,128]{2,1,0:T(8,128)(2,1)S(1)}, bf16[3,384,128]{2,1,0:T(8,128)(2,1)S(1)}, u32[]{:S(2)}, u32[]{:S(2)}) collective-permute-start(bf16[3,384,128]{2,1,0:T(8,128)(2,1)S(1)} %pad_maximum_fusion.1), channel_id=1, source_target_pairs={{0,16},{16,32},{32,48},{48,64},{64,80},{80,96},{96,112},{112,128},... | collective-permute-start | bytes 884744 | tf_op jit(solution)/shard_map/ppermute | solution.py:393
  89.0 10.1 %collective-permute-start.11 = (bf16[3,384,128]{2,1,0:T(8,128)(2,1)S(1)}, bf16[3,384,128]{2,1,0:T(8,128)(2,1)S(1)}, u32[]{:S(2)}, u32[]{:S(2)}) collective-permute-start(bf16[3,384,128]{2,1,0:T(8,128)(2,1)S(1)} %pad_maximum_fusion.1), channel_id=1, source_target_pairs={{16,0},{32,16},{48,32},{64,48},{80,64},{96,80},{112,96},{128,112},... | collective-permute-start | bytes 884744 | tf_op jit(solution)/shard_map/ppermute | solution.py:395
  99.1 0.9 copy-start.1
  113.8 55.9 %copy-start.4 = (bf16[64,384]{1,0:T(8,128)(2,1)S(1)}, bf16[64,384]{1,0:T(8,128)(2,1)}, u32[]{:S(2)}) copy-start(bf16[64,384]{1,0:T(8,128)(2,1)} %first.1) | copy-start | bytes 147460
  113.8 31.6 %collective-permute-start.13 = (bf16[64,384]{1,0:T(8,128)(2,1)}, bf16[64,384]{1,0:T(8,128)(2,1)S(1)}, u32[]{:S(2)}, u32[]{:S(2)}) collective-permute-start(bf16[64,384]{1,0:T(8,128)(2,1)} %first.1), channel_id=1, source_target_pairs={{1,0},{2,1},{3,2},{4,3},{5,4},{6,5},{7,6},{8,7},{9,8},{10,9},{11,1... | collective-permute-start | bytes 147464 | tf_op jit(solution)/shard_map/ppermute | solution.py:388
  119.7 25.7 %collective-permute-start.12 = (bf16[64,384]{1,0:T(8,128)(2,1)}, bf16[64,384]{1,0:T(8,128)(2,1)S(1)}, u32[]{:S(2)}, u32[]{:S(2)}) collective-permute-start(bf16[64,384]{1,0:T(8,128)(2,1)} %first.1), channel_id=1, source_target_pairs={{0,1},{1,2},{2,3},{3,4},{4,5},{5,6},{6,7},{7,8},{8,9},{9,10},{10,1... | collective-permute-start | bytes 147464 | tf_op jit(solution)/shard_map/ppermute | solution.py:386
  146.2 23.4 %collective-permute-start.14 = (bf16[3,64,384]{2,1,0:T(8,128)(2,1)S(1)}, bf16[3,64,384]{2,1,0:T(8,128)(2,1)S(1)}, u32[]{:S(2)}, u32[]{:S(2)}) collective-permute-start(bf16[3,64,384]{2,1,0:T(8,128)(2,1)S(1)} %pad_maximum_fusion.2), channel_id=1, source_target_pairs={{0,16},{16,32},{32,48},{48,64},{64,80},{80,96},{96,112},{112,128},... | collective-permute-start | bytes 442376 | tf_op jit(solution)/shard_map/ppermute | solution.py:393
  164.6 7.5 %collective-permute-start.15 = (bf16[3,64,384]{2,1,0:T(8,128)(2,1)S(1)}, bf16[3,64,384]{2,1,0:T(8,128)(2,1)S(1)}, u32[]{:S(2)}, u32[]{:S(2)}) collective-permute-start(bf16[3,64,384]{2,1,0:T(8,128)(2,1)S(1)} %pad_maximum_fusion.2), channel_id=1, source_target_pairs={{16,0},{32,16},{48,32},{64,48},{80,64},{96,80},{112,96},{128,112},... | collective-permute-start | bytes 442376 | tf_op jit(solution)/shard_map/ppermute | solution.py:395
  172.1 0.8 copy-start.2

commit v2 on v1

v2 whole, which is shorter than its diff:
```python
import functools
import math

import jax
import jax.numpy as jnp
from jax import lax
from jax.experimental import pallas as pl
from jax.experimental.pallas import tpu as pltpu
from jax.sharding import PartitionSpec as P

SIDE = 10.0
REACH = 5.0
HALF_STEP = 0.25
DECAY = math.exp(-0.5)
FAR = 1.0e4

ORDERS = 8
KINDS = 8
SLOTS = 128
COLUMN = 3
ATOMS = COLUMN * SLOTS
CHANNELS = 128
PARTS = 9
CHUNK = 32
OUTER = -1
LIMIT = 12 * 2**20

F32 = jnp.float32
BF16 = jnp.bfloat16
HIGHEST = lax.Precision.HIGHEST
ODD = (3.14159265160, -5.16771249, 2.55012026, -0.59890223, 0.07772681)
EVEN = (1.0, -4.93480219, 4.05869615, -1.33500654, 0.23347127, -0.02380946)


def fit_terms():
    import numpy as np

    nodes = 0.5 * np.cos(np.pi * (np.arange(400) + 0.5) / 800)
    odd = np.polynomial.polynomial.polyfit(nodes * nodes, np.sin(np.pi * nodes) / nodes, 4)
    even = np.polynomial.polynomial.polyfit(nodes * nodes, np.cos(np.pi * nodes), 4)
    return tuple(float(value) for value in odd), tuple(float(value) for value in even)


ODD, EVEN = fit_terms()


def horner(terms, square):
    total = terms[-1]
    for term in terms[-2::-1]:
        total = total * square + term
    return total


def turned(row):
    return jnp.broadcast_to(row, (SLOTS, SLOTS)).T


def dot(left, right, contract=((1,), (0,)), precision=None):
    return lax.dot_general(
        left, right, (contract, ((), ())), precision=precision, preferred_element_type=F32
    )


def spread_own(own_ref, own_cols):
    for block in range(COLUMN):
        for axis in range(3):
            own_cols[axis, pl.ds(block * SLOTS, SLOTS), :] = turned(
                own_ref[0, block, axis : axis + 1, :] * (1.0 / REACH)
            )


def mark_diagonal(column, diagonal):
    rows = lax.broadcasted_iota(jnp.int32, (SLOTS, SLOTS), 0)
    lanes = lax.broadcasted_iota(jnp.int32, (SLOTS, SLOTS), 1)
    hit = jnp.logical_and(rows == lanes, column == 4)
    diagonal[...] = jnp.where(hit, FAR * FAR, 0.0)


def offset_z(block, near):
    return (near - block + 1) % 3 - 1


def place_of(part):
    step = pl.program_id(0)
    if part == OUTER:
        return step + 3 * (step // 3)
    return step + 3 * part


def mark_listed(own_ref, near_ref, column, picked, listed):
    lanes = lax.broadcasted_iota(jnp.int32, (1, SLOTS), 1)
    for block in range(COLUMN):
        for near in range(COLUMN):
            stencil = column * 3 + offset_z(block, near) + 1
            ahead = jnp.where(lanes == stencil - 14, own_ref[0, block, 5:6, :], 0.0)
            behind = jnp.where(lanes == 12 - stencil, near_ref[0, near, 5:6, :], 0.0)
            own = jnp.where(lanes == jnp.where(stencil == 13, 0, -1), 1.0, 0.0)
            row = block * COLUMN + near
            picked[row : row + 1, :] = own + ahead + behind
    sums = jnp.sum(picked[...], axis=1, keepdims=True)
    listed[...] = jnp.broadcast_to(sums, listed.shape)


def near_rows(listed, near_ref, column, block, near):
    x, y, z = true_rows(near_ref, column, near)
    z = z + (SIDE / REACH) * offset_z(block, near)
    slots = lax.broadcasted_iota(jnp.int32, (1, SLOTS), 1).astype(F32)
    row = block * COLUMN + near
    counts = jnp.logical_and(
        slots < near_ref[0, near, 4:5, :], listed[row : row + 1, :] > 0.5
    )
    return jnp.where(counts, x, FAR), y, z


def left_over(rows, own_cols, diagonal, block, near, start):
    span = pl.ds(block * SLOTS + start, CHUNK)
    dx = rows[0] - own_cols[0, span, :]
    dy = rows[1] - own_cols[1, span, :]
    dz = rows[2] - own_cols[2, span, :]
    square = dx * dx + dy * dy + dz * dz
    if near == block:
        square = square + diagonal[pl.ds(start, CHUNK), :]
    return jnp.maximum(1.0 - square, 0.0)


def species_features(near_ref, embedding, near):
    kinds = turned(near_ref[0, near, 3:4, :])
    lanes = lax.broadcasted_iota(jnp.int32, (SLOTS, SLOTS), 1).astype(F32)
    one_hot = jnp.where(kinds == lanes, 1.0, 0.0).astype(BF16)
    return dot(one_hot, embedding).astype(BF16)


def basis_kernel(part, own_ref, *refs):
    if part == OUTER:
        near_0, near_2, embedding_ref, radial_ref, mix_ref, before_ref = refs[:6]
        basis_ref, hidden_ref, gate_ref = refs[6:9]
        fields = (near_0, near_2)
    else:
        near_1, embedding_ref, radial_ref, basis_ref, after_ref = refs[:5]
        fields = (near_1,)
    own_cols, near_ref, diagonal, picked, listed, message, features = refs[-7:]
    column = place_of(part)
    near_ref[0] = pick(fields)

    @pl.when(pl.program_id(0) == 0)
    def _():
        spread_own(own_ref, own_cols)
        picked[...] = jnp.zeros_like(picked)
        if part == OUTER:
            message[...] = before_ref[...]
        else:
            message[...] = jnp.zeros_like(message)

    mark_diagonal(column, diagonal)
    mark_listed(own_ref, near_ref, column, picked, listed)
    for near in range(COLUMN):
        features[pl.ds(near * SLOTS, SLOTS), :] = species_features(
            near_ref, embedding_ref[...].astype(BF16), near
        )
    for block in range(COLUMN):
        for near in range(COLUMN):
            rows = near_rows(listed, near_ref, column, block, near)
            for start in range(0, SLOTS, CHUNK):
                left = left_over(rows, own_cols, diagonal, block, near, start)
                middle = left - 0.5
                cosine = middle * horner(ODD, middle * middle)
                twice = cosine + cosine
                last = left * left
                now = last * cosine
                span = (
                    pl.ds(block * SLOTS + start, CHUNK),
                    pl.ds(near * SLOTS, SLOTS),
                )
                basis_ref[0, 0, span[0], span[1]] = last.astype(BF16)
                basis_ref[0, 1, span[0], span[1]] = now.astype(BF16)
                for order in range(2, ORDERS):
                    last, now = now, twice * now - last
                    basis_ref[0, order, span[0], span[1]] = now.astype(BF16)
    gathered = dot(basis_ref[0].reshape(ORDERS * ATOMS, ATOMS), features[...])
    add_orders(gathered, radial_ref, message)

    @pl.when(pl.program_id(0) == pl.num_programs(0) - 1)
    def _():
        if part == OUTER:
            gate = dot(message[...].astype(BF16), mix_ref[...].astype(BF16))
            gate_ref[...] = gate
            base = jnp.concatenate(
                [species_features(own_ref, embedding_ref[...].astype(BF16), block) for block in range(COLUMN)]
            )
            hidden_ref[...] = (base.astype(F32) + gate * jax.nn.sigmoid(gate)).astype(BF16)
        else:
            after_ref[...] = message[...]


def silu_slope(values):
    sigmoid = jax.nn.sigmoid(values)
    return sigmoid * (1.0 + values * (1.0 - sigmoid))


def pick(refs):
    if len(refs) == 1:
        return refs[0][0]
    return jnp.where(pl.program_id(0) < 3, refs[0][0], refs[1][0])


def add_orders(gathered, radial_ref, message):
    total = message[...]
    for order in range(ORDERS):
        rows = gathered[order * ATOMS : (order + 1) * ATOMS, :]
        total = total + radial_ref[order : order + 1, :] * rows
    message[...] = total


def gather_kernel(basis_ref, field_ref, radial_ref, after_ref, message):
    @pl.when(pl.program_id(0) == 0)
    def _():
        message[...] = jnp.zeros_like(message)

    gathered = dot(basis_ref[0].reshape(ORDERS * ATOMS, ATOMS), field_ref[0])
    add_orders(gathered, radial_ref, message)

    @pl.when(pl.program_id(0) == 2)
    def _():
        after_ref[...] = message[...]


def gather_outer(basis_ref, fields, radial_ref, before_ref, message):
    @pl.when(pl.program_id(0) == 0)
    def _():
        message[...] = before_ref[...]

    gathered = dot(basis_ref[0].reshape(ORDERS * ATOMS, ATOMS), pick(fields))
    add_orders(gathered, radial_ref, message)


def second_kernel(
    basis_ref, hidden_0, hidden_2, radial_ref, mix_ref, upstream_ref, before_ref, grad_ref, message
):
    gather_outer(basis_ref, (hidden_0, hidden_2), radial_ref, before_ref, message)

    @pl.when(pl.program_id(0) == 5)
    def _():
        gate = dot(message[...].astype(BF16), mix_ref[...].astype(BF16))
        second = (upstream_ref[...] * silu_slope(gate)).astype(BF16)
        grad_ref[...] = dot(second, mix_ref[...].astype(BF16), ((1,), (1,))).astype(BF16)


def first_kernel(
    basis_ref, grad_0, grad_2, radial_ref, mix_ref, upstream_ref, gate_ref, table_ref, before_ref,
    projected_ref, message,
):
    gather_outer(basis_ref, (grad_0, grad_2), radial_ref, before_ref, message)

    @pl.when(pl.program_id(0) == 5)
    def _():
        hidden_grad = upstream_ref[...] + message[...]
        first = (hidden_grad * silu_slope(gate_ref[...])).astype(BF16)
        message_grad = dot(first, mix_ref[...].astype(BF16), ((1,), (1,)))
        projected_ref[...] = dot(
            table_ref[...], message_grad, ((1,), (1,)), HIGHEST
        ).astype(BF16)


def start_from(before_ref, total_ref):
    if before_ref is None:
        total_ref[...] = jnp.zeros_like(total_ref)
    else:
        total_ref[...] = before_ref[...]


def slope_kernel(
    group, own_ref, near_ref, *refs
):
    before_ref = None if group == 1 else refs[0]
    slope_ref, kind_ref, own_cols, diagonal, picked, listed, table = refs[-7:]
    column = place_of(group)

    @pl.when(pl.program_id(0) == 0)
    def _():
        spread_own(own_ref, own_cols)
        picked[...] = jnp.zeros_like(picked)
        start_from(before_ref, kind_ref)

    mark_diagonal(column, diagonal)
    mark_listed(own_ref, near_ref, column, picked, listed)
    one_hots = [kind_rows(near_ref, near) for near in range(COLUMN)]
    fill_table(table, one_hots, near_ref, column)
    for block in range(COLUMN):
        for near in range(COLUMN):
            rows = near_rows(listed, near_ref, column, block, near)
            for start in range(0, SLOTS, CHUNK):
                left = left_over(rows, own_cols, diagonal, block, near, start)
                middle = left - 0.5
                square = middle * middle
                cosine = middle * horner(ODD, square)
                sine = horner(EVEN, square)
                twice = cosine + cosine
                last_a = -2.0 * left
                now_a = last_a * cosine
                now_b = (left * left) * (sine * -math.pi)
                last_b = None
                span = (
                    pl.ds(block * SLOTS + start, CHUNK),
                    pl.ds(near * SLOTS, SLOTS),
                )
                slope_ref[0, 0, span[0], span[1]] = last_a.astype(BF16)
                slope_ref[0, 1, span[0], span[1]] = (now_a + now_b).astype(BF16)
                for order in range(2, ORDERS):
                    last_a, now_a = now_a, twice * now_a - last_a
                    if last_b is None:
                        last_b, now_b = now_b, twice * now_b
                    else:
                        last_b, now_b = now_b, twice * now_b - last_b
                    slope_ref[0, order, span[0], span[1]] = (
                        now_a + float(order) * now_b
                    ).astype(BF16)
    sums = dot(slope_ref[0].reshape(ORDERS * ATOMS, ATOMS), table[...], ((1,), (1,)))
    kind_ref[...] += sums.reshape(ORDERS, ATOMS, SLOTS)


def true_rows(near_ref, column, near):
    steps = ((column // 3 - 1).astype(F32), (column % 3 - 1).astype(F32), 0.0)
    return [
        (near_ref[0, near, axis : axis + 1, :] + SIDE * steps[axis]) * (1.0 / REACH)
        for axis in range(3)
    ]


def kind_rows(near_ref, near):
    kinds = lax.broadcasted_iota(jnp.int32, (KINDS, SLOTS), 0).astype(F32)
    return jnp.where(near_ref[0, near, 3:4, :] == kinds, 1.0, 0.0)


def fill_table(table, values, near_ref, column):
    for near in range(COLUMN):
        zero = jnp.zeros((KINDS, SLOTS), F32)
        pieces = [values[near] if part == near else zero for part in range(COLUMN)]
        for row in true_rows(near_ref, column, near):
            product = values[near] * row
            high = product.astype(BF16).astype(F32)
            pieces.extend((high, product - high))
        pieces.extend([zero] * (SLOTS // KINDS - PARTS))
        table[:, pl.ds(near * SLOTS, SLOTS)] = jnp.concatenate(pieces, axis=0).astype(BF16)


def pair_kernel(
    group, own_ref, near_ref, slope_ref, near_hidden_ref, near_grad_ref, hidden_ref, grad_ref,
    radial_ref, *refs,
):
    before_ref = None if group == 1 else refs[0]
    force_ref, own_cols, left_side, right_side = refs[-4:]
    column = place_of(group)

    @pl.when(pl.program_id(0) == 0)
    def _():
        spread_own(own_ref, own_cols)
        start_from(before_ref, force_ref)
        for block in range(COLUMN):
            span = pl.ds(block * SLOTS, SLOTS)
            grad = grad_ref[0, span, :].astype(F32)
            hidden = hidden_ref[0, span, :].astype(F32)
            for order in range(ORDERS):
                radial = radial_ref[order : order + 1, :]
                place = pl.ds(order * SLOTS, SLOTS)
                left_side[block, place, 0:CHANNELS] = (radial * grad).astype(BF16)
                left_side[block, place, CHANNELS : 2 * CHANNELS] = (radial * hidden).astype(BF16)

    right_side[:, 0:CHANNELS] = near_hidden_ref[0]
    right_side[:, CHANNELS : 2 * CHANNELS] = near_grad_ref[0]
    near_places = [true_rows(near_ref, column, near) for near in range(COLUMN)]
    for block in range(COLUMN):
        pair = dot(left_side[block], right_side[...], ((1,), (1,)))
        for start in range(0, SLOTS, CHUNK):
            span = pl.ds(block * SLOTS + start, CHUNK)
            strength = jnp.zeros((CHUNK, ATOMS), F32)
            for order in range(ORDERS):
                rows = pair[order * SLOTS + start : order * SLOTS + start + CHUNK, :]
                strength = strength + rows * slope_ref[0, order, span, :].astype(F32)
            for axis in range(3):
                total = force_ref[axis, span, :]
                for near in range(COLUMN):
                    row = near_places[near][axis]
                    if axis == 2:
                        row = row + (SIDE / REACH) * offset_z(block, near)
                    part = strength[:, near * SLOTS : (near + 1) * SLOTS]
                    total = total + part * (row - own_cols[axis, span, :])
                force_ref[axis, span, :] = total


def kind_kernel(group, slope_ref, projected_ref, near_ref, *refs):
    before_ref = None if group == 1 else refs[0]
    near_kind_ref, table = refs[-2:]

    @pl.when(pl.program_id(0) == 0)
    def _():
        start_from(before_ref, near_kind_ref)

    add_kinds(place_of(group), slope_ref, projected_ref, near_ref, near_kind_ref, table)


def add_kinds(column, slope_ref, projected_ref, near_ref, near_kind, table):
    projected = projected_ref[0].astype(F32)
    total = near_kind[...]
    for order in range(ORDERS):
        values = [
            projected[order * KINDS : (order + 1) * KINDS, near * SLOTS : (near + 1) * SLOTS]
            for near in range(COLUMN)
        ]
        fill_table(table.at[order], values, near_ref, column)
        total = total + dot(slope_ref[0, order], table[order], ((1,), (1,)))
    near_kind[...] = total


def last_kernel(
    slope_ref, projected_ref, near_ref, before_ref, own_projected_ref, own_ref, force_ref,
    kind_ref, mixed_ref, mass_ref, new_force_ref, new_velocity_ref, own_cols, table, near_kind,
):
    @pl.when(pl.program_id(0) == 0)
    def _():
        spread_own(own_ref, own_cols)
        near_kind[...] = before_ref[...]

    add_kinds(place_of(2), slope_ref, projected_ref, near_ref, near_kind, table)

    @pl.when(pl.program_id(0) == 2)
    def _():
        lanes = lax.broadcasted_iota(jnp.int32, (SLOTS, SLOTS), 1)
        lane_kind = (lanes % KINDS).astype(F32)
        part = lanes // KINDS
        inner = lax.broadcasted_iota(jnp.int32, (ORDERS * KINDS, SLOTS), 0)
        outer = lax.broadcasted_iota(jnp.int32, (ORDERS * KINDS, SLOTS), 1) % KINDS
        slots = lax.broadcasted_iota(jnp.int32, (1, SLOTS), 1)
        for block in range(COLUMN):
            span = pl.ds(block * SLOTS, SLOTS)
            kinds = turned(own_ref[0, block, 3:4, :])
            total = jnp.where(kinds == lane_kind, near_kind[span, :], 0.0)
            own = own_projected_ref[0, :, span]
            for order in range(ORDERS):
                chosen = jnp.where(inner == outer + order * KINDS, 1.0, 0.0).astype(BF16)
                spread = dot(own, chosen, ((0,), (0,)))
                total = total + spread * kind_ref[order, span, :]
            for axis in range(3):
                factor = jnp.zeros((SLOTS, SLOTS), F32)
                for near in range(COLUMN):
                    shift = -own_cols[axis, span, :]
                    if axis == 2:
                        shift = shift + (SIDE / REACH) * offset_z(block, near)
                    factor = jnp.where(part == near, shift, factor)
                here = jnp.logical_or(
                    part == COLUMN + 2 * axis, part == COLUMN + 1 + 2 * axis
                )
                factor = jnp.where(here, 1.0, factor)
                lanes_force = force_ref[axis, span, :] + total * factor
                summed = jnp.sum(lanes_force.T, axis=0, keepdims=True)
                live = slots.astype(F32) < own_ref[0, block, 4:5, :]
                force = jnp.where(live, summed * (2.0 / REACH), 0.0)
                row = 3 * block + axis
                new_force_ref[row] = force
                new_velocity_ref[row] = mixed_ref[row] + HALF_STEP * force / mass_ref[block]


RADIAL_ONE = 0
RADIAL_TWO = ORDERS
TABLE = ORDERS * KINDS
MIX_ONE = CHANNELS
MIX_TWO = 2 * CHANNELS
WIDE = 3 * CHANNELS
UPSTREAM = 2 * ATOMS
WEIGHT_ROWS = 3 * ATOMS


def prepare_kernel(
    counts_ref, masses_ref, positions_ref, velocities_ref, forces_ref, noise_ref, species_ref,
    pair_list_ref, embedding_ref, radial_one_ref, radial_two_ref, mix_one_ref, mix_two_ref,
    readout_ref, new_positions_ref, geometry_ref, mixed_ref, mass_ref, weights_ref,
):
    geometry_ref[...] = jnp.zeros_like(geometry_ref)
    kinds = embedding_ref.shape[0]
    weights_ref[RADIAL_ONE : RADIAL_ONE + ORDERS, :] = radial_one_ref[...]
    weights_ref[RADIAL_TWO : RADIAL_TWO + ORDERS, :] = radial_two_ref[...].astype(F32)
    weights_ref[MIX_ONE : MIX_ONE + CHANNELS, :] = mix_one_ref[...].astype(F32)
    weights_ref[MIX_TWO : MIX_TWO + CHANNELS, :] = mix_two_ref[...].astype(F32)
    weights_ref[WIDE : WIDE + SLOTS, :] = jnp.zeros((SLOTS, CHANNELS), F32)
    weights_ref[WIDE : WIDE + kinds, :] = embedding_ref[...].astype(F32)
    for order in range(ORDERS):
        weights_ref[TABLE + order * KINDS : TABLE + (order + 1) * KINDS, :] = (
            radial_one_ref[order : order + 1, :] * weights_ref[WIDE : WIDE + KINDS, :]
        )
    slots = lax.broadcasted_iota(jnp.int32, (SLOTS, CHANNELS), 0)
    for block in range(COLUMN):
        live = slots < counts_ref[0, 0, block]
        start = UPSTREAM + block * SLOTS
        weights_ref[start : start + SLOTS, :] = jnp.where(live, readout_ref[...], 0.0)
        species = species_ref[block]
        mass = jnp.zeros((1, SLOTS), F32)
        for kind in range(kinds):
            mass = jnp.where(species == kind, masses_ref[kind], mass)
        mass_ref[block] = mass
        for axis in range(3):
            row = 3 * block + axis
            half_velocity = velocities_ref[row] + HALF_STEP * forces_ref[row] / mass
            half_position = positions_ref[row] + HALF_STEP * half_velocity
            mixed = (
                DECAY * half_velocity
                + jnp.sqrt((1.0 - DECAY * DECAY) / mass) * noise_ref[row]
            )
            new_positions = half_position + HALF_STEP * mixed
            mixed_ref[row] = mixed
            new_positions_ref[row] = new_positions
            geometry_ref[block, axis : axis + 1, :] = new_positions
        geometry_ref[block, 3:4, :] = species.astype(F32)
        geometry_ref[block, 4:5, :] = jnp.full(
            (1, SLOTS), counts_ref[0, 0, block], jnp.int32
        ).astype(F32)
        geometry_ref[block, 5:6, 0:13] = pair_list_ref[block].astype(F32)


def shift(cell, axis, step):
    count = lax.axis_size(axis)
    return lax.ppermute(cell, axis, [((i + step) % count, i) for i in range(count)])


def own_row(cell):
    return jnp.stack([shift(cell, "gy", -1), cell, shift(cell, "gy", 1)])


def outer_rows(row):
    return shift(row, "gx", -1), shift(row, "gx", 1)


SMEM = pl.BlockSpec(memory_space=pltpu.SMEM)


def whole(*shape):
    return pl.BlockSpec(
        shape, lambda column: (0,) * len(shape), pipeline_mode=pl.Buffered(1)
    )


def weight(first, rows):
    return pl.BlockSpec(
        (rows, CHANNELS), lambda column: (first // rows, 0), pipeline_mode=pl.Buffered(1)
    )


def result(*shape):
    return pl.BlockSpec(shape, lambda column: (0,) * len(shape))


def at_column(*shape):
    return pl.BlockSpec((1,) + shape, lambda column: (column,) + (0,) * len(shape))


def at_centre(*shape):
    return pl.BlockSpec((1,) + shape, lambda column: (1,) + (0,) * len(shape))


def outer_specs(*shape):
    zeros = (0,) * len(shape)
    return [
        pl.BlockSpec((1,) + shape, lambda column: (jnp.minimum(column, 2),) + zeros),
        pl.BlockSpec((1,) + shape, lambda column: (jnp.maximum(column - 3, 0),) + zeros),
    ]


def call(kernel, name, columns, out_shape, in_specs, out_specs, scratch, flops):
    return pl.pallas_call(
        kernel,
        name=name,
        out_shape=out_shape,
        grid=(columns,),
        in_specs=in_specs,
        out_specs=out_specs,
        scratch_shapes=scratch,
        cost_estimate=pl.CostEstimate(
            flops=columns * flops, bytes_accessed=columns * PAIR_BYTES, transcendentals=0
        ),
        compiler_params=pltpu.CompilerParams(
            dimension_semantics=("arbitrary",), vmem_limit_bytes=LIMIT
        ),
    )


def shape_of(*shape, kind=F32):
    return jax.ShapeDtypeStruct(shape, kind)


PAIR_BYTES = ORDERS * ATOMS * ATOMS * 2
PAIR_FLOPS = ORDERS * ATOMS * ATOMS * CHANNELS * 2


def on_device(
    positions, velocities, forces, noise, species, counts, pair_list, masses, embedding,
    radial_one, mix_one, radial_two, mix_two, readout,
):
    vmem = pl.BlockSpec(memory_space=pltpu.VMEM)
    rows = (3 * COLUMN, 1, SLOTS)
    new_positions, geometry, mixed_velocity, atom_mass, weights = pl.pallas_call(
        prepare_kernel,
        name="prepare",
        out_shape=(
            shape_of(*rows),
            shape_of(COLUMN, 8, SLOTS),
            shape_of(*rows),
            shape_of(COLUMN, 1, SLOTS),
            shape_of(WEIGHT_ROWS, CHANNELS),
        ),
        in_specs=[SMEM, SMEM] + [vmem] * 12,
    )(
        counts, masses, positions.reshape(rows), velocities.reshape(rows), forces.reshape(rows),
        noise.reshape(rows), species.reshape(COLUMN, 1, SLOTS), pair_list.reshape(COLUMN, 1, 13),
        embedding, radial_one, radial_two, mix_one, mix_two, readout[None, :],
    )

    cols = pltpu.VMEM((3, ATOMS, SLOTS), F32)
    place = pltpu.VMEM((1, COLUMN, 8, SLOTS), F32)
    message = pltpu.VMEM((ATOMS, CHANNELS), F32)
    square = pltpu.VMEM((SLOTS, SLOTS), F32)
    flags = [pltpu.VMEM((16, SLOTS), F32), pltpu.VMEM((16, SLOTS), F32)]
    pairs = (ORDERS, ATOMS, ATOMS)
    cell = (COLUMN, 8, SLOTS)
    field = (ATOMS, CHANNELS)
    own_spec = at_centre(*cell)
    radial_one_spec = weight(RADIAL_ONE, ORDERS)
    radial_two_spec = weight(RADIAL_TWO, ORDERS)
    mix_one_spec = weight(MIX_ONE, CHANNELS)
    mix_two_spec = weight(MIX_TWO, CHANNELS)
    wide_spec = weight(WIDE, SLOTS)
    upstream_spec = weight(UPSTREAM, ATOMS)

    geometry_row = own_row(geometry)
    geometry_outer = outer_rows(geometry_row)
    geometries = (geometry_outer[0], geometry_row, geometry_outer[1])
    basis_scratch = [cols, place, square, *flags, message, pltpu.VMEM(field, BF16)]
    basis_row, message_row = call(
        functools.partial(basis_kernel, 1),
        "basis_row",
        3,
        (shape_of(3, *pairs, kind=BF16), shape_of(*field)),
        [own_spec, at_column(*cell), wide_spec, radial_one_spec],
        (at_column(*pairs), result(*field)),
        basis_scratch,
        PAIR_FLOPS,
    )(geometry_row, geometry_row, weights, weights)
    basis_outer, hidden, first_gate = call(
        functools.partial(basis_kernel, OUTER),
        "basis_outer",
        6,
        (shape_of(6, *pairs, kind=BF16), shape_of(*field, kind=BF16), shape_of(*field)),
        [own_spec, *outer_specs(*cell), wide_spec, radial_one_spec, mix_one_spec, whole(*field)],
        (at_column(*pairs), result(*field), result(*field)),
        basis_scratch,
        PAIR_FLOPS,
    )(geometry_row, *geometry_outer, weights, weights, weights, message_row)

    def slope_of(group, before):
        sums = (ORDERS, ATOMS, SLOTS)
        return call(
            functools.partial(slope_kernel, group),
            f"slope_{group}",
            3,
            (shape_of(3, *pairs, kind=BF16), shape_of(*sums)),
            [own_spec, at_column(*cell)] + [whole(*sums)] * len(before),
            (at_column(*pairs), result(*sums)),
            [cols, square, *flags, pltpu.VMEM((SLOTS, ATOMS), BF16)],
            PAIR_FLOPS,
        )(geometry_row, geometries[group], *before)

    def gather_row(name, row):
        return call(
            gather_kernel,
            name,
            3,
            shape_of(*field),
            [at_column(*pairs), at_column(*field), radial_two_spec],
            result(*field),
            [message],
            PAIR_FLOPS,
        )(basis_row, row, weights)

    hidden_row = own_row(hidden)
    slope_1, kind_sums = slope_of(1, ())
    hidden_row, kind_sums = lax.optimization_barrier((hidden_row, kind_sums))
    hidden_outer = outer_rows(hidden_row)
    second_row = gather_row("second_row", hidden_row)
    slope_0, kind_sums = slope_of(0, (kind_sums,))
    second_row, kind_sums = lax.optimization_barrier((second_row, kind_sums))
    message_grad = call(
        second_kernel,
        "second_outer",
        6,
        shape_of(*field, kind=BF16),
        [
            at_column(*pairs), *outer_specs(*field), radial_two_spec, mix_two_spec, upstream_spec,
            whole(*field),
        ],
        result(*field),
        [message],
        PAIR_FLOPS,
    )(basis_outer, *hidden_outer, weights, weights, weights, second_row)

    grad_row = own_row(message_grad)
    slope_2, kind_sums = slope_of(2, (kind_sums,))
    grad_row, kind_sums = lax.optimization_barrier((grad_row, kind_sums))
    slopes = (slope_0, slope_1, slope_2)
    grad_outer = outer_rows(grad_row)
    projected = call(
        first_kernel,
        "first_outer",
        6,
        shape_of(ORDERS * KINDS, ATOMS, kind=BF16),
        [
            at_column(*pairs), *outer_specs(*field), radial_two_spec, mix_one_spec, upstream_spec,
            whole(*field), weight(TABLE, ORDERS * KINDS), whole(*field),
        ],
        result(ORDERS * KINDS, ATOMS),
        [message],
        PAIR_FLOPS,
    )(
        basis_outer, *grad_outer, weights, weights, weights, first_gate, weights,
        gather_row("first_row", grad_row),
    )

    hiddens = (hidden_outer[0], hidden_row, hidden_outer[1])
    grads = (grad_outer[0], grad_row, grad_outer[1])
    forces_so_far = ()
    for group in (1, 0, 2):
        total = call(
            functools.partial(pair_kernel, group),
            f"pair_{group}",
            3,
            shape_of(3, ATOMS, SLOTS),
            [
                own_spec, at_column(*cell), at_column(*pairs), at_column(*field),
                at_column(*field), at_centre(*field), at_centre(*field), radial_two_spec,
            ]
            + [whole(3, ATOMS, SLOTS)] * len(forces_so_far),
            result(3, ATOMS, SLOTS),
            [
                cols, pltpu.VMEM((COLUMN, ORDERS * SLOTS, 2 * CHANNELS), BF16),
                pltpu.VMEM((ATOMS, 2 * CHANNELS), BF16),
            ],
            2 * PAIR_FLOPS,
        )(
            geometry_row, geometries[group], slopes[group], hiddens[group], grads[group],
            hidden_row, grad_row, weights, *forces_so_far,
        )
        forces_so_far = (total,)

    projected_row = own_row(projected)
    projected_outer = outer_rows(projected_row)
    projecteds = (projected_outer[0], projected_row, projected_outer[1])
    kinds = (ORDERS * KINDS, ATOMS)
    tables = pltpu.VMEM((ORDERS, SLOTS, ATOMS), BF16)
    kind_specs = [at_column(*pairs), at_column(*kinds), at_column(*cell)]
    near_kind = ()
    for group in (1, 0):
        near_kind = (
            call(
                functools.partial(kind_kernel, group),
                f"last_{group}",
                3,
                shape_of(ATOMS, SLOTS),
                kind_specs + [whole(ATOMS, SLOTS)] * len(near_kind),
                result(ATOMS, SLOTS),
                [tables],
                PAIR_FLOPS,
            )(slopes[group], projecteds[group], geometries[group], *near_kind),
        )
    new_forces, new_velocities = call(
        last_kernel,
        "last_2",
        3,
        (shape_of(*rows), shape_of(*rows)),
        kind_specs
        + [
            whole(ATOMS, SLOTS), at_centre(*kinds), own_spec, whole(3, ATOMS, SLOTS),
            whole(ORDERS, ATOMS, SLOTS), whole(*rows), whole(COLUMN, 1, SLOTS),
        ],
        (result(*rows), result(*rows)),
        [cols, tables, pltpu.VMEM((ATOMS, SLOTS), F32)],
        PAIR_FLOPS,
    )(
        slopes[2], projecteds[2], geometries[2], *near_kind, projected_row, geometry_row,
        *forces_so_far, kind_sums, mixed_velocity, atom_mass,
    )
    return tuple(
        value.reshape(positions.shape) for value in (new_positions, new_velocities, new_forces)
    )


def solution(mesh):
    split_spec = P("gx", "gy")
    return jax.shard_map(
        on_device,
        mesh=mesh,
        in_specs=(split_spec,) * 7 + (P(),) * 7,
        out_specs=(split_spec,) * 3,
        check_vma=False,
    )
```

time: 194 us -> 124 us (0.64)
  the two profiles are of different devices: /device:TPU:1 before, /device:TPU:0 now
where the time goes in v2:
time: 124 us
  Pallas kernels  75.6 us (61%)
  starting transfers between devices  34.1 us (28%)
  waiting for transfers between devices  8.55 us (7%)
  local copies, waits for them, and re-layouts  4.09 us (3%)
    ppermute x16, starting transfers between devices, shift(): lax.ppermute(cell, axis, [((i + step) % count, i) for i in range(count)])  34.1 us
    pallas_call x3, Pallas kernels, slope_of(): call(functools.partial(slope_kernel, group), f'slope_{group}', 3, (shape_...  22.1 us
    pallas_call x3, Pallas kernels, on_device(): call(functools.partial(pair_kernel, group), f'pair_{group}', 3, shape_of(...  11.9 us
    pallas_call x1, Pallas kernels, on_device(): call(functools.partial(basis_kernel, OUTER), 'basis_outer', 6, (shape_of(...  10.1 us
    ppermute x16, waiting for transfers between devices, shift(): lax.ppermute(cell, axis, [((i + step) % count, i) for i in range(count)])  8.55 us
    pallas_call x1, Pallas kernels, on_device(): call(first_kernel, 'first_outer', 6, shape_of(ORDERS * KINDS, ATOMS, kind...  5.37 us
    pallas_call x2, Pallas kernels, on_device(): call(functools.partial(kind_kernel, group), f'last_{group}', 3, shape_of(...  5.27 us
    pallas_call x1, Pallas kernels, on_device(): call(second_kernel, 'second_outer', 6, shape_of(*field, kind=BF16), [at_c...  5.14 us
  transfers between devices with their start and end apart: 16, of which 4 were waited for; matrix products, arithmetic and copies ran while one was open for 0% of the time, Pallas kernels for 40%

profile of v2, /device:TPU:0, one launch (start us, length us, event | category | flops | bytes accessed | tf_op | source)
XLA Modules:
  0.0 124.1 jit_solution(5146316067767323400)
XLA Ops:
  0.6 1.8 %prepare.1 = (f32[9,1,128]{2,1,0:T(1,128)}, f32[3,8,128]{2,1,0:T(8,128)}, f32[9,1,128]{2,1,0:T(1,128)}, f32[3,1,128]{2,1,0:T(1,128)}, f32[1152,128]{1,0:T(8,128)}) custom-call(s32[1,1,3]{2,1,0:T(1,128)} %counts_ref.1, f32[6]{0:T(128)} %masses_ref.1, f32[9,1,128]{2,1,0:T(1,128)} %bitcast.40, f32[9,1,128]{2,1,0:T(1,128)} %bitcast.41, f32[9,1,128]{2,1,0:T(1,128)} %bitcast.42, ...), custom_call_target="tpu_custom_call" | custom-call | tf_op jit(solution)/shard_map/prepare/pallas_call | solution.py:598
  2.4 1.7 %collective-permute-start.1 = (f32[3,8,128]{2,1,0:T(8,128)}, f32[3,8,128]{2,1,0:T(8,128)S(1)}, u32[]{:S(2)}, u32[]{:S(2)}) collective-permute-start(f32[3,8,128]{2,1,0:T(8,128)} %get-tuple-element.28), channel_id=1, source_target_pairs={{1,0},{2,1},{3,2},{4,3},{5,4},{6,5},{7,6},{8,7},{9,8},{10,9},{11,1... | collective-permute-start | bytes 36872 | tf_op jit(solution)/shard_map/ppermute | solution.py:520
  4.1 0.0 collective-permute-start
  4.1 1.6 %collective-permute-done.1 = f32[3,8,128]{2,1,0:T(8,128)S(1)} collective-permute-done((f32[3,8,128]{2,1,0:T(8,128)}, f32[3,8,128]{2,1,0:T(8,128)S(1)}, u32[]{:S(2)}, u32[]{:S(2)}) %collective-permute-start.1) | collective-permute-done | bytes 12320 | tf_op jit(solution)/shard_map/ppermute | solution.py:520
  5.7 3.8 %collective-permute-done = f32[3,8,128]{2,1,0:T(8,128)S(1)} collective-permute-done((f32[3,8,128]{2,1,0:T(8,128)}, f32[3,8,128]{2,1,0:T(8,128)S(1)}, u32[]{:S(2)}, u32[]{:S(2)}) %collective-permute-start) | collective-permute-done | bytes 12320 | tf_op jit(solution)/shard_map/ppermute | solution.py:520
  9.5 0.7 pad_maximum_fusion.3.own_ref.refs_0_.near_ref
  10.3 8.0 %collective-permute-start.2 = (f32[3,3,8,128]{3,2,1,0:T(8,128)S(1)}, f32[3,3,8,128]{3,2,1,0:T(8,128)S(1)}, u32[]{:S(2)}, u32[]{:S(2)}) collective-permute-start(f32[3,3,8,128]{3,2,1,0:T(8,128)S(1)} %pad_maximum_fusion.3.own_ref.refs_0_.near_ref), channel_id=1, source_target_pairs={{16,0},{32,16},{48,32},{64,48},{80,64},{96,80},{112,96},{128,112},... | collective-permute-start | bytes 110600 | tf_op jit(solution)/shard_map/ppermute | solution.py:520
  18.3 0.0 collective-permute-start.3
  18.3 1.1 copy-done
  19.3 5.0 %basis_row.1 = (bf16[3,8,384,384]{3,2,1,0:T(8,128)(2,1)S(1)}, f32[384,128]{1,0:T(8,128)S(1)}) custom-call(f32[3,3,8,128]{3,2,1,0:T(8,128)S(1)} %pad_maximum_fusion.3.own_ref.refs_0_.near_ref, f32[3,3,8,128]{3,2,1,0:T(8,128)S(1)} %pad_maximum_fusion.3.own_ref.refs_0_.near_ref, f32[1152,128]{1,0:T(8,128)S(1)} %copy-done, f32[1152,128]{1,0:T(8,128)S(1)} %copy-done), custom_call_target="tpu_custom_call" | custom-call | flops 905969664 | bytes 7077888 | tf_op jit(solution)/shard_map/basis_row/pallas_call | solution.py:635
  24.4 0.0 collective-permute-done.2.refs_1_.near_ref
  24.4 1.4 %collective-permute-done.3.refs_0_.near_ref = f32[3,3,8,128]{3,2,1,0:T(8,128)S(1)} collective-permute-done((f32[3,3,8,128]{3,2,1,0:T(8,128)S(1)}, f32[3,3,8,128]{3,2,1,0:T(8,128)S(1)}, u32[]{:S(2)}, u32[]{:S(2)}) %collective-permute-start.3) | collective-permute-done | bytes 36896 | tf_op jit(solution)/shard_map/ppermute | solution.py:520
  25.8 10.1 %basis_outer.1 = (bf16[6,8,384,384]{3,2,1,0:T(8,128)(2,1)S(1)}, bf16[384,128]{1,0:T(8,128)(2,1)S(1)}, f32[384,128]{1,0:T(8,128)S(1)}) custom-call(f32[3,3,8,128]{3,2,1,0:T(8,128)S(1)} %pad_maximum_fusion.3.own_ref.refs_0_.near_ref, f32[3,3,8,128]{3,2,1,0:T(8,128)S(1)} %collective-permute-done.3.refs_0_.near_ref, ...), custom_call_target="tpu_custom_call" | custom-call | flops 1811939328 | bytes 14155776 | tf_op jit(solution)/shard_map/basis_outer/pallas_call | solution.py:645
  36.0 0.1 collective-permute-start.5
  36.1 0.5 collective-permute-start.4
  36.6 7.4 %slope_1.1 = (bf16[3,8,384,384]{3,2,1,0:T(8,128)(2,1)S(1)}, f32[8,384,128]{2,1,0:T(8,128)S(1)}) custom-call(f32[3,3,8,128]{3,2,1,0:T(8,128)S(1)} %pad_maximum_fusion.3.own_ref.refs_0_.near_ref, f32[3,3,8,128]{3,2,1,0:T(8,128)S(1)} %pad_maximum_fusion.3.own_ref.refs_0_.near_ref), custom_call_target="tpu_custom_call" | custom-call | flops 905969664 | bytes 7077888 | tf_op jit(solution)/shard_map/slope_1/pallas_call | solution.py:658
  44.0 0.0 collective-permute-done.5
  44.0 0.0 collective-permute-done.4
  44.0 0.1 collective-permute-start.6
  44.1 5.6 %collective-permute-start.7 = (bf16[3,384,128]{2,1,0:T(8,128)(2,1)S(1)}, bf16[3,384,128]{2,1,0:T(8,128)(2,1)S(1)}, u32[]{:S(2)}, u32[]{:S(2)}) collective-permute-start(bf16[3,384,128]{2,1,0:T(8,128)(2,1)S(1)} %pad_maximum_fusion.field_ref.near_hidden_ref.hidden_ref), channel_id=1, source_target_pairs={{16,0},{32,16},{48,32},{64,48},{80,64},{96,80},{112,96},{128,112},... | collective-permute-start | bytes 884744 | tf_op jit(solution)/shard_map/ppermute | solution.py:520
  49.8 2.4 %second_row.1.before_ref = f32[384,128]{1,0:T(8,128)S(1)} custom-call(bf16[3,8,384,384]{3,2,1,0:T(8,128)(2,1)S(1)} %get-tuple-element.30.basis_ref, bf16[3,384,128]{2,1,0:T(8,128)(2,1)S(1)} %pad_maximum_fusion.field_ref.near_hidden_ref.hidden_ref, f32[1152,128]{1,0:T(8,128)S(1)} %copy-done.1), custom_call_target="tpu_custom_call" | custom-call | flops 905969664 | bytes 7077888 | tf_op jit(solution)/shard_map/second_row/pallas_call | solution.py:670
  52.2 7.3 %slope_0.1 = (bf16[3,8,384,384]{3,2,1,0:T(8,128)(2,1)S(1)}, f32[8,384,128]{2,1,0:T(8,128)S(1)}) custom-call(f32[3,3,8,128]{3,2,1,0:T(8,128)S(1)} %pad_maximum_fusion.3.own_ref.refs_0_.near_ref, f32[3,3,8,128]{3,2,1,0:T(8,128)S(1)} %collective-permute-done.3.refs_0_.near_ref, f32[8,384,128]{2,1,0:T(8,128)S(1)} %get-tuple-element.35.refs_0_), custom_call_target="tpu_custom_call" | custom-call | flops 905969664 | bytes 7077888 | tf_op jit(solution)/shard_map/slope_0/pallas_call | solution.py:658
  59.5 0.0 collective-permute-done.6.hidden_0.near_hidden_ref
  59.5 0.0 collective-permute-done.7.hidden_2.near_hidden_ref
  59.5 5.1 %second_outer.1 = bf16[384,128]{1,0:T(8,128)(2,1)S(1)} custom-call(bf16[6,8,384,384]{3,2,1,0:T(8,128)(2,1)S(1)} %get-tuple-element.39.basis_ref, bf16[3,384,128]{2,1,0:T(8,128)(2,1)S(1)} %collective-permute-done.6.hidden_0.near_hidden_ref, bf16[3,384,128]{2,1,0:T(8,128)(2,1)S(1)} %collective-permute-done.7.hidden_2.near_hidden_ref, ...), custom_call_target="tpu_custom_call" | custom-call | flops 1811939328 | bytes 14155776 | tf_op jit(solution)/shard_map/second_outer/pallas_call | solution.py:688
  64.7 3.0 %collective-permute-start.9 = (bf16[384,128]{1,0:T(8,128)(2,1)S(1)}, bf16[384,128]{1,0:T(8,128)(2,1)S(1)}, u32[]{:S(2)}, u32[]{:S(2)}) collective-permute-start(bf16[384,128]{1,0:T(8,128)(2,1)S(1)} %second_outer.1), channel_id=1, source_target_pairs={{1,0},{2,1},{3,2},{4,3},{5,4},{6,5},{7,6},{8,7},{9,8},{10,9},{11,1... | collective-permute-start | bytes 294920 | tf_op jit(solution)/shard_map/ppermute | solution.py:520
  67.6 0.0 collective-permute-start.8
  67.6 7.4 %slope_2.1 = (bf16[3,8,384,384]{3,2,1,0:T(8,128)(2,1)S(1)}, f32[8,384,128]{2,1,0:T(8,128)S(1)}) custom-call(f32[3,3,8,128]{3,2,1,0:T(8,128)S(1)} %pad_maximum_fusion.3.own_ref.refs_0_.near_ref, f32[3,3,8,128]{3,2,1,0:T(8,128)S(1)} %collective-permute-done.2.refs_1_.near_ref, f32[8,384,128]{2,1,0:T(8,128)S(1)} %get-tuple-element.37.refs_0_), custom_call_target="tpu_custom_call" | custom-call | flops 905969664 | bytes 7077888 | tf_op jit(solution)/shard_map/slope_2/pallas_call | solution.py:658
  75.1 0.0 collective-permute-done.9
  75.1 0.1 collective-permute-start.10
  75.2 5.6 %collective-permute-start.11 = (bf16[3,384,128]{2,1,0:T(8,128)(2,1)S(1)}, bf16[3,384,128]{2,1,0:T(8,128)(2,1)S(1)}, u32[]{:S(2)}, u32[]{:S(2)}) collective-permute-start(bf16[3,384,128]{2,1,0:T(8,128)(2,1)S(1)} %pad_maximum_fusion.1.field_ref.near_grad_ref.grad_ref), channel_id=1, source_target_pairs={{16,0},{32,16},{48,32},{64,48},{80,64},{96,80},{112,96},{128,112},... | collective-permute-start | bytes 884744 | tf_op jit(solution)/shard_map/ppermute | solution.py:520
  80.8 3.0 %copy-done.3 = bf16[3,8,384,384]{3,2,1,0:T(8,128)(2,1)S(1)} copy-done((bf16[3,8,384,384]{3,2,1,0:T(8,128)(2,1)S(1)}, bf16[3,8,384,384]{3,2,1,0:T(8,128)(2,1)}, u32[]{:S(2)}) %copy-start.3) | copy-done | bytes 7077912
  83.8 2.4 %first_row.1.before_ref = f32[384,128]{1,0:T(8,128)S(1)} custom-call(bf16[3,8,384,384]{3,2,1,0:T(8,128)(2,1)S(1)} %copy-done.3, bf16[3,384,128]{2,1,0:T(8,128)(2,1)S(1)} %pad_maximum_fusion.1.field_ref.near_grad_ref.grad_ref, f32[1152,128]{1,0:T(8,128)S(1)} %copy-done.1), custom_call_target="tpu_custom_call" | custom-call | flops 905969664 | bytes 7077888 | tf_op jit(solution)/shard_map/first_row/pallas_call | solution.py:670
  86.2 4.0 %pair_1.1.refs_0_ = f32[3,384,128]{2,1,0:T(8,128)S(1)} custom-call(f32[3,3,8,128]{3,2,1,0:T(8,128)S(1)} %pad_maximum_fusion.3.own_ref.refs_0_.near_ref, f32[3,3,8,128]{3,2,1,0:T(8,128)S(1)} %pad_maximum_fusion.3.own_ref.refs_0_.near_ref, bf16[3,8,384,384]{3,2,1,0:T(8,128)(2,1)S(1)} %get-tuple-element.45.slope_ref, ...), custom_call_target="tpu_custom_call" | custom-call | flops 1811939328 | bytes 7077888 | tf_op jit(solution)/shard_map/pair_1/pallas_call | solution.py:728
  90.2 0.0 collective-permute-done.10.grad_0.near_grad_ref
  90.2 5.4 %first_outer.1 = bf16[64,384]{1,0:T(8,128)(2,1)S(1)} custom-call(bf16[6,8,384,384]{3,2,1,0:T(8,128)(2,1)S(1)} %get-tuple-element.39.basis_ref, bf16[3,384,128]{2,1,0:T(8,128)(2,1)S(1)} %collective-permute-done.10.grad_0.near_grad_ref, bf16[3,384,128]{2,1,0:T(8,128)(2,1)S(1)} %collective-permute-done.11.grad_2.near_grad_ref, f32[1152,128]{1,0:T(8,128)S(1)} %copy-done.1, ...), custom_call_target="tpu_custom_call" | custom-call | flops 1811939328 | bytes 14155776 | tf_op jit(solution)/shard_map/first_outer/pallas_call | solution.py:707
  95.6 3.4 %collective-permute-start.13 = (bf16[64,384]{1,0:T(8,128)(2,1)S(1)}, bf16[64,384]{1,0:T(8,128)(2,1)S(1)}, u32[]{:S(2)}, u32[]{:S(2)}) collective-permute-start(bf16[64,384]{1,0:T(8,128)(2,1)S(1)} %first_outer.1), channel_id=1, source_target_pairs={{1,0},{2,1},{3,2},{4,3},{5,4},{6,5},{7,6},{8,7},{9,8},{10,9},{11,1... | collective-permute-start | bytes 147464 | tf_op jit(solution)/shard_map/ppermute | solution.py:520
  99.0 0.0 collective-permute-start.12
  99.0 4.0 %pair_0.1.refs_0_ = f32[3,384,128]{2,1,0:T(8,128)S(1)} custom-call(f32[3,3,8,128]{3,2,1,0:T(8,128)S(1)} %pad_maximum_fusion.3.own_ref.refs_0_.near_ref, f32[3,3,8,128]{3,2,1,0:T(8,128)S(1)} %collective-permute-done.3.refs_0_.near_ref, bf16[3,8,384,384]{3,2,1,0:T(8,128)(2,1)S(1)} %get-tuple-element.44.slope_ref, ...), custom_call_target="tpu_custom_call" | custom-call | flops 1811939328 | bytes 7077888 | tf_op jit(solution)/shard_map/pair_0/pallas_call | solution.py:728
  103.0 1.6 %collective-permute-done.12 = bf16[64,384]{1,0:T(8,128)(2,1)S(1)} collective-permute-done((bf16[64,384]{1,0:T(8,128)(2,1)S(1)}, bf16[64,384]{1,0:T(8,128)(2,1)S(1)}, u32[]{:S(2)}, u32[]{:S(2)}) %collective-permute-start.12) | collective-permute-done | bytes 49184 | tf_op jit(solution)/shard_map/ppermute | solution.py:520
  104.6 0.1 collective-permute-start.15
  104.7 4.0 %pair_2.1.force_ref = f32[3,384,128]{2,1,0:T(8,128)S(1)} custom-call(f32[3,3,8,128]{3,2,1,0:T(8,128)S(1)} %pad_maximum_fusion.3.own_ref.refs_0_.near_ref, f32[3,3,8,128]{3,2,1,0:T(8,128)S(1)} %collective-permute-done.2.refs_1_.near_ref, bf16[3,8,384,384]{3,2,1,0:T(8,128)(2,1)S(1)} %get-tuple-element.38.slope_ref, ...), custom_call_target="tpu_custom_call" | custom-call | flops 1811939328 | bytes 7077888 | tf_op jit(solution)/shard_map/pair_2/pallas_call | solution.py:728
  108.7 0.0 copy-start.4
  108.7 0.0 copy-start.5
  108.7 5.9 %collective-permute-start.14 = (bf16[3,64,384]{2,1,0:T(8,128)(2,1)S(1)}, bf16[3,64,384]{2,1,0:T(8,128)(2,1)S(1)}, u32[]{:S(2)}, u32[]{:S(2)}) collective-permute-start(bf16[3,64,384]{2,1,0:T(8,128)(2,1)S(1)} %pad_maximum_fusion.2.projected_ref.own_projected_ref), channel_id=1, source_target_pairs={{16,0},{32,16},{48,32},{64,48},{80,64},{96,80},{112,96},{128,112},... | collective-permute-start | bytes 442376 | tf_op jit(solution)/shard_map/ppermute | solution.py:520
  114.7 2.6 %last_1.1.refs_0_ = f32[384,128]{1,0:T(8,128)S(1)} custom-call(bf16[3,8,384,384]{3,2,1,0:T(8,128)(2,1)S(1)} %get-tuple-element.45.slope_ref, bf16[3,64,384]{2,1,0:T(8,128)(2,1)S(1)} %pad_maximum_fusion.2.projected_ref.own_projected_ref, f32[3,3,8,128]{3,2,1,0:T(8,128)S(1)} %pad_maximum_fusion.3.own_ref.refs_0_.near_ref), custom_call_target="tpu_custom_call" | custom-call | flops 905969664 | bytes 7077888 | tf_op jit(solution)/shard_map/last_1/pallas_call | solution.py:759
  117.3 2.6 %last_0.1.before_ref = f32[384,128]{1,0:T(8,128)S(1)} custom-call(bf16[3,8,384,384]{3,2,1,0:T(8,128)(2,1)S(1)} %get-tuple-element.44.slope_ref, bf16[3,64,384]{2,1,0:T(8,128)(2,1)S(1)} %collective-permute-done.15.projected_ref, f32[3,3,8,128]{3,2,1,0:T(8,128)S(1)} %collective-permute-done.3.refs_0_.near_ref, f32[384,128]{1,0:T(8,128)S(1)} %last_1.1.refs_0_), custom_call_target="tpu_custom_call" | custom-call | flops 905969664 | bytes 7077888 | tf_op jit(solution)/shard_map/last_0/pallas_call | solution.py:759
  120.0 4.1 %last_2.1 = (f32[9,1,128]{2,1,0:T(1,128)}, f32[9,1,128]{2,1,0:T(1,128)}) custom-call(bf16[3,8,384,384]{3,2,1,0:T(8,128)(2,1)S(1)} %get-tuple-element.38.slope_ref, bf16[3,64,384]{2,1,0:T(8,128)(2,1)S(1)} %collective-permute-done.14.projected_ref, f32[3,3,8,128]{3,2,1,0:T(8,128)S(1)} %collective-permute-done.2.refs_1_.near_ref, ...), custom_call_target="tpu_custom_call" | custom-call | flops 905969664 | bytes 7077888 | tf_op jit(solution)/shard_map/last_2/pallas_call | solution.py:770
  (16 shorter events, 0.1 us)
Async XLA Ops:
  2.4 3.3 %collective-permute-start.1 = (f32[3,8,128]{2,1,0:T(8,128)}, f32[3,8,128]{2,1,0:T(8,128)S(1)}, u32[]{:S(2)}, u32[]{:S(2)}) collective-permute-start(f32[3,8,128]{2,1,0:T(8,128)} %get-tuple-element.28), channel_id=1, source_target_pairs={{1,0},{2,1},{3,2},{4,3},{5,4},{6,5},{7,6},{8,7},{9,8},{10,9},{11,1... | collective-permute-start | bytes 36872 | tf_op jit(solution)/shard_map/ppermute | solution.py:520
  4.1 5.4 %collective-permute-start = (f32[3,8,128]{2,1,0:T(8,128)}, f32[3,8,128]{2,1,0:T(8,128)S(1)}, u32[]{:S(2)}, u32[]{:S(2)}) collective-permute-start(f32[3,8,128]{2,1,0:T(8,128)} %get-tuple-element.28), channel_id=1, source_target_pairs={{15,0},{0,1},{1,2},{2,3},{3,4},{4,5},{5,6},{6,7},{7,8},{8,9},{9,10... | collective-permute-start | bytes 36872 | tf_op jit(solution)/shard_map/ppermute | solution.py:520
  10.3 14.2 %collective-permute-start.2 = (f32[3,3,8,128]{3,2,1,0:T(8,128)S(1)}, f32[3,3,8,128]{3,2,1,0:T(8,128)S(1)}, u32[]{:S(2)}, u32[]{:S(2)}) collective-permute-start(f32[3,3,8,128]{3,2,1,0:T(8,128)S(1)} %pad_maximum_fusion.3.own_ref.refs_0_.near_ref), channel_id=1, source_target_pairs={{16,0},{32,16},{48,32},{64,48},{80,64},{96,80},{112,96},{128,112},... | collective-permute-start | bytes 110600 | tf_op jit(solution)/shard_map/ppermute | solution.py:520
  18.3 7.6 %collective-permute-start.3 = (f32[3,3,8,128]{3,2,1,0:T(8,128)S(1)}, f32[3,3,8,128]{3,2,1,0:T(8,128)S(1)}, u32[]{:S(2)}, u32[]{:S(2)}) collective-permute-start(f32[3,3,8,128]{3,2,1,0:T(8,128)S(1)} %pad_maximum_fusion.3.own_ref.refs_0_.near_ref), channel_id=1, source_target_pairs={{240,0},{0,16},{16,32},{32,48},{48,64},{64,80},{80,96},{96,112},{1... | collective-permute-start | bytes 110600 | tf_op jit(solution)/shard_map/ppermute | solution.py:520
  18.3 1.1 copy-start
  19.3 30.4 %copy-start.1 = (f32[1152,128]{1,0:T(8,128)S(1)}, f32[1152,128]{1,0:T(8,128)}, u32[]{:S(2)}) copy-start(f32[1152,128]{1,0:T(8,128)} %get-tuple-element.29.refs_1_.refs_2_.refs_3_.refs_4_.radial_ref.mix_ref.upstream_ref.table_ref) | copy-start | bytes 1769476
  24.4 25.4 %copy-start.2 = (bf16[3,8,384,384]{3,2,1,0:T(8,128)(2,1)}, bf16[3,8,384,384]{3,2,1,0:T(8,128)(2,1)S(1)}, u32[]{:S(2)}) copy-start(bf16[3,8,384,384]{3,2,1,0:T(8,128)(2,1)S(1)} %get-tuple-element.30.basis_ref) | copy-start | bytes 21233668
  36.0 8.0 %collective-permute-start.5 = (bf16[384,128]{1,0:T(8,128)(2,1)S(1)}, bf16[384,128]{1,0:T(8,128)(2,1)S(1)}, u32[]{:S(2)}, u32[]{:S(2)}) collective-permute-start(bf16[384,128]{1,0:T(8,128)(2,1)S(1)} %get-tuple-element.32), channel_id=1, source_target_pairs={{1,0},{2,1},{3,2},{4,3},{5,4},{6,5},{7,6},{8,7},{9,8},{10,9},{11,1... | collective-permute-start | bytes 294920 | tf_op jit(solution)/shard_map/ppermute | solution.py:520
  36.1 7.9 %collective-permute-start.4 = (bf16[384,128]{1,0:T(8,128)(2,1)S(1)}, bf16[384,128]{1,0:T(8,128)(2,1)S(1)}, u32[]{:S(2)}, u32[]{:S(2)}) collective-permute-start(bf16[384,128]{1,0:T(8,128)(2,1)S(1)} %get-tuple-element.32), channel_id=1, source_target_pairs={{15,0},{0,1},{1,2},{2,3},{3,4},{4,5},{5,6},{6,7},{7,8},{8,9},{9,10... | collective-permute-start | bytes 294920 | tf_op jit(solution)/shard_map/ppermute | solution.py:520
  44.0 15.5 %collective-permute-start.6 = (bf16[3,384,128]{2,1,0:T(8,128)(2,1)S(1)}, bf16[3,384,128]{2,1,0:T(8,128)(2,1)S(1)}, u32[]{:S(2)}, u32[]{:S(2)}) collective-permute-start(bf16[3,384,128]{2,1,0:T(8,128)(2,1)S(1)} %pad_maximum_fusion.field_ref.near_hidden_ref.hidden_ref), channel_id=1, source_target_pairs={{240,0},{0,16},{16,32},{32,48},{48,64},{64,80},{80,96},{96,112},{1... | collective-permute-start | bytes 884744 | tf_op jit(solution)/shard_map/ppermute | solution.py:520
  44.1 15.4 %collective-permute-start.7 = (bf16[3,384,128]{2,1,0:T(8,128)(2,1)S(1)}, bf16[3,384,128]{2,1,0:T(8,128)(2,1)S(1)}, u32[]{:S(2)}, u32[]{:S(2)}) collective-permute-start(bf16[3,384,128]{2,1,0:T(8,128)(2,1)S(1)} %pad_maximum_fusion.field_ref.near_hidden_ref.hidden_ref), channel_id=1, source_target_pairs={{16,0},{32,16},{48,32},{64,48},{80,64},{96,80},{112,96},{128,112},... | collective-permute-start | bytes 884744 | tf_op jit(solution)/shard_map/ppermute | solution.py:520
  64.7 10.4 %collective-permute-start.9 = (bf16[384,128]{1,0:T(8,128)(2,1)S(1)}, bf16[384,128]{1,0:T(8,128)(2,1)S(1)}, u32[]{:S(2)}, u32[]{:S(2)}) collective-permute-start(bf16[384,128]{1,0:T(8,128)(2,1)S(1)} %second_outer.1), channel_id=1, source_target_pairs={{1,0},{2,1},{3,2},{4,3},{5,4},{6,5},{7,6},{8,7},{9,8},{10,9},{11,1... | collective-permute-start | bytes 294920 | tf_op jit(solution)/shard_map/ppermute | solution.py:520
  67.6 7.4 %collective-permute-start.8 = (bf16[384,128]{1,0:T(8,128)(2,1)S(1)}, bf16[384,128]{1,0:T(8,128)(2,1)S(1)}, u32[]{:S(2)}, u32[]{:S(2)}) collective-permute-start(bf16[384,128]{1,0:T(8,128)(2,1)S(1)} %second_outer.1), channel_id=1, source_target_pairs={{15,0},{0,1},{1,2},{2,3},{3,4},{4,5},{5,6},{6,7},{7,8},{8,9},{9,10... | collective-permute-start | bytes 294920 | tf_op jit(solution)/shard_map/ppermute | solution.py:520
  75.1 15.1 %collective-permute-start.10 = (bf16[3,384,128]{2,1,0:T(8,128)(2,1)S(1)}, bf16[3,384,128]{2,1,0:T(8,128)(2,1)S(1)}, u32[]{:S(2)}, u32[]{:S(2)}) collective-permute-start(bf16[3,384,128]{2,1,0:T(8,128)(2,1)S(1)} %pad_maximum_fusion.1.field_ref.near_grad_ref.grad_ref), channel_id=1, source_target_pairs={{240,0},{0,16},{16,32},{32,48},{48,64},{64,80},{80,96},{96,112},{1... | collective-permute-start | bytes 884744 | tf_op jit(solution)/shard_map/ppermute | solution.py:520
  75.2 15.0 %collective-permute-start.11 = (bf16[3,384,128]{2,1,0:T(8,128)(2,1)S(1)}, bf16[3,384,128]{2,1,0:T(8,128)(2,1)S(1)}, u32[]{:S(2)}, u32[]{:S(2)}) collective-permute-start(bf16[3,384,128]{2,1,0:T(8,128)(2,1)S(1)} %pad_maximum_fusion.1.field_ref.near_grad_ref.grad_ref), channel_id=1, source_target_pairs={{16,0},{32,16},{48,32},{64,48},{80,64},{96,80},{112,96},{128,112},... | collective-permute-start | bytes 884744 | tf_op jit(solution)/shard_map/ppermute | solution.py:520
  80.8 3.0 %copy-start.3 = (bf16[3,8,384,384]{3,2,1,0:T(8,128)(2,1)S(1)}, bf16[3,8,384,384]{3,2,1,0:T(8,128)(2,1)}, u32[]{:S(2)}) copy-start(bf16[3,8,384,384]{3,2,1,0:T(8,128)(2,1)} %copy-done.2) | copy-start | bytes 21233668
  95.6 7.3 %collective-permute-start.13 = (bf16[64,384]{1,0:T(8,128)(2,1)S(1)}, bf16[64,384]{1,0:T(8,128)(2,1)S(1)}, u32[]{:S(2)}, u32[]{:S(2)}) collective-permute-start(bf16[64,384]{1,0:T(8,128)(2,1)S(1)} %first_outer.1), channel_id=1, source_target_pairs={{1,0},{2,1},{3,2},{4,3},{5,4},{6,5},{7,6},{8,7},{9,8},{10,9},{11,1... | collective-permute-start | bytes 147464 | tf_op jit(solution)/shard_map/ppermute | solution.py:520
  99.0 5.6 %collective-permute-start.12 = (bf16[64,384]{1,0:T(8,128)(2,1)S(1)}, bf16[64,384]{1,0:T(8,128)(2,1)S(1)}, u32[]{:S(2)}, u32[]{:S(2)}) collective-permute-start(bf16[64,384]{1,0:T(8,128)(2,1)S(1)} %first_outer.1), channel_id=1, source_target_pairs={{15,0},{0,1},{1,2},{2,3},{3,4},{4,5},{5,6},{6,7},{7,8},{8,9},{9,10... | collective-permute-start | bytes 147464 | tf_op jit(solution)/shard_map/ppermute | solution.py:520
  104.6 12.7 %collective-permute-start.15 = (bf16[3,64,384]{2,1,0:T(8,128)(2,1)S(1)}, bf16[3,64,384]{2,1,0:T(8,128)(2,1)S(1)}, u32[]{:S(2)}, u32[]{:S(2)}) collective-permute-start(bf16[3,64,384]{2,1,0:T(8,128)(2,1)S(1)} %pad_maximum_fusion.2.projected_ref.own_projected_ref), channel_id=1, source_target_pairs={{240,0},{0,16},{16,32},{32,48},{48,64},{64,80},{80,96},{96,112},{1... | collective-permute-start | bytes 442376 | tf_op jit(solution)/shard_map/ppermute | solution.py:520
  108.7 11.3 %copy-start.4 = (f32[9,1,128]{2,1,0:T(1,128)S(1)}, f32[9,1,128]{2,1,0:T(1,128)}, u32[]{:S(2)}) copy-start(f32[9,1,128]{2,1,0:T(1,128)} %get-tuple-element.47.mixed_ref) | copy-start | bytes 13828
  108.7 11.3 %copy-start.5 = (f32[3,1,128]{2,1,0:T(1,128)S(1)}, f32[3,1,128]{2,1,0:T(1,128)}, u32[]{:S(2)}) copy-start(f32[3,1,128]{2,1,0:T(1,128)} %get-tuple-element.48.mass_ref) | copy-start | bytes 4612
  108.7 11.2 %collective-permute-start.14 = (bf16[3,64,384]{2,1,0:T(8,128)(2,1)S(1)}, bf16[3,64,384]{2,1,0:T(8,128)(2,1)S(1)}, u32[]{:S(2)}, u32[]{:S(2)}) collective-permute-start(bf16[3,64,384]{2,1,0:T(8,128)(2,1)S(1)} %pad_maximum_fusion.2.projected_ref.own_projected_ref), channel_id=1, source_target_pairs={{16,0},{32,16},{48,32},{64,48},{80,64},{96,80},{112,96},{128,112},... | collective-permute-start | bytes 442376 | tf_op jit(solution)/shard_map/ppermute | solution.py:520

commit v3 on v2

--- a/solution.py
+++ b/solution.py
@@ -69,10 +69,11 @@
             )
 
 
-def mark_diagonal(column, diagonal):
+def mark_diagonal(part, diagonal):
     rows = lax.broadcasted_iota(jnp.int32, (SLOTS, SLOTS), 0)
     lanes = lax.broadcasted_iota(jnp.int32, (SLOTS, SLOTS), 1)
-    hit = jnp.logical_and(rows == lanes, column == 4)
+    centre = jnp.logical_and(pl.program_id(0) == 1, part == 1)
+    hit = jnp.logical_and(rows == lanes, centre)
     diagonal[...] = jnp.where(hit, FAR * FAR, 0.0)
 
 
@@ -80,29 +81,34 @@
     return (near - block + 1) % 3 - 1
 
 
-def place_of(part):
+def signs_of(part):
     step = pl.program_id(0)
     if part == OUTER:
-        return step + 3 * (step // 3)
-    return step + 3 * part
-
-
-def mark_listed(own_ref, near_ref, column, picked, listed):
-    lanes = lax.broadcasted_iota(jnp.int32, (1, SLOTS), 1)
+        return (1 - 2 * (step // 3)).astype(F32), (1 - step % 3).astype(F32)
+    return float(1 - part), (1 - step % 3).astype(F32)
+
+
+def steps_to(near_ref, near, signs):
+    return -signs[0] * near_ref[0, near, 6:7, :], -signs[1] * near_ref[0, near, 7:8, :]
+
+
+def mark_listed(own_ref, near_ref, signs, picked, listed):
+    lanes = lax.broadcasted_iota(jnp.int32, (1, SLOTS), 1).astype(F32)
     for block in range(COLUMN):
         for near in range(COLUMN):
-            stencil = column * 3 + offset_z(block, near) + 1
-            ahead = jnp.where(lanes == stencil - 14, own_ref[0, block, 5:6, :], 0.0)
-            behind = jnp.where(lanes == 12 - stencil, near_ref[0, near, 5:6, :], 0.0)
-            own = jnp.where(lanes == jnp.where(stencil == 13, 0, -1), 1.0, 0.0)
+            step_x, step_y = steps_to(near_ref, near, signs)
+            stencil = 9.0 * step_x + 3.0 * step_y + (13.0 + offset_z(block, near))
+            ahead = jnp.where(lanes == stencil - 14.0, own_ref[0, block, 5:6, :], 0.0)
+            behind = jnp.where(lanes == 12.0 - stencil, near_ref[0, near, 5:6, :], 0.0)
+            own = jnp.where(jnp.logical_and(stencil == 13.0, lanes == 0.0), 1.0, 0.0)
             row = block * COLUMN + near
             picked[row : row + 1, :] = own + ahead + behind
     sums = jnp.sum(picked[...], axis=1, keepdims=True)
     listed[...] = jnp.broadcast_to(sums, listed.shape)
 
 
-def near_rows(listed, near_ref, column, block, near):
-    x, y, z = true_rows(near_ref, column, near)
+def near_rows(listed, near_ref, signs, block, near):
+    x, y, z = true_rows(near_ref, signs, near)
     z = z + (SIDE / REACH) * offset_z(block, near)
     slots = lax.broadcasted_iota(jnp.int32, (1, SLOTS), 1).astype(F32)
     row = block * COLUMN + near
@@ -139,7 +145,7 @@
         near_1, embedding_ref, radial_ref, basis_ref, after_ref = refs[:5]
         fields = (near_1,)
     own_cols, near_ref, diagonal, picked, listed, message, features = refs[-7:]
-    column = place_of(part)
+    signs = signs_of(part)
     near_ref[0] = pick(fields)
 
     @pl.when(pl.program_id(0) == 0)
@@ -151,15 +157,15 @@
         else:
             message[...] = jnp.zeros_like(message)
 
-    mark_diagonal(column, diagonal)
-    mark_listed(own_ref, near_ref, column, picked, listed)
+    mark_diagonal(part, diagonal)
+    mark_listed(own_ref, near_ref, signs, picked, listed)
     for near in range(COLUMN):
         features[pl.ds(near * SLOTS, SLOTS), :] = species_features(
             near_ref, embedding_ref[...].astype(BF16), near
         )
     for block in range(COLUMN):
         for near in range(COLUMN):
-            rows = near_rows(listed, near_ref, column, block, near)
+            rows = near_rows(listed, near_ref, signs, block, near)
             for start in range(0, SLOTS, CHUNK):
                 left = left_over(rows, own_cols, diagonal, block, near, start)
                 middle = left - 0.5
@@ -273,7 +279,7 @@
 ):
     before_ref = None if group == 1 else refs[0]
     slope_ref, kind_ref, own_cols, diagonal, picked, listed, table = refs[-7:]
-    column = place_of(group)
+    signs = signs_of(group)
 
     @pl.when(pl.program_id(0) == 0)
     def _():
@@ -281,13 +287,13 @@
         picked[...] = jnp.zeros_like(picked)
         start_from(before_ref, kind_ref)
 
-    mark_diagonal(column, diagonal)
-    mark_listed(own_ref, near_ref, column, picked, listed)
+    mark_diagonal(group, diagonal)
+    mark_listed(own_ref, near_ref, signs, picked, listed)
     one_hots = [kind_rows(near_ref, near) for near in range(COLUMN)]
-    fill_table(table, one_hots, near_ref, column)
+    fill_table(table, one_hots, near_ref, signs)
     for block in range(COLUMN):
         for near in range(COLUMN):
-            rows = near_rows(listed, near_ref, column, block, near)
+            rows = near_rows(listed, near_ref, signs, block, near)
             for start in range(0, SLOTS, CHUNK):
                 left = left_over(rows, own_cols, diagonal, block, near, start)
                 middle = left - 0.5
@@ -318,12 +324,11 @@
     kind_ref[...] += sums.reshape(ORDERS, ATOMS, SLOTS)
 
 
-def true_rows(near_ref, column, near):
-    steps = ((column // 3 - 1).astype(F32), (column % 3 - 1).astype(F32), 0.0)
-    return [
-        (near_ref[0, near, axis : axis + 1, :] + SIDE * steps[axis]) * (1.0 / REACH)
-        for axis in range(3)
-    ]
+def true_rows(near_ref, signs, near):
+    steps = steps_to(near_ref, near, signs)
+    x = (near_ref[0, near, 0:1, :] + SIDE * steps[0]) * (1.0 / REACH)
+    y = (near_ref[0, near, 1:2, :] + SIDE * steps[1]) * (1.0 / REACH)
+    return x, y, near_ref[0, near, 2:3, :] * (1.0 / REACH)
 
 
 def kind_rows(near_ref, near):
@@ -331,11 +336,11 @@
     return jnp.where(near_ref[0, near, 3:4, :] == kinds, 1.0, 0.0)
 
 
-def fill_table(table, values, near_ref, column):
+def fill_table(table, values, near_ref, signs):
     for near in range(COLUMN):
         zero = jnp.zeros((KINDS, SLOTS), F32)
         pieces = [values[near] if part == near else zero for part in range(COLUMN)]
-        for row in true_rows(near_ref, column, near):
+        for row in true_rows(near_ref, signs, near):
             product = values[near] * row
             high = product.astype(BF16).astype(F32)
             pieces.extend((high, product - high))
@@ -349,7 +354,7 @@
 ):
     before_ref = None if group == 1 else refs[0]
     force_ref, own_cols, left_side, right_side = refs[-4:]
-    column = place_of(group)
+    signs = signs_of(group)
 
     @pl.when(pl.program_id(0) == 0)
     def _():
@@ -367,7 +372,7 @@
 
     right_side[:, 0:CHANNELS] = near_hidden_ref[0]
     right_side[:, CHANNELS : 2 * CHANNELS] = near_grad_ref[0]
-    near_places = [true_rows(near_ref, column, near) for near in range(COLUMN)]
+    near_places = [true_rows(near_ref, signs, near) for near in range(COLUMN)]
     for block in range(COLUMN):
         pair = dot(left_side[block], right_side[...], ((1,), (1,)))
         for start in range(0, SLOTS, CHUNK):
@@ -395,10 +400,10 @@
     def _():
         start_from(before_ref, near_kind_ref)
 
-    add_kinds(place_of(group), slope_ref, projected_ref, near_ref, near_kind_ref, table)
-
-
-def add_kinds(column, slope_ref, projected_ref, near_ref, near_kind, table):
+    add_kinds(signs_of(group), slope_ref, projected_ref, near_ref, near_kind_ref, table)
+
+
+def add_kinds(signs, slope_ref, projected_ref, near_ref, near_kind, table):
     projected = projected_ref[0].astype(F32)
     total = near_kind[...]
     for order in range(ORDERS):
@@ -406,7 +411,7 @@
             projected[order * KINDS : (order + 1) * KINDS, near * SLOTS : (near + 1) * SLOTS]
             for near in range(COLUMN)
         ]
-        fill_table(table.at[order], values, near_ref, column)
+        fill_table(table.at[order], values, near_ref, signs)
         total = total + dot(slope_ref[0, order], table[order], ((1,), (1,)))
     near_kind[...] = total
 
@@ -420,7 +425,7 @@
         spread_own(own_ref, own_cols)
         near_kind[...] = before_ref[...]
 
-    add_kinds(place_of(2), slope_ref, projected_ref, near_ref, near_kind, table)
+    add_kinds(signs_of(2), slope_ref, projected_ref, near_ref, near_kind, table)
 
     @pl.when(pl.program_id(0) == 2)
     def _():
@@ -470,7 +475,7 @@
 
 
 def prepare_kernel(
-    counts_ref, masses_ref, positions_ref, velocities_ref, forces_ref, noise_ref, species_ref,
+    parity_ref, counts_ref, masses_ref, positions_ref, velocities_ref, forces_ref, noise_ref, species_ref,
     pair_list_ref, embedding_ref, radial_one_ref, radial_two_ref, mix_one_ref, mix_two_ref,
     readout_ref, new_positions_ref, geometry_ref, mixed_ref, mass_ref, weights_ref,
 ):
@@ -512,20 +517,25 @@
         geometry_ref[block, 4:5, :] = jnp.full(
             (1, SLOTS), counts_ref[0, 0, block], jnp.int32
         ).astype(F32)
+        for axis in range(2):
+            geometry_ref[block, 6 + axis : 7 + axis, :] = jnp.full(
+                (1, SLOTS), 1 - 2 * parity_ref[axis], jnp.int32
+            ).astype(F32)
         geometry_ref[block, 5:6, 0:13] = pair_list_ref[block].astype(F32)
 
 
-def shift(cell, axis, step):
+def swap(cell, axis, first):
     count = lax.axis_size(axis)
-    return lax.ppermute(cell, axis, [((i + step) % count, i) for i in range(count)])
+    pairs = [((first + i) % count, (first + i + 1) % count) for i in range(0, count, 2)]
+    return lax.ppermute(cell, axis, pairs + [(right, left) for left, right in pairs])
 
 
 def own_row(cell):
-    return jnp.stack([shift(cell, "gy", -1), cell, shift(cell, "gy", 1)])
+    return jnp.stack([swap(cell, "gy", 0), cell, swap(cell, "gy", 1)])
 
 
 def outer_rows(row):
-    return shift(row, "gx", -1), shift(row, "gx", 1)
+    return swap(row, "gx", 0), swap(row, "gx", 1)
 
 
 SMEM = pl.BlockSpec(memory_space=pltpu.SMEM)
@@ -595,6 +605,7 @@
 ):
     vmem = pl.BlockSpec(memory_space=pltpu.VMEM)
     rows = (3 * COLUMN, 1, SLOTS)
+    parity = jnp.stack([lax.axis_index("gx") % 2, lax.axis_index("gy") % 2])
     new_positions, geometry, mixed_velocity, atom_mass, weights = pl.pallas_call(
         prepare_kernel,
         name="prepare",
@@ -605,9 +616,9 @@
             shape_of(COLUMN, 1, SLOTS),
             shape_of(WEIGHT_ROWS, CHANNELS),
         ),
-        in_specs=[SMEM, SMEM] + [vmem] * 12,
+        in_specs=[SMEM] * 3 + [vmem] * 12,
     )(
-        counts, masses, positions.reshape(rows), velocities.reshape(rows), forces.reshape(rows),
+        parity, counts, masses, positions.reshape(rows), velocities.reshape(rows), forces.reshape(rows),
         noise.reshape(rows), species.reshape(COLUMN, 1, SLOTS), pair_list.reshape(COLUMN, 1, 13),
         embedding, radial_one, radial_two, mix_one, mix_two, readout[None, :],
     )

time: 124 us -> 116 us (0.935)
  the two profiles are of different devices: /device:TPU:0 before, /device:TPU:1 now
where the time goes in v3:
time: 116 us; the launch traced here: 115 us
  Pallas kernels  76.3 us (66%)
  starting transfers between devices  30.3 us (26%)
  local copies, waits for them, and re-layouts  4.09 us (4%)
  waiting for transfers between devices  2.29 us (2%)
  other arithmetic  1.42 us (1%)
    ppermute x16, starting transfers between devices, swap(): lax.ppermute(cell, axis, pairs + [(right, left) for left, right in pairs])  30.3 us
    pallas_call x3, Pallas kernels, slope_of(): call(functools.partial(slope_kernel, group), f'slope_{group}', 3, (shape_...  22.3 us
    pallas_call x3, Pallas kernels, on_device(): call(functools.partial(pair_kernel, group), f'pair_{group}', 3, shape_of(...  12 us
    pallas_call x1, Pallas kernels, on_device(): call(functools.partial(basis_kernel, OUTER), 'basis_outer', 6, (shape_of(...  10.4 us
    pallas_call x2, Pallas kernels, on_device(): call(functools.partial(kind_kernel, group), f'last_{group}', 3, shape_of(...  5.37 us
    pallas_call x1, Pallas kernels, on_device(): call(first_kernel, 'first_outer', 6, shape_of(ORDERS * KINDS, ATOMS, kind...  5.35 us
    pallas_call x1, Pallas kernels, on_device(): call(functools.partial(basis_kernel, 1), 'basis_row', 3, (shape_of(3, *pa...  5.14 us
    pallas_call x1, Pallas kernels, on_device(): call(second_kernel, 'second_outer', 6, shape_of(*field, kind=BF16), [at_c...  5.12 us
  transfers between devices with their start and end apart: 16, of which 2 were waited for; matrix products, arithmetic and copies ran while one was open for 0% of the time, Pallas kernels for 43%

profile of v3, /device:TPU:1, one launch (start us, length us, event | category | flops | bytes accessed | tf_op | source)
XLA Modules:
  0.0 115.5 jit_solution(15757349781223410462)
XLA Ops:
  0.6 0.6 pad_add_fusion.parity_ref
  1.3 1.8 %prepare.1 = (f32[9,1,128]{2,1,0:T(1,128)}, f32[3,8,128]{2,1,0:T(8,128)}, f32[9,1,128]{2,1,0:T(1,128)}, f32[3,1,128]{2,1,0:T(1,128)}, f32[1152,128]{1,0:T(8,128)}) custom-call(s32[2]{0:T(128)} %pad_add_fusion.parity_ref, s32[1,1,3]{2,1,0:T(1,128)} %counts_ref.1, f32[6]{0:T(128)} %masses_ref.1, f32[9,1,128]{2,1,0:T(1,128)} %bitcast.42, ...), custom_call_target="tpu_custom_call" | custom-call | tf_op jit(solution)/shard_map/prepare/pallas_call | solution.py:609
  3.0 2.6 %collective-permute-start.1 = (f32[3,8,128]{2,1,0:T(8,128)}, f32[3,8,128]{2,1,0:T(8,128)S(1)}, u32[]{:S(2)}, u32[]{:S(2)}) collective-permute-start(f32[3,8,128]{2,1,0:T(8,128)} %get-tuple-element.28), channel_id=1, source_target_pairs={{1,2},{3,4},{5,6},{7,8},{9,10},{11,12},{13,14},{15,0},{2,1},{4,3},... | collective-permute-start | bytes 36872 | tf_op jit(solution)/shard_map/ppermute | solution.py:530
  5.6 2.3 %collective-permute-start = (f32[3,8,128]{2,1,0:T(8,128)}, f32[3,8,128]{2,1,0:T(8,128)S(1)}, u32[]{:S(2)}, u32[]{:S(2)}) collective-permute-start(f32[3,8,128]{2,1,0:T(8,128)} %get-tuple-element.28), channel_id=1, source_target_pairs={{0,1},{2,3},{4,5},{6,7},{8,9},{10,11},{12,13},{14,15},{1,0},{3,2},... | collective-permute-start | bytes 36872 | tf_op jit(solution)/shard_map/ppermute | solution.py:530
  7.9 1.0 collective-permute-done
  9.0 0.7 pad_maximum_fusion.3.own_ref.refs_0_.near_ref
  9.7 7.7 %collective-permute-start.2 = (f32[3,3,8,128]{3,2,1,0:T(8,128)S(1)}, f32[3,3,8,128]{3,2,1,0:T(8,128)S(1)}, u32[]{:S(2)}, u32[]{:S(2)}) collective-permute-start(f32[3,3,8,128]{3,2,1,0:T(8,128)S(1)} %pad_maximum_fusion.3.own_ref.refs_0_.near_ref), channel_id=1, source_target_pairs={{16,32},{48,64},{80,96},{112,128},{144,160},{176,192},{208,224},{2... | collective-permute-start | bytes 110600 | tf_op jit(solution)/shard_map/ppermute | solution.py:530
  17.4 1.1 copy-done
  18.5 5.1 %basis_row.1 = (bf16[3,8,384,384]{3,2,1,0:T(8,128)(2,1)S(1)}, f32[384,128]{1,0:T(8,128)S(1)}) custom-call(f32[3,3,8,128]{3,2,1,0:T(8,128)S(1)} %pad_maximum_fusion.3.own_ref.refs_0_.near_ref, f32[3,3,8,128]{3,2,1,0:T(8,128)S(1)} %pad_maximum_fusion.3.own_ref.refs_0_.near_ref, f32[1152,128]{1,0:T(8,128)S(1)} %copy-done, f32[1152,128]{1,0:T(8,128)S(1)} %copy-done), custom_call_target="tpu_custom_call" | custom-call | flops 905969664 | bytes 7077888 | tf_op jit(solution)/shard_map/basis_row/pallas_call | solution.py:646
  23.6 0.0 collective-permute-done.2.refs_1_.near_ref
  23.7 0.0 collective-permute-done.3.refs_0_.near_ref
  23.7 10.4 %basis_outer.1 = (bf16[6,8,384,384]{3,2,1,0:T(8,128)(2,1)S(1)}, bf16[384,128]{1,0:T(8,128)(2,1)S(1)}, f32[384,128]{1,0:T(8,128)S(1)}) custom-call(f32[3,3,8,128]{3,2,1,0:T(8,128)S(1)} %pad_maximum_fusion.3.own_ref.refs_0_.near_ref, f32[3,3,8,128]{3,2,1,0:T(8,128)S(1)} %collective-permute-done.3.refs_0_.near_ref, ...), custom_call_target="tpu_custom_call" | custom-call | flops 1811939328 | bytes 14155776 | tf_op jit(solution)/shard_map/basis_outer/pallas_call | solution.py:656
  34.0 0.1 collective-permute-start.5
  34.1 3.8 %collective-permute-start.4 = (bf16[384,128]{1,0:T(8,128)(2,1)S(1)}, bf16[384,128]{1,0:T(8,128)(2,1)S(1)}, u32[]{:S(2)}, u32[]{:S(2)}) collective-permute-start(bf16[384,128]{1,0:T(8,128)(2,1)S(1)} %get-tuple-element.32), channel_id=1, source_target_pairs={{0,1},{2,3},{4,5},{6,7},{8,9},{10,11},{12,13},{14,15},{1,0},{3,2},... | collective-permute-start | bytes 294920 | tf_op jit(solution)/shard_map/ppermute | solution.py:530
  37.9 7.5 %slope_1.1 = (bf16[3,8,384,384]{3,2,1,0:T(8,128)(2,1)S(1)}, f32[8,384,128]{2,1,0:T(8,128)S(1)}) custom-call(f32[3,3,8,128]{3,2,1,0:T(8,128)S(1)} %pad_maximum_fusion.3.own_ref.refs_0_.near_ref, f32[3,3,8,128]{3,2,1,0:T(8,128)S(1)} %pad_maximum_fusion.3.own_ref.refs_0_.near_ref), custom_call_target="tpu_custom_call" | custom-call | flops 905969664 | bytes 7077888 | tf_op jit(solution)/shard_map/slope_1/pallas_call | solution.py:669
  45.4 0.0 collective-permute-done.5
  45.4 0.0 collective-permute-done.4
  45.4 1.5 %collective-permute-start.6 = (bf16[3,384,128]{2,1,0:T(8,128)(2,1)S(1)}, bf16[3,384,128]{2,1,0:T(8,128)(2,1)S(1)}, u32[]{:S(2)}, u32[]{:S(2)}) collective-permute-start(bf16[3,384,128]{2,1,0:T(8,128)(2,1)S(1)} %pad_maximum_fusion.field_ref.near_hidden_ref.hidden_ref), channel_id=1, source_target_pairs={{0,16},{32,48},{64,80},{96,112},{128,144},{160,176},{192,208},{224... | collective-permute-start | bytes 884744 | tf_op jit(solution)/shard_map/ppermute | solution.py:530
  47.0 0.9 collective-permute-start.7
  47.9 2.4 %second_row.1.before_ref = f32[384,128]{1,0:T(8,128)S(1)} custom-call(bf16[3,8,384,384]{3,2,1,0:T(8,128)(2,1)S(1)} %get-tuple-element.30.basis_ref, bf16[3,384,128]{2,1,0:T(8,128)(2,1)S(1)} %pad_maximum_fusion.field_ref.near_hidden_ref.hidden_ref, f32[1152,128]{1,0:T(8,128)S(1)} %copy-done.1), custom_call_target="tpu_custom_call" | custom-call | flops 905969664 | bytes 7077888 | tf_op jit(solution)/shard_map/second_row/pallas_call | solution.py:681
  50.3 7.4 %slope_0.1 = (bf16[3,8,384,384]{3,2,1,0:T(8,128)(2,1)S(1)}, f32[8,384,128]{2,1,0:T(8,128)S(1)}) custom-call(f32[3,3,8,128]{3,2,1,0:T(8,128)S(1)} %pad_maximum_fusion.3.own_ref.refs_0_.near_ref, f32[3,3,8,128]{3,2,1,0:T(8,128)S(1)} %collective-permute-done.3.refs_0_.near_ref, f32[8,384,128]{2,1,0:T(8,128)S(1)} %get-tuple-element.35.refs_0_), custom_call_target="tpu_custom_call" | custom-call | flops 905969664 | bytes 7077888 | tf_op jit(solution)/shard_map/slope_0/pallas_call | solution.py:669
  57.7 0.0 collective-permute-done.6.hidden_0.near_hidden_ref
  57.7 1.2 %collective-permute-done.7.hidden_2.near_hidden_ref = bf16[3,384,128]{2,1,0:T(8,128)(2,1)S(1)} collective-permute-done((bf16[3,384,128]{2,1,0:T(8,128)(2,1)S(1)}, bf16[3,384,128]{2,1,0:T(8,128)(2,1)S(1)}, u32[]{:S(2)}, u32[]{:S(2)}) %collective-permute-start.7) | collective-permute-done | bytes 294944 | tf_op jit(solution)/shard_map/ppermute | solution.py:530
  58.9 5.1 %second_outer.1 = bf16[384,128]{1,0:T(8,128)(2,1)S(1)} custom-call(bf16[6,8,384,384]{3,2,1,0:T(8,128)(2,1)S(1)} %get-tuple-element.39.basis_ref, bf16[3,384,128]{2,1,0:T(8,128)(2,1)S(1)} %collective-permute-done.6.hidden_0.near_hidden_ref, bf16[3,384,128]{2,1,0:T(8,128)(2,1)S(1)} %collective-permute-done.7.hidden_2.near_hidden_ref, ...), custom_call_target="tpu_custom_call" | custom-call | flops 1811939328 | bytes 14155776 | tf_op jit(solution)/shard_map/second_outer/pallas_call | solution.py:699
  64.0 0.3 collective-permute-start.9
  64.4 1.2 %collective-permute-start.8 = (bf16[384,128]{1,0:T(8,128)(2,1)S(1)}, bf16[384,128]{1,0:T(8,128)(2,1)S(1)}, u32[]{:S(2)}, u32[]{:S(2)}) collective-permute-start(bf16[384,128]{1,0:T(8,128)(2,1)S(1)} %second_outer.1), channel_id=1, source_target_pairs={{0,1},{2,3},{4,5},{6,7},{8,9},{10,11},{12,13},{14,15},{1,0},{3,2},... | collective-permute-start | bytes 294920 | tf_op jit(solution)/shard_map/ppermute | solution.py:530
  65.5 7.5 %slope_2.1 = (bf16[3,8,384,384]{3,2,1,0:T(8,128)(2,1)S(1)}, f32[8,384,128]{2,1,0:T(8,128)S(1)}) custom-call(f32[3,3,8,128]{3,2,1,0:T(8,128)S(1)} %pad_maximum_fusion.3.own_ref.refs_0_.near_ref, f32[3,3,8,128]{3,2,1,0:T(8,128)S(1)} %collective-permute-done.2.refs_1_.near_ref, f32[8,384,128]{2,1,0:T(8,128)S(1)} %get-tuple-element.37.refs_0_), custom_call_target="tpu_custom_call" | custom-call | flops 905969664 | bytes 7077888 | tf_op jit(solution)/shard_map/slope_2/pallas_call | solution.py:669
  73.0 0.0 collective-permute-done.8
  73.1 0.1 collective-permute-start.10
  73.2 4.2 %collective-permute-start.11 = (bf16[3,384,128]{2,1,0:T(8,128)(2,1)S(1)}, bf16[3,384,128]{2,1,0:T(8,128)(2,1)S(1)}, u32[]{:S(2)}, u32[]{:S(2)}) collective-permute-start(bf16[3,384,128]{2,1,0:T(8,128)(2,1)S(1)} %pad_maximum_fusion.1.field_ref.near_grad_ref.grad_ref), channel_id=1, source_target_pairs={{16,32},{48,64},{80,96},{112,128},{144,160},{176,192},{208,224},{2... | collective-permute-start | bytes 884744 | tf_op jit(solution)/shard_map/ppermute | solution.py:530
  77.4 3.0 %copy-done.3 = bf16[3,8,384,384]{3,2,1,0:T(8,128)(2,1)S(1)} copy-done((bf16[3,8,384,384]{3,2,1,0:T(8,128)(2,1)S(1)}, bf16[3,8,384,384]{3,2,1,0:T(8,128)(2,1)}, u32[]{:S(2)}) %copy-start.3) | copy-done | bytes 7077912
  80.4 2.4 %first_row.1.before_ref = f32[384,128]{1,0:T(8,128)S(1)} custom-call(bf16[3,8,384,384]{3,2,1,0:T(8,128)(2,1)S(1)} %copy-done.3, bf16[3,384,128]{2,1,0:T(8,128)(2,1)S(1)} %pad_maximum_fusion.1.field_ref.near_grad_ref.grad_ref, f32[1152,128]{1,0:T(8,128)S(1)} %copy-done.1), custom_call_target="tpu_custom_call" | custom-call | flops 905969664 | bytes 7077888 | tf_op jit(solution)/shard_map/first_row/pallas_call | solution.py:681
  82.8 4.0 %pair_1.1.refs_0_ = f32[3,384,128]{2,1,0:T(8,128)S(1)} custom-call(f32[3,3,8,128]{3,2,1,0:T(8,128)S(1)} %pad_maximum_fusion.3.own_ref.refs_0_.near_ref, f32[3,3,8,128]{3,2,1,0:T(8,128)S(1)} %pad_maximum_fusion.3.own_ref.refs_0_.near_ref, bf16[3,8,384,384]{3,2,1,0:T(8,128)(2,1)S(1)} %get-tuple-element.45.slope_ref, ...), custom_call_target="tpu_custom_call" | custom-call | flops 1811939328 | bytes 7077888 | tf_op jit(solution)/shard_map/pair_1/pallas_call | solution.py:739
  86.8 0.0 collective-permute-done.10.grad_0.near_grad_ref
  86.9 5.3 %first_outer.1 = bf16[64,384]{1,0:T(8,128)(2,1)S(1)} custom-call(bf16[6,8,384,384]{3,2,1,0:T(8,128)(2,1)S(1)} %get-tuple-element.39.basis_ref, bf16[3,384,128]{2,1,0:T(8,128)(2,1)S(1)} %collective-permute-done.10.grad_0.near_grad_ref, bf16[3,384,128]{2,1,0:T(8,128)(2,1)S(1)} %collective-permute-done.11.grad_2.near_grad_ref, f32[1152,128]{1,0:T(8,128)S(1)} %copy-done.1, ...), custom_call_target="tpu_custom_call" | custom-call | flops 1811939328 | bytes 14155776 | tf_op jit(solution)/shard_map/first_outer/pallas_call | solution.py:718
  92.2 0.3 collective-permute-start.13
  92.5 1.6 %collective-permute-start.12 = (bf16[64,384]{1,0:T(8,128)(2,1)S(1)}, bf16[64,384]{1,0:T(8,128)(2,1)S(1)}, u32[]{:S(2)}, u32[]{:S(2)}) collective-permute-start(bf16[64,384]{1,0:T(8,128)(2,1)S(1)} %first_outer.1), channel_id=1, source_target_pairs={{0,1},{2,3},{4,5},{6,7},{8,9},{10,11},{12,13},{14,15},{1,0},{3,2},... | collective-permute-start | bytes 147464 | tf_op jit(solution)/shard_map/ppermute | solution.py:530
  94.2 4.0 %pair_0.1.refs_0_ = f32[3,384,128]{2,1,0:T(8,128)S(1)} custom-call(f32[3,3,8,128]{3,2,1,0:T(8,128)S(1)} %pad_maximum_fusion.3.own_ref.refs_0_.near_ref, f32[3,3,8,128]{3,2,1,0:T(8,128)S(1)} %collective-permute-done.3.refs_0_.near_ref, bf16[3,8,384,384]{3,2,1,0:T(8,128)(2,1)S(1)} %get-tuple-element.44.slope_ref, ...), custom_call_target="tpu_custom_call" | custom-call | flops 1811939328 | bytes 7077888 | tf_op jit(solution)/shard_map/pair_0/pallas_call | solution.py:739
  98.2 0.0 collective-permute-done.13
  98.2 0.1 collective-permute-start.15
  98.3 4.0 %pair_2.1.force_ref = f32[3,384,128]{2,1,0:T(8,128)S(1)} custom-call(f32[3,3,8,128]{3,2,1,0:T(8,128)S(1)} %pad_maximum_fusion.3.own_ref.refs_0_.near_ref, f32[3,3,8,128]{3,2,1,0:T(8,128)S(1)} %collective-permute-done.2.refs_1_.near_ref, bf16[3,8,384,384]{3,2,1,0:T(8,128)(2,1)S(1)} %get-tuple-element.38.slope_ref, ...), custom_call_target="tpu_custom_call" | custom-call | flops 1811939328 | bytes 7077888 | tf_op jit(solution)/shard_map/pair_2/pallas_call | solution.py:739
  102.3 0.0 copy-start.4
  102.3 0.0 copy-start.5
  102.4 3.6 %collective-permute-start.14 = (bf16[3,64,384]{2,1,0:T(8,128)(2,1)S(1)}, bf16[3,64,384]{2,1,0:T(8,128)(2,1)S(1)}, u32[]{:S(2)}, u32[]{:S(2)}) collective-permute-start(bf16[3,64,384]{2,1,0:T(8,128)(2,1)S(1)} %pad_maximum_fusion.2.projected_ref.own_projected_ref), channel_id=1, source_target_pairs={{16,32},{48,64},{80,96},{112,128},{144,160},{176,192},{208,224},{2... | collective-permute-start | bytes 442376 | tf_op jit(solution)/shard_map/ppermute | solution.py:530
  105.9 2.7 %last_1.1.refs_0_ = f32[384,128]{1,0:T(8,128)S(1)} custom-call(bf16[3,8,384,384]{3,2,1,0:T(8,128)(2,1)S(1)} %get-tuple-element.45.slope_ref, bf16[3,64,384]{2,1,0:T(8,128)(2,1)S(1)} %pad_maximum_fusion.2.projected_ref.own_projected_ref, f32[3,3,8,128]{3,2,1,0:T(8,128)S(1)} %pad_maximum_fusion.3.own_ref.refs_0_.near_ref), custom_call_target="tpu_custom_call" | custom-call | flops 905969664 | bytes 7077888 | tf_op jit(solution)/shard_map/last_1/pallas_call | solution.py:770
  108.6 0.0 collective-permute-done.15.projected_ref
  108.6 2.7 %last_0.1.before_ref = f32[384,128]{1,0:T(8,128)S(1)} custom-call(bf16[3,8,384,384]{3,2,1,0:T(8,128)(2,1)S(1)} %get-tuple-element.44.slope_ref, bf16[3,64,384]{2,1,0:T(8,128)(2,1)S(1)} %collective-permute-done.15.projected_ref, f32[3,3,8,128]{3,2,1,0:T(8,128)S(1)} %collective-permute-done.3.refs_0_.near_ref, f32[384,128]{1,0:T(8,128)S(1)} %last_1.1.refs_0_), custom_call_target="tpu_custom_call" | custom-call | flops 905969664 | bytes 7077888 | tf_op jit(solution)/shard_map/last_0/pallas_call | solution.py:770
  111.3 4.1 %last_2.1 = (f32[9,1,128]{2,1,0:T(1,128)}, f32[9,1,128]{2,1,0:T(1,128)}) custom-call(bf16[3,8,384,384]{3,2,1,0:T(8,128)(2,1)S(1)} %get-tuple-element.38.slope_ref, bf16[3,64,384]{2,1,0:T(8,128)(2,1)S(1)} %collective-permute-done.14.projected_ref, f32[3,3,8,128]{3,2,1,0:T(8,128)S(1)} %collective-permute-done.2.refs_1_.near_ref, ...), custom_call_target="tpu_custom_call" | custom-call | flops 905969664 | bytes 7077888 | tf_op jit(solution)/shard_map/last_2/pallas_call | solution.py:781
  (17 shorter events, 0.1 us)
Async XLA Ops:
  3.0 4.9 %collective-permute-start.1 = (f32[3,8,128]{2,1,0:T(8,128)}, f32[3,8,128]{2,1,0:T(8,128)S(1)}, u32[]{:S(2)}, u32[]{:S(2)}) collective-permute-start(f32[3,8,128]{2,1,0:T(8,128)} %get-tuple-element.28), channel_id=1, source_target_pairs={{1,2},{3,4},{5,6},{7,8},{9,10},{11,12},{13,14},{15,0},{2,1},{4,3},... | collective-permute-start | bytes 36872 | tf_op jit(solution)/shard_map/ppermute | solution.py:530
  5.6 3.3 %collective-permute-start = (f32[3,8,128]{2,1,0:T(8,128)}, f32[3,8,128]{2,1,0:T(8,128)S(1)}, u32[]{:S(2)}, u32[]{:S(2)}) collective-permute-start(f32[3,8,128]{2,1,0:T(8,128)} %get-tuple-element.28), channel_id=1, source_target_pairs={{0,1},{2,3},{4,5},{6,7},{8,9},{10,11},{12,13},{14,15},{1,0},{3,2},... | collective-permute-start | bytes 36872 | tf_op jit(solution)/shard_map/ppermute | solution.py:530
  9.7 14.0 %collective-permute-start.2 = (f32[3,3,8,128]{3,2,1,0:T(8,128)S(1)}, f32[3,3,8,128]{3,2,1,0:T(8,128)S(1)}, u32[]{:S(2)}, u32[]{:S(2)}) collective-permute-start(f32[3,3,8,128]{3,2,1,0:T(8,128)S(1)} %pad_maximum_fusion.3.own_ref.refs_0_.near_ref), channel_id=1, source_target_pairs={{16,32},{48,64},{80,96},{112,128},{144,160},{176,192},{208,224},{2... | collective-permute-start | bytes 110600 | tf_op jit(solution)/shard_map/ppermute | solution.py:530
  17.4 6.2 %collective-permute-start.3 = (f32[3,3,8,128]{3,2,1,0:T(8,128)S(1)}, f32[3,3,8,128]{3,2,1,0:T(8,128)S(1)}, u32[]{:S(2)}, u32[]{:S(2)}) collective-permute-start(f32[3,3,8,128]{3,2,1,0:T(8,128)S(1)} %pad_maximum_fusion.3.own_ref.refs_0_.near_ref), channel_id=1, source_target_pairs={{0,16},{32,48},{64,80},{96,112},{128,144},{160,176},{192,208},{224... | collective-permute-start | bytes 110600 | tf_op jit(solution)/shard_map/ppermute | solution.py:530
  17.4 1.1 copy-start
  18.5 29.4 %copy-start.1 = (f32[1152,128]{1,0:T(8,128)S(1)}, f32[1152,128]{1,0:T(8,128)}, u32[]{:S(2)}) copy-start(f32[1152,128]{1,0:T(8,128)} %get-tuple-element.29.refs_1_.refs_2_.refs_3_.refs_4_.radial_ref.mix_ref.upstream_ref.table_ref) | copy-start | bytes 1769476
  23.6 24.2 %copy-start.2 = (bf16[3,8,384,384]{3,2,1,0:T(8,128)(2,1)}, bf16[3,8,384,384]{3,2,1,0:T(8,128)(2,1)S(1)}, u32[]{:S(2)}) copy-start(bf16[3,8,384,384]{3,2,1,0:T(8,128)(2,1)S(1)} %get-tuple-element.30.basis_ref) | copy-start | bytes 21233668
  34.0 11.4 %collective-permute-start.5 = (bf16[384,128]{1,0:T(8,128)(2,1)S(1)}, bf16[384,128]{1,0:T(8,128)(2,1)S(1)}, u32[]{:S(2)}, u32[]{:S(2)}) collective-permute-start(bf16[384,128]{1,0:T(8,128)(2,1)S(1)} %get-tuple-element.32), channel_id=1, source_target_pairs={{1,2},{3,4},{5,6},{7,8},{9,10},{11,12},{13,14},{15,0},{2,1},{4,3},... | collective-permute-start | bytes 294920 | tf_op jit(solution)/shard_map/ppermute | solution.py:530
  34.1 11.3 %collective-permute-start.4 = (bf16[384,128]{1,0:T(8,128)(2,1)S(1)}, bf16[384,128]{1,0:T(8,128)(2,1)S(1)}, u32[]{:S(2)}, u32[]{:S(2)}) collective-permute-start(bf16[384,128]{1,0:T(8,128)(2,1)S(1)} %get-tuple-element.32), channel_id=1, source_target_pairs={{0,1},{2,3},{4,5},{6,7},{8,9},{10,11},{12,13},{14,15},{1,0},{3,2},... | collective-permute-start | bytes 294920 | tf_op jit(solution)/shard_map/ppermute | solution.py:530
  45.4 12.2 %collective-permute-start.6 = (bf16[3,384,128]{2,1,0:T(8,128)(2,1)S(1)}, bf16[3,384,128]{2,1,0:T(8,128)(2,1)S(1)}, u32[]{:S(2)}, u32[]{:S(2)}) collective-permute-start(bf16[3,384,128]{2,1,0:T(8,128)(2,1)S(1)} %pad_maximum_fusion.field_ref.near_hidden_ref.hidden_ref), channel_id=1, source_target_pairs={{0,16},{32,48},{64,80},{96,112},{128,144},{160,176},{192,208},{224... | collective-permute-start | bytes 884744 | tf_op jit(solution)/shard_map/ppermute | solution.py:530
  47.0 11.9 %collective-permute-start.7 = (bf16[3,384,128]{2,1,0:T(8,128)(2,1)S(1)}, bf16[3,384,128]{2,1,0:T(8,128)(2,1)S(1)}, u32[]{:S(2)}, u32[]{:S(2)}) collective-permute-start(bf16[3,384,128]{2,1,0:T(8,128)(2,1)S(1)} %pad_maximum_fusion.field_ref.near_hidden_ref.hidden_ref), channel_id=1, source_target_pairs={{16,32},{48,64},{80,96},{112,128},{144,160},{176,192},{208,224},{2... | collective-permute-start | bytes 884744 | tf_op jit(solution)/shard_map/ppermute | solution.py:530
  64.0 9.0 %collective-permute-start.9 = (bf16[384,128]{1,0:T(8,128)(2,1)S(1)}, bf16[384,128]{1,0:T(8,128)(2,1)S(1)}, u32[]{:S(2)}, u32[]{:S(2)}) collective-permute-start(bf16[384,128]{1,0:T(8,128)(2,1)S(1)} %second_outer.1), channel_id=1, source_target_pairs={{1,2},{3,4},{5,6},{7,8},{9,10},{11,12},{13,14},{15,0},{2,1},{4,3},... | collective-permute-start | bytes 294920 | tf_op jit(solution)/shard_map/ppermute | solution.py:530
  64.4 8.7 %collective-permute-start.8 = (bf16[384,128]{1,0:T(8,128)(2,1)S(1)}, bf16[384,128]{1,0:T(8,128)(2,1)S(1)}, u32[]{:S(2)}, u32[]{:S(2)}) collective-permute-start(bf16[384,128]{1,0:T(8,128)(2,1)S(1)} %second_outer.1), channel_id=1, source_target_pairs={{0,1},{2,3},{4,5},{6,7},{8,9},{10,11},{12,13},{14,15},{1,0},{3,2},... | collective-permute-start | bytes 294920 | tf_op jit(solution)/shard_map/ppermute | solution.py:530
  73.1 13.8 %collective-permute-start.10 = (bf16[3,384,128]{2,1,0:T(8,128)(2,1)S(1)}, bf16[3,384,128]{2,1,0:T(8,128)(2,1)S(1)}, u32[]{:S(2)}, u32[]{:S(2)}) collective-permute-start(bf16[3,384,128]{2,1,0:T(8,128)(2,1)S(1)} %pad_maximum_fusion.1.field_ref.near_grad_ref.grad_ref), channel_id=1, source_target_pairs={{0,16},{32,48},{64,80},{96,112},{128,144},{160,176},{192,208},{224... | collective-permute-start | bytes 884744 | tf_op jit(solution)/shard_map/ppermute | solution.py:530
  73.2 13.7 %collective-permute-start.11 = (bf16[3,384,128]{2,1,0:T(8,128)(2,1)S(1)}, bf16[3,384,128]{2,1,0:T(8,128)(2,1)S(1)}, u32[]{:S(2)}, u32[]{:S(2)}) collective-permute-start(bf16[3,384,128]{2,1,0:T(8,128)(2,1)S(1)} %pad_maximum_fusion.1.field_ref.near_grad_ref.grad_ref), channel_id=1, source_target_pairs={{16,32},{48,64},{80,96},{112,128},{144,160},{176,192},{208,224},{2... | collective-permute-start | bytes 884744 | tf_op jit(solution)/shard_map/ppermute | solution.py:530
  77.4 3.0 %copy-start.3 = (bf16[3,8,384,384]{3,2,1,0:T(8,128)(2,1)S(1)}, bf16[3,8,384,384]{3,2,1,0:T(8,128)(2,1)}, u32[]{:S(2)}) copy-start(bf16[3,8,384,384]{3,2,1,0:T(8,128)(2,1)} %copy-done.2) | copy-start | bytes 21233668
  92.2 5.9 %collective-permute-start.13 = (bf16[64,384]{1,0:T(8,128)(2,1)S(1)}, bf16[64,384]{1,0:T(8,128)(2,1)S(1)}, u32[]{:S(2)}, u32[]{:S(2)}) collective-permute-start(bf16[64,384]{1,0:T(8,128)(2,1)S(1)} %first_outer.1), channel_id=1, source_target_pairs={{1,2},{3,4},{5,6},{7,8},{9,10},{11,12},{13,14},{15,0},{2,1},{4,3},... | collective-permute-start | bytes 147464 | tf_op jit(solution)/shard_map/ppermute | solution.py:530
  92.5 5.6 %collective-permute-start.12 = (bf16[64,384]{1,0:T(8,128)(2,1)S(1)}, bf16[64,384]{1,0:T(8,128)(2,1)S(1)}, u32[]{:S(2)}, u32[]{:S(2)}) collective-permute-start(bf16[64,384]{1,0:T(8,128)(2,1)S(1)} %first_outer.1), channel_id=1, source_target_pairs={{0,1},{2,3},{4,5},{6,7},{8,9},{10,11},{12,13},{14,15},{1,0},{3,2},... | collective-permute-start | bytes 147464 | tf_op jit(solution)/shard_map/ppermute | solution.py:530
  98.2 10.4 %collective-permute-start.15 = (bf16[3,64,384]{2,1,0:T(8,128)(2,1)S(1)}, bf16[3,64,384]{2,1,0:T(8,128)(2,1)S(1)}, u32[]{:S(2)}, u32[]{:S(2)}) collective-permute-start(bf16[3,64,384]{2,1,0:T(8,128)(2,1)S(1)} %pad_maximum_fusion.2.projected_ref.own_projected_ref), channel_id=1, source_target_pairs={{0,16},{32,48},{64,80},{96,112},{128,144},{160,176},{192,208},{224... | collective-permute-start | bytes 442376 | tf_op jit(solution)/shard_map/ppermute | solution.py:530
  102.3 9.0 %copy-start.4 = (f32[9,1,128]{2,1,0:T(1,128)S(1)}, f32[9,1,128]{2,1,0:T(1,128)}, u32[]{:S(2)}) copy-start(f32[9,1,128]{2,1,0:T(1,128)} %get-tuple-element.47.mixed_ref) | copy-start | bytes 13828
  102.3 9.0 %copy-start.5 = (f32[3,1,128]{2,1,0:T(1,128)S(1)}, f32[3,1,128]{2,1,0:T(1,128)}, u32[]{:S(2)}) copy-start(f32[3,1,128]{2,1,0:T(1,128)} %get-tuple-element.48.mass_ref) | copy-start | bytes 4612
  102.4 8.9 %collective-permute-start.14 = (bf16[3,64,384]{2,1,0:T(8,128)(2,1)S(1)}, bf16[3,64,384]{2,1,0:T(8,128)(2,1)S(1)}, u32[]{:S(2)}, u32[]{:S(2)}) collective-permute-start(bf16[3,64,384]{2,1,0:T(8,128)(2,1)S(1)} %pad_maximum_fusion.2.projected_ref.own_projected_ref), channel_id=1, source_target_pairs={{16,32},{48,64},{80,96},{112,128},{144,160},{176,192},{208,224},{2... | collective-permute-start | bytes 442376 | tf_op jit(solution)/shard_map/ppermute | solution.py:530

commit v4 on v3

--- a/solution.py
+++ b/solution.py
@@ -23,7 +23,7 @@
 PARTS = 9
 CHUNK = 32
 OUTER = -1
-LIMIT = 12 * 2**20
+LIMIT = 8 * 2**20
 
 F32 = jnp.float32
 BF16 = jnp.bfloat16
@@ -83,9 +83,10 @@
 
 def signs_of(part):
     step = pl.program_id(0)
+    along_x = (1 - step % 3).astype(F32)
     if part == OUTER:
-        return (1 - 2 * (step // 3)).astype(F32), (1 - step % 3).astype(F32)
-    return float(1 - part), (1 - step % 3).astype(F32)
+        return along_x, (1 - 2 * (step // 3)).astype(F32)
+    return along_x, float(1 - part)
 
 
 def steps_to(near_ref, near, signs):
@@ -217,54 +218,55 @@
     message[...] = total
 
 
-def gather_kernel(basis_ref, field_ref, radial_ref, after_ref, message):
-    @pl.when(pl.program_id(0) == 0)
-    def _():
-        message[...] = jnp.zeros_like(message)
-
-    gathered = dot(basis_ref[0].reshape(ORDERS * ATOMS, ATOMS), field_ref[0])
-    add_orders(gathered, radial_ref, message)
-
-    @pl.when(pl.program_id(0) == 2)
-    def _():
-        after_ref[...] = message[...]
+def gather_columns(basis_ref, first, field_ref, radial_ref, message):
+    def add(column, carry):
+        gathered = dot(
+            basis_ref[first + column].reshape(ORDERS * ATOMS, ATOMS), field_ref[column]
+        )
+        add_orders(gathered, radial_ref, message)
+        return carry
+
+    lax.fori_loop(0, 3, add, 0)
+
+
+def gather_kernel(basis_ref, field_ref, weights_ref, after_ref):
+    after_ref[...] = jnp.zeros_like(after_ref)
+    radial_ref = rows_of(weights_ref, RADIAL_TWO, ORDERS)
+    gather_columns(basis_ref, 0, field_ref, radial_ref, after_ref)
 
 
 def gather_outer(basis_ref, fields, radial_ref, before_ref, message):
-    @pl.when(pl.program_id(0) == 0)
-    def _():
-        message[...] = before_ref[...]
-
-    gathered = dot(basis_ref[0].reshape(ORDERS * ATOMS, ATOMS), pick(fields))
-    add_orders(gathered, radial_ref, message)
-
-
-def second_kernel(
-    basis_ref, hidden_0, hidden_2, radial_ref, mix_ref, upstream_ref, before_ref, grad_ref, message
+    message[...] = before_ref[...]
+    for group, field_ref in enumerate(fields):
+        gather_columns(basis_ref, 3 * group, field_ref, radial_ref, message)
+
+
+def rows_of(weights_ref, first, rows):
+    return weights_ref.at[first : first + rows, :]
+
+
+def second_kernel(basis_ref, hidden_0, hidden_2, weights_ref, before_ref, grad_ref, message):
+    radial_ref = rows_of(weights_ref, RADIAL_TWO, ORDERS)
+    mix_ref = rows_of(weights_ref, MIX_TWO, CHANNELS)
+    upstream_ref = rows_of(weights_ref, UPSTREAM, ATOMS)
+    gather_outer(basis_ref, (hidden_0, hidden_2), radial_ref, before_ref, message)
+    gate = dot(message[...].astype(BF16), mix_ref[...].astype(BF16))
+    second = (upstream_ref[...] * silu_slope(gate)).astype(BF16)
+    grad_ref[...] = dot(second, mix_ref[...].astype(BF16), ((1,), (1,))).astype(BF16)
+
+
+def first_kernel(
+    basis_ref, grad_0, grad_2, weights_ref, gate_ref, before_ref, projected_ref, message
 ):
-    gather_outer(basis_ref, (hidden_0, hidden_2), radial_ref, before_ref, message)
-
-    @pl.when(pl.program_id(0) == 5)
-    def _():
-        gate = dot(message[...].astype(BF16), mix_ref[...].astype(BF16))
-        second = (upstream_ref[...] * silu_slope(gate)).astype(BF16)
-        grad_ref[...] = dot(second, mix_ref[...].astype(BF16), ((1,), (1,))).astype(BF16)
-
-
-def first_kernel(
-    basis_ref, grad_0, grad_2, radial_ref, mix_ref, upstream_ref, gate_ref, table_ref, before_ref,
-    projected_ref, message,
-):
+    radial_ref = rows_of(weights_ref, RADIAL_TWO, ORDERS)
+    mix_ref = rows_of(weights_ref, MIX_ONE, CHANNELS)
+    upstream_ref = rows_of(weights_ref, UPSTREAM, ATOMS)
+    table_ref = rows_of(weights_ref, TABLE, ORDERS * KINDS)
     gather_outer(basis_ref, (grad_0, grad_2), radial_ref, before_ref, message)
-
-    @pl.when(pl.program_id(0) == 5)
-    def _():
-        hidden_grad = upstream_ref[...] + message[...]
-        first = (hidden_grad * silu_slope(gate_ref[...])).astype(BF16)
-        message_grad = dot(first, mix_ref[...].astype(BF16), ((1,), (1,)))
-        projected_ref[...] = dot(
-            table_ref[...], message_grad, ((1,), (1,)), HIGHEST
-        ).astype(BF16)
+    hidden_grad = upstream_ref[...] + message[...]
+    first = (hidden_grad * silu_slope(gate_ref[...])).astype(BF16)
+    message_grad = dot(first, mix_ref[...].astype(BF16), ((1,), (1,)))
+    projected_ref[...] = dot(table_ref[...], message_grad, ((1,), (1,)), HIGHEST).astype(BF16)
 
 
 def start_from(before_ref, total_ref):
@@ -301,25 +303,18 @@
                 cosine = middle * horner(ODD, square)
                 sine = horner(EVEN, square)
                 twice = cosine + cosine
-                last_a = -2.0 * left
-                now_a = last_a * cosine
-                now_b = (left * left) * (sine * -math.pi)
-                last_b = None
-                span = (
-                    pl.ds(block * SLOTS + start, CHUNK),
-                    pl.ds(near * SLOTS, SLOTS),
-                )
-                slope_ref[0, 0, span[0], span[1]] = last_a.astype(BF16)
-                slope_ref[0, 1, span[0], span[1]] = (now_a + now_b).astype(BF16)
+                last = -2.0 * left
+                last_g = (left * left) * (sine * (-2.0 * math.pi))
+                now = last * cosine + 0.5 * last_g
+                now_g = last_g * cosine
+                span = (pl.ds(block * SLOTS + start, CHUNK), pl.ds(near * SLOTS, SLOTS))
+                slope_ref[0, 0, span[0], span[1]] = last.astype(BF16)
+                slope_ref[0, 1, span[0], span[1]] = now.astype(BF16)
                 for order in range(2, ORDERS):
-                    last_a, now_a = now_a, twice * now_a - last_a
-                    if last_b is None:
-                        last_b, now_b = now_b, twice * now_b
-                    else:
-                        last_b, now_b = now_b, twice * now_b - last_b
-                    slope_ref[0, order, span[0], span[1]] = (
-                        now_a + float(order) * now_b
-                    ).astype(BF16)
+                    last, now = now, twice * now - last + now_g
+                    if order < ORDERS - 1:
+                        last_g, now_g = now_g, twice * now_g - last_g
+                    slope_ref[0, order, span[0], span[1]] = now.astype(BF16)
     sums = dot(slope_ref[0].reshape(ORDERS * ATOMS, ATOMS), table[...], ((1,), (1,)))
     kind_ref[...] += sums.reshape(ORDERS, ATOMS, SLOTS)
 
@@ -531,11 +526,11 @@
 
 
 def own_row(cell):
-    return jnp.stack([swap(cell, "gy", 0), cell, swap(cell, "gy", 1)])
+    return jnp.stack([swap(cell, "gx", 0), cell, swap(cell, "gx", 1)])
 
 
 def outer_rows(row):
-    return swap(row, "gx", 0), swap(row, "gx", 1)
+    return swap(row, "gy", 0), swap(row, "gy", 1)
 
 
 SMEM = pl.BlockSpec(memory_space=pltpu.SMEM)
@@ -677,17 +672,22 @@
             PAIR_FLOPS,
         )(geometry_row, geometries[group], *before)
 
+    def single(kernel, name, out_shape, scratch, *operands):
+        return pl.pallas_call(
+            kernel,
+            name=name,
+            out_shape=out_shape,
+            in_specs=[vmem] * len(operands),
+            out_specs=vmem,
+            scratch_shapes=scratch,
+            cost_estimate=pl.CostEstimate(
+                flops=6 * PAIR_FLOPS, bytes_accessed=6 * PAIR_BYTES, transcendentals=0
+            ),
+            compiler_params=pltpu.CompilerParams(vmem_limit_bytes=LIMIT),
+        )(*operands)
+
     def gather_row(name, row):
-        return call(
-            gather_kernel,
-            name,
-            3,
-            shape_of(*field),
-            [at_column(*pairs), at_column(*field), radial_two_spec],
-            result(*field),
-            [message],
-            PAIR_FLOPS,
-        )(basis_row, row, weights)
+        return single(gather_kernel, name, shape_of(*field), [], basis_row, row, weights)
 
     hidden_row = own_row(hidden)
     slope_1, kind_sums = slope_of(1, ())
@@ -696,40 +696,19 @@
     second_row = gather_row("second_row", hidden_row)
     slope_0, kind_sums = slope_of(0, (kind_sums,))
     second_row, kind_sums = lax.optimization_barrier((second_row, kind_sums))
-    message_grad = call(
-        second_kernel,
-        "second_outer",
-        6,
-        shape_of(*field, kind=BF16),
-        [
-            at_column(*pairs), *outer_specs(*field), radial_two_spec, mix_two_spec, upstream_spec,
-            whole(*field),
-        ],
-        result(*field),
-        [message],
-        PAIR_FLOPS,
-    )(basis_outer, *hidden_outer, weights, weights, weights, second_row)
+    message_grad = single(
+        second_kernel, "second_outer", shape_of(*field, kind=BF16), [message],
+        basis_outer, *hidden_outer, weights, second_row,
+    )
 
     grad_row = own_row(message_grad)
     slope_2, kind_sums = slope_of(2, (kind_sums,))
     grad_row, kind_sums = lax.optimization_barrier((grad_row, kind_sums))
     slopes = (slope_0, slope_1, slope_2)
     grad_outer = outer_rows(grad_row)
-    projected = call(
-        first_kernel,
-        "first_outer",
-        6,
-        shape_of(ORDERS * KINDS, ATOMS, kind=BF16),
-        [
-            at_column(*pairs), *outer_specs(*field), radial_two_spec, mix_one_spec, upstream_spec,
-            whole(*field), weight(TABLE, ORDERS * KINDS), whole(*field),
-        ],
-        result(ORDERS * KINDS, ATOMS),
-        [message],
-        PAIR_FLOPS,
-    )(
-        basis_outer, *grad_outer, weights, weights, weights, first_gate, weights,
-        gather_row("first_row", grad_row),
+    projected = single(
+        first_kernel, "first_outer", shape_of(ORDERS * KINDS, ATOMS, kind=BF16), [message],
+        basis_outer, *grad_outer, weights, first_gate, gather_row("first_row", grad_row),
     )
 
     hiddens = (hidden_outer[0], hidden_row, hidden_outer[1])

time: 116 us -> 113 us (0.974)
  waiting for transfers between devices: 2.29 us -> 5.99 us
  local copies, waits for them, and re-layouts: 4.09 us -> 1.08 us
  starting transfers between devices: 30.3 us -> 27.9 us
  Pallas kernels: 76.3 us -> 75 us
    ppermute x16, waiting for transfers between devices: 2.29 us -> 5.99 us  [swap(): lax.ppermute(cell, axis, pairs + [(right, left) for left, right in pairs])]
    unnamed x12 -> x8, local copies, waits for them, and re-layouts: 4.09 us -> 1.08 us
    ppermute x16, starting transfers between devices: 30.3 us -> 27.9 us  [swap(): lax.ppermute(cell, axis, pairs + [(right, left) for left, right in pairs])]
  transfers between devices with their start and end apart: 16 -> 16, of which waited for: 2 -> 4; matrix products, arithmetic and copies ran while one was open for 0% -> 0% of each run, Pallas kernels for 43% -> 43%
where the time goes in v4:
time: 113 us; the launch traced here: 112 us
  Pallas kernels  75 us (66%)
  starting transfers between devices  27.9 us (25%)
  waiting for transfers between devices  5.99 us (5%)
  other arithmetic  1.47 us (1%)
    ppermute x16, starting transfers between devices, swap(): lax.ppermute(cell, axis, pairs + [(right, left) for left, right in pairs])  27.9 us
    pallas_call x3, Pallas kernels, slope_of(): call(functools.partial(slope_kernel, group), f'slope_{group}', 3, (shape_...  21.5 us
    pallas_call x4, Pallas kernels, single(): pl.pallas_call(kernel, name=name, out_shape=out_shape, in_specs=[vmem] *...  15 us
    pallas_call x3, Pallas kernels, on_device(): call(functools.partial(pair_kernel, group), f'pair_{group}', 3, shape_of(...  11.8 us
    pallas_call x1, Pallas kernels, on_device(): call(functools.partial(basis_kernel, OUTER), 'basis_outer', 6, (shape_of(...  10.4 us
    ppermute x16, waiting for transfers between devices, swap(): lax.ppermute(cell, axis, pairs + [(right, left) for left, right in pairs])  5.99 us
    pallas_call x2, Pallas kernels, on_device(): call(functools.partial(kind_kernel, group), f'last_{group}', 3, shape_of(...  5.38 us
    pallas_call x1, Pallas kernels, on_device(): call(functools.partial(basis_kernel, 1), 'basis_row', 3, (shape_of(3, *pa...  5.05 us
  transfers between devices with their start and end apart: 16, of which 4 were waited for; matrix products, arithmetic and copies ran while one was open for 0% of the time, Pallas kernels for 43%

profile of v4, /device:TPU:1, one launch (start us, length us, event | category | flops | bytes accessed | tf_op | source)
XLA Modules:
  0.0 112.4 jit_solution(17194566405491802228)
XLA Ops:
  0.6 0.7 pad_add_fusion.parity_ref
  1.3 1.8 %prepare.1 = (f32[9,1,128]{2,1,0:T(1,128)}, f32[3,8,128]{2,1,0:T(8,128)}, f32[9,1,128]{2,1,0:T(1,128)}, f32[3,1,128]{2,1,0:T(1,128)}, f32[1152,128]{1,0:T(8,128)}) custom-call(s32[2]{0:T(128)} %pad_add_fusion.parity_ref, s32[1,1,3]{2,1,0:T(1,128)} %counts_ref.1, f32[6]{0:T(128)} %masses_ref.1, f32[9,1,128]{2,1,0:T(1,128)} %bitcast.42, ...), custom_call_target="tpu_custom_call" | custom-call | tf_op jit(solution)/shard_map/prepare/pallas_call | solution.py:604
  3.1 8.9 %collective-permute-start.1 = (f32[3,8,128]{2,1,0:T(8,128)}, f32[3,8,128]{2,1,0:T(8,128)S(1)}, u32[]{:S(2)}, u32[]{:S(2)}) collective-permute-start(f32[3,8,128]{2,1,0:T(8,128)} %get-tuple-element.28), channel_id=1, source_target_pairs={{16,32},{48,64},{80,96},{112,128},{144,160},{176,192},{208,224},{2... | collective-permute-start | bytes 36872 | tf_op jit(solution)/shard_map/ppermute | solution.py:525
  12.0 0.0 collective-permute-start
  12.0 1.3 %collective-permute-done.1 = f32[3,8,128]{2,1,0:T(8,128)S(1)} collective-permute-done((f32[3,8,128]{2,1,0:T(8,128)}, f32[3,8,128]{2,1,0:T(8,128)S(1)}, u32[]{:S(2)}, u32[]{:S(2)}) %collective-permute-start.1) | collective-permute-done | bytes 12320 | tf_op jit(solution)/shard_map/ppermute | solution.py:525
  13.3 1.5 %collective-permute-done = f32[3,8,128]{2,1,0:T(8,128)S(1)} collective-permute-done((f32[3,8,128]{2,1,0:T(8,128)}, f32[3,8,128]{2,1,0:T(8,128)S(1)}, u32[]{:S(2)}, u32[]{:S(2)}) %collective-permute-start) | collective-permute-done | bytes 12320 | tf_op jit(solution)/shard_map/ppermute | solution.py:525
  14.7 0.7 pad_maximum_fusion.3.own_ref.refs_0_.near_ref
  15.5 2.3 %collective-permute-start.2 = (f32[3,3,8,128]{3,2,1,0:T(8,128)S(1)}, f32[3,3,8,128]{3,2,1,0:T(8,128)S(1)}, u32[]{:S(2)}, u32[]{:S(2)}) collective-permute-start(f32[3,3,8,128]{3,2,1,0:T(8,128)S(1)} %pad_maximum_fusion.3.own_ref.refs_0_.near_ref), channel_id=1, source_target_pairs={{1,2},{3,4},{5,6},{7,8},{9,10},{11,12},{13,14},{15,0},{2,1},{4,3},... | collective-permute-start | bytes 110600 | tf_op jit(solution)/shard_map/ppermute | solution.py:525
  17.8 0.9 collective-permute-start.3
  18.6 1.1 copy-done
  19.7 5.0 %basis_row.1 = (bf16[3,8,384,384]{3,2,1,0:T(8,128)(2,1)S(1)}, f32[384,128]{1,0:T(8,128)S(1)}) custom-call(f32[3,3,8,128]{3,2,1,0:T(8,128)S(1)} %pad_maximum_fusion.3.own_ref.refs_0_.near_ref, f32[3,3,8,128]{3,2,1,0:T(8,128)S(1)} %pad_maximum_fusion.3.own_ref.refs_0_.near_ref, f32[1152,128]{1,0:T(8,128)S(1)} %copy-done, f32[1152,128]{1,0:T(8,128)S(1)} %copy-done), custom_call_target="tpu_custom_call" | custom-call | flops 905969664 | bytes 7077888 | tf_op jit(solution)/shard_map/basis_row/pallas_call | solution.py:641
  24.7 0.0 collective-permute-done.2.refs_1_.near_ref
  24.8 0.0 collective-permute-done.3.refs_0_.near_ref
  24.8 10.4 %basis_outer.1 = (bf16[6,8,384,384]{3,2,1,0:T(8,128)(2,1)S(1)}, bf16[384,128]{1,0:T(8,128)(2,1)S(1)}, f32[384,128]{1,0:T(8,128)S(1)}) custom-call(f32[3,3,8,128]{3,2,1,0:T(8,128)S(1)} %pad_maximum_fusion.3.own_ref.refs_0_.near_ref, f32[3,3,8,128]{3,2,1,0:T(8,128)S(1)} %collective-permute-done.3.refs_0_.near_ref, ...), custom_call_target="tpu_custom_call" | custom-call | flops 1811939328 | bytes 14155776 | tf_op jit(solution)/shard_map/basis_outer/pallas_call | solution.py:651
  35.1 4.3 %collective-permute-start.5 = (bf16[384,128]{1,0:T(8,128)(2,1)S(1)}, bf16[384,128]{1,0:T(8,128)(2,1)S(1)}, u32[]{:S(2)}, u32[]{:S(2)}) collective-permute-start(bf16[384,128]{1,0:T(8,128)(2,1)S(1)} %get-tuple-element.32), channel_id=1, source_target_pairs={{16,32},{48,64},{80,96},{112,128},{144,160},{176,192},{208,224},{2... | collective-permute-start | bytes 294920 | tf_op jit(solution)/shard_map/ppermute | solution.py:525
  39.4 0.0 collective-permute-start.4
  39.4 7.2 %slope_1.1 = (bf16[3,8,384,384]{3,2,1,0:T(8,128)(2,1)S(1)}, f32[8,384,128]{2,1,0:T(8,128)S(1)}) custom-call(f32[3,3,8,128]{3,2,1,0:T(8,128)S(1)} %pad_maximum_fusion.3.own_ref.refs_0_.near_ref, f32[3,3,8,128]{3,2,1,0:T(8,128)S(1)} %pad_maximum_fusion.3.own_ref.refs_0_.near_ref), custom_call_target="tpu_custom_call" | custom-call | flops 905969664 | bytes 7077888 | tf_op jit(solution)/shard_map/slope_1/pallas_call | solution.py:664
  46.6 0.0 collective-permute-done.5
  46.6 0.0 collective-permute-done.4
  46.7 0.4 collective-permute-start.6
  47.1 0.5 collective-permute-start.7
  47.6 7.2 %slope_0.1 = (bf16[3,8,384,384]{3,2,1,0:T(8,128)(2,1)S(1)}, f32[8,384,128]{2,1,0:T(8,128)S(1)}) custom-call(f32[3,3,8,128]{3,2,1,0:T(8,128)S(1)} %pad_maximum_fusion.3.own_ref.refs_0_.near_ref, f32[3,3,8,128]{3,2,1,0:T(8,128)S(1)} %collective-permute-done.3.refs_0_.near_ref, f32[8,384,128]{2,1,0:T(8,128)S(1)} %get-tuple-element.35.refs_0_), custom_call_target="tpu_custom_call" | custom-call | flops 905969664 | bytes 7077888 | tf_op jit(solution)/shard_map/slope_0/pallas_call | solution.py:664
  54.7 2.4 %second_row.1.before_ref = f32[384,128]{1,0:T(8,128)S(1)} custom-call(bf16[3,8,384,384]{3,2,1,0:T(8,128)(2,1)S(1)} %get-tuple-element.30.basis_ref, bf16[3,384,128]{2,1,0:T(8,128)(2,1)S(1)} %pad_maximum_fusion.field_ref.near_hidden_ref.hidden_ref, f32[1152,128]{1,0:T(8,128)S(1)} %copy-done.1), custom_call_target="tpu_custom_call" | custom-call | flops 1811939328 | bytes 14155776 | tf_op jit(solution)/shard_map/second_row/pallas_call | solution.py:676
  57.1 0.0 collective-permute-done.6.hidden_0.near_hidden_ref
  57.1 0.0 collective-permute-done.7.hidden_2.near_hidden_ref
  57.1 5.0 %second_outer.1 = bf16[384,128]{1,0:T(8,128)(2,1)S(1)} custom-call(bf16[6,8,384,384]{3,2,1,0:T(8,128)(2,1)S(1)} %get-tuple-element.39.basis_ref, bf16[3,384,128]{2,1,0:T(8,128)(2,1)S(1)} %collective-permute-done.6.hidden_0.near_hidden_ref, bf16[3,384,128]{2,1,0:T(8,128)(2,1)S(1)} %collective-permute-done.7.hidden_2.near_hidden_ref, ...), custom_call_target="tpu_custom_call" | custom-call | flops 1811939328 | bytes 14155776 | tf_op jit(solution)/shard_map/second_outer/pallas_call | solution.py:676
  62.2 3.0 %collective-permute-start.9 = (bf16[384,128]{1,0:T(8,128)(2,1)S(1)}, bf16[384,128]{1,0:T(8,128)(2,1)S(1)}, u32[]{:S(2)}, u32[]{:S(2)}) collective-permute-start(bf16[384,128]{1,0:T(8,128)(2,1)S(1)} %second_outer.1), channel_id=1, source_target_pairs={{16,32},{48,64},{80,96},{112,128},{144,160},{176,192},{208,224},{2... | collective-permute-start | bytes 294920 | tf_op jit(solution)/shard_map/ppermute | solution.py:525
  65.2 0.0 collective-permute-start.8
  65.2 7.2 %slope_2.1 = (bf16[3,8,384,384]{3,2,1,0:T(8,128)(2,1)S(1)}, f32[8,384,128]{2,1,0:T(8,128)S(1)}) custom-call(f32[3,3,8,128]{3,2,1,0:T(8,128)S(1)} %pad_maximum_fusion.3.own_ref.refs_0_.near_ref, f32[3,3,8,128]{3,2,1,0:T(8,128)S(1)} %collective-permute-done.2.refs_1_.near_ref, f32[8,384,128]{2,1,0:T(8,128)S(1)} %get-tuple-element.37.refs_0_), custom_call_target="tpu_custom_call" | custom-call | flops 905969664 | bytes 7077888 | tf_op jit(solution)/shard_map/slope_2/pallas_call | solution.py:664
  72.4 0.0 collective-permute-done.8
  72.5 1.7 %collective-permute-start.10 = (bf16[3,384,128]{2,1,0:T(8,128)(2,1)S(1)}, bf16[3,384,128]{2,1,0:T(8,128)(2,1)S(1)}, u32[]{:S(2)}, u32[]{:S(2)}) collective-permute-start(bf16[3,384,128]{2,1,0:T(8,128)(2,1)S(1)} %pad_maximum_fusion.1.field_ref.near_grad_ref.grad_ref), channel_id=1, source_target_pairs={{0,1},{2,3},{4,5},{6,7},{8,9},{10,11},{12,13},{14,15},{1,0},{3,2},... | collective-permute-start | bytes 884744 | tf_op jit(solution)/shard_map/ppermute | solution.py:525
  74.2 0.0 collective-permute-start.11
  74.2 2.4 %first_row.1.before_ref = f32[384,128]{1,0:T(8,128)S(1)} custom-call(bf16[3,8,384,384]{3,2,1,0:T(8,128)(2,1)S(1)} %get-tuple-element.30.basis_ref, bf16[3,384,128]{2,1,0:T(8,128)(2,1)S(1)} %pad_maximum_fusion.1.field_ref.near_grad_ref.grad_ref, f32[1152,128]{1,0:T(8,128)S(1)} %copy-done.1), custom_call_target="tpu_custom_call" | custom-call | flops 1811939328 | bytes 14155776 | tf_op jit(solution)/shard_map/first_row/pallas_call | solution.py:676
  76.5 3.9 %pair_1.1.refs_0_ = f32[3,384,128]{2,1,0:T(8,128)S(1)} custom-call(f32[3,3,8,128]{3,2,1,0:T(8,128)S(1)} %pad_maximum_fusion.3.own_ref.refs_0_.near_ref, f32[3,3,8,128]{3,2,1,0:T(8,128)S(1)} %pad_maximum_fusion.3.own_ref.refs_0_.near_ref, bf16[3,8,384,384]{3,2,1,0:T(8,128)(2,1)S(1)} %get-tuple-element.45.slope_ref, ...), custom_call_target="tpu_custom_call" | custom-call | flops 1811939328 | bytes 7077888 | tf_op jit(solution)/shard_map/pair_1/pallas_call | solution.py:718
  80.4 2.8 %collective-permute-done.11.grad_2.near_grad_ref = bf16[3,384,128]{2,1,0:T(8,128)(2,1)S(1)} collective-permute-done((bf16[3,384,128]{2,1,0:T(8,128)(2,1)S(1)}, bf16[3,384,128]{2,1,0:T(8,128)(2,1)S(1)}, u32[]{:S(2)}, u32[]{:S(2)}) %collective-permute-start.11) | collective-permute-done | bytes 294944 | tf_op jit(solution)/shard_map/ppermute | solution.py:525
  83.2 5.2 %first_outer.1 = bf16[64,384]{1,0:T(8,128)(2,1)S(1)} custom-call(bf16[6,8,384,384]{3,2,1,0:T(8,128)(2,1)S(1)} %get-tuple-element.39.basis_ref, bf16[3,384,128]{2,1,0:T(8,128)(2,1)S(1)} %collective-permute-done.10.grad_0.near_grad_ref, bf16[3,384,128]{2,1,0:T(8,128)(2,1)S(1)} %collective-permute-done.11.grad_2.near_grad_ref, f32[1152,128]{1,0:T(8,128)S(1)} %copy-done.1, ...), custom_call_target="tpu_custom_call" | custom-call | flops 1811939328 | bytes 14155776 | tf_op jit(solution)/shard_map/first_outer/pallas_call | solution.py:676
  88.4 2.2 %collective-permute-start.13 = (bf16[64,384]{1,0:T(8,128)(2,1)S(1)}, bf16[64,384]{1,0:T(8,128)(2,1)S(1)}, u32[]{:S(2)}, u32[]{:S(2)}) collective-permute-start(bf16[64,384]{1,0:T(8,128)(2,1)S(1)} %first_outer.1), channel_id=1, source_target_pairs={{16,32},{48,64},{80,96},{112,128},{144,160},{176,192},{208,224},{2... | collective-permute-start | bytes 147464 | tf_op jit(solution)/shard_map/ppermute | solution.py:525
  90.6 4.0 %pair_0.1.refs_0_ = f32[3,384,128]{2,1,0:T(8,128)S(1)} custom-call(f32[3,3,8,128]{3,2,1,0:T(8,128)S(1)} %pad_maximum_fusion.3.own_ref.refs_0_.near_ref, f32[3,3,8,128]{3,2,1,0:T(8,128)S(1)} %collective-permute-done.3.refs_0_.near_ref, bf16[3,8,384,384]{3,2,1,0:T(8,128)(2,1)S(1)} %get-tuple-element.44.slope_ref, ...), custom_call_target="tpu_custom_call" | custom-call | flops 1811939328 | bytes 7077888 | tf_op jit(solution)/shard_map/pair_0/pallas_call | solution.py:718
  94.6 0.4 collective-permute-done.13
  95.1 3.4 %collective-permute-start.15 = (bf16[3,64,384]{2,1,0:T(8,128)(2,1)S(1)}, bf16[3,64,384]{2,1,0:T(8,128)(2,1)S(1)}, u32[]{:S(2)}, u32[]{:S(2)}) collective-permute-start(bf16[3,64,384]{2,1,0:T(8,128)(2,1)S(1)} %pad_maximum_fusion.2.projected_ref.own_projected_ref), channel_id=1, source_target_pairs={{0,1},{2,3},{4,5},{6,7},{8,9},{10,11},{12,13},{14,15},{1,0},{3,2},... | collective-permute-start | bytes 442376 | tf_op jit(solution)/shard_map/ppermute | solution.py:525
  98.5 3.9 %pair_2.1.force_ref = f32[3,384,128]{2,1,0:T(8,128)S(1)} custom-call(f32[3,3,8,128]{3,2,1,0:T(8,128)S(1)} %pad_maximum_fusion.3.own_ref.refs_0_.near_ref, f32[3,3,8,128]{3,2,1,0:T(8,128)S(1)} %collective-permute-done.2.refs_1_.near_ref, bf16[3,8,384,384]{3,2,1,0:T(8,128)(2,1)S(1)} %get-tuple-element.38.slope_ref, ...), custom_call_target="tpu_custom_call" | custom-call | flops 1811939328 | bytes 7077888 | tf_op jit(solution)/shard_map/pair_2/pallas_call | solution.py:718
  102.5 0.0 copy-start.2
  102.5 0.0 copy-start.3
  102.5 0.4 collective-permute-start.14
  102.9 2.7 %last_1.1.refs_0_ = f32[384,128]{1,0:T(8,128)S(1)} custom-call(bf16[3,8,384,384]{3,2,1,0:T(8,128)(2,1)S(1)} %get-tuple-element.45.slope_ref, bf16[3,64,384]{2,1,0:T(8,128)(2,1)S(1)} %pad_maximum_fusion.2.projected_ref.own_projected_ref, f32[3,3,8,128]{3,2,1,0:T(8,128)S(1)} %pad_maximum_fusion.3.own_ref.refs_0_.near_ref), custom_call_target="tpu_custom_call" | custom-call | flops 905969664 | bytes 7077888 | tf_op jit(solution)/shard_map/last_1/pallas_call | solution.py:749
  105.6 0.0 collective-permute-done.15.projected_ref
  105.6 2.7 %last_0.1.before_ref = f32[384,128]{1,0:T(8,128)S(1)} custom-call(bf16[3,8,384,384]{3,2,1,0:T(8,128)(2,1)S(1)} %get-tuple-element.44.slope_ref, bf16[3,64,384]{2,1,0:T(8,128)(2,1)S(1)} %collective-permute-done.15.projected_ref, f32[3,3,8,128]{3,2,1,0:T(8,128)S(1)} %collective-permute-done.3.refs_0_.near_ref, f32[384,128]{1,0:T(8,128)S(1)} %last_1.1.refs_0_), custom_call_target="tpu_custom_call" | custom-call | flops 905969664 | bytes 7077888 | tf_op jit(solution)/shard_map/last_0/pallas_call | solution.py:749
  108.3 4.1 %last_2.1 = (f32[9,1,128]{2,1,0:T(1,128)}, f32[9,1,128]{2,1,0:T(1,128)}) custom-call(bf16[3,8,384,384]{3,2,1,0:T(8,128)(2,1)S(1)} %get-tuple-element.38.slope_ref, bf16[3,64,384]{2,1,0:T(8,128)(2,1)S(1)} %collective-permute-done.14.projected_ref, f32[3,3,8,128]{3,2,1,0:T(8,128)S(1)} %collective-permute-done.2.refs_1_.near_ref, ...), custom_call_target="tpu_custom_call" | custom-call | flops 905969664 | bytes 7077888 | tf_op jit(solution)/shard_map/last_2/pallas_call | solution.py:760
  (13 shorter events, 0.1 us)
Async XLA Ops:
  3.1 10.1 %collective-permute-start.1 = (f32[3,8,128]{2,1,0:T(8,128)}, f32[3,8,128]{2,1,0:T(8,128)S(1)}, u32[]{:S(2)}, u32[]{:S(2)}) collective-permute-start(f32[3,8,128]{2,1,0:T(8,128)} %get-tuple-element.28), channel_id=1, source_target_pairs={{16,32},{48,64},{80,96},{112,128},{144,160},{176,192},{208,224},{2... | collective-permute-start | bytes 36872 | tf_op jit(solution)/shard_map/ppermute | solution.py:525
  12.0 2.8 %collective-permute-start = (f32[3,8,128]{2,1,0:T(8,128)}, f32[3,8,128]{2,1,0:T(8,128)S(1)}, u32[]{:S(2)}, u32[]{:S(2)}) collective-permute-start(f32[3,8,128]{2,1,0:T(8,128)} %get-tuple-element.28), channel_id=1, source_target_pairs={{0,16},{32,48},{64,80},{96,112},{128,144},{160,176},{192,208},{224... | collective-permute-start | bytes 36872 | tf_op jit(solution)/shard_map/ppermute | solution.py:525
  15.5 9.3 %collective-permute-start.2 = (f32[3,3,8,128]{3,2,1,0:T(8,128)S(1)}, f32[3,3,8,128]{3,2,1,0:T(8,128)S(1)}, u32[]{:S(2)}, u32[]{:S(2)}) collective-permute-start(f32[3,3,8,128]{3,2,1,0:T(8,128)S(1)} %pad_maximum_fusion.3.own_ref.refs_0_.near_ref), channel_id=1, source_target_pairs={{1,2},{3,4},{5,6},{7,8},{9,10},{11,12},{13,14},{15,0},{2,1},{4,3},... | collective-permute-start | bytes 110600 | tf_op jit(solution)/shard_map/ppermute | solution.py:525
  17.8 7.0 %collective-permute-start.3 = (f32[3,3,8,128]{3,2,1,0:T(8,128)S(1)}, f32[3,3,8,128]{3,2,1,0:T(8,128)S(1)}, u32[]{:S(2)}, u32[]{:S(2)}) collective-permute-start(f32[3,3,8,128]{3,2,1,0:T(8,128)S(1)} %pad_maximum_fusion.3.own_ref.refs_0_.near_ref), channel_id=1, source_target_pairs={{0,1},{2,3},{4,5},{6,7},{8,9},{10,11},{12,13},{14,15},{1,0},{3,2},... | collective-permute-start | bytes 110600 | tf_op jit(solution)/shard_map/ppermute | solution.py:525
  18.6 1.1 copy-start
  24.7 30.0 %copy-start.1 = (f32[1152,128]{1,0:T(8,128)S(1)}, f32[1152,128]{1,0:T(8,128)}, u32[]{:S(2)}) copy-start(f32[1152,128]{1,0:T(8,128)} %get-tuple-element.29.refs_1_.refs_2_.refs_3_.refs_4_.weights_ref.radial_ref) | copy-start | bytes 1769476
  35.1 11.5 %collective-permute-start.5 = (bf16[384,128]{1,0:T(8,128)(2,1)S(1)}, bf16[384,128]{1,0:T(8,128)(2,1)S(1)}, u32[]{:S(2)}, u32[]{:S(2)}) collective-permute-start(bf16[384,128]{1,0:T(8,128)(2,1)S(1)} %get-tuple-element.32), channel_id=1, source_target_pairs={{16,32},{48,64},{80,96},{112,128},{144,160},{176,192},{208,224},{2... | collective-permute-start | bytes 294920 | tf_op jit(solution)/shard_map/ppermute | solution.py:525
  39.4 7.2 %collective-permute-start.4 = (bf16[384,128]{1,0:T(8,128)(2,1)S(1)}, bf16[384,128]{1,0:T(8,128)(2,1)S(1)}, u32[]{:S(2)}, u32[]{:S(2)}) collective-permute-start(bf16[384,128]{1,0:T(8,128)(2,1)S(1)} %get-tuple-element.32), channel_id=1, source_target_pairs={{0,16},{32,48},{64,80},{96,112},{128,144},{160,176},{192,208},{224... | collective-permute-start | bytes 294920 | tf_op jit(solution)/shard_map/ppermute | solution.py:525
  46.7 10.4 %collective-permute-start.6 = (bf16[3,384,128]{2,1,0:T(8,128)(2,1)S(1)}, bf16[3,384,128]{2,1,0:T(8,128)(2,1)S(1)}, u32[]{:S(2)}, u32[]{:S(2)}) collective-permute-start(bf16[3,384,128]{2,1,0:T(8,128)(2,1)S(1)} %pad_maximum_fusion.field_ref.near_hidden_ref.hidden_ref), channel_id=1, source_target_pairs={{0,1},{2,3},{4,5},{6,7},{8,9},{10,11},{12,13},{14,15},{1,0},{3,2},... | collective-permute-start | bytes 884744 | tf_op jit(solution)/shard_map/ppermute | solution.py:525
  47.1 10.1 %collective-permute-start.7 = (bf16[3,384,128]{2,1,0:T(8,128)(2,1)S(1)}, bf16[3,384,128]{2,1,0:T(8,128)(2,1)S(1)}, u32[]{:S(2)}, u32[]{:S(2)}) collective-permute-start(bf16[3,384,128]{2,1,0:T(8,128)(2,1)S(1)} %pad_maximum_fusion.field_ref.near_hidden_ref.hidden_ref), channel_id=1, source_target_pairs={{1,2},{3,4},{5,6},{7,8},{9,10},{11,12},{13,14},{15,0},{2,1},{4,3},... | collective-permute-start | bytes 884744 | tf_op jit(solution)/shard_map/ppermute | solution.py:525
  62.2 10.2 %collective-permute-start.9 = (bf16[384,128]{1,0:T(8,128)(2,1)S(1)}, bf16[384,128]{1,0:T(8,128)(2,1)S(1)}, u32[]{:S(2)}, u32[]{:S(2)}) collective-permute-start(bf16[384,128]{1,0:T(8,128)(2,1)S(1)} %second_outer.1), channel_id=1, source_target_pairs={{16,32},{48,64},{80,96},{112,128},{144,160},{176,192},{208,224},{2... | collective-permute-start | bytes 294920 | tf_op jit(solution)/shard_map/ppermute | solution.py:525
  65.2 7.2 %collective-permute-start.8 = (bf16[384,128]{1,0:T(8,128)(2,1)S(1)}, bf16[384,128]{1,0:T(8,128)(2,1)S(1)}, u32[]{:S(2)}, u32[]{:S(2)}) collective-permute-start(bf16[384,128]{1,0:T(8,128)(2,1)S(1)} %second_outer.1), channel_id=1, source_target_pairs={{0,16},{32,48},{64,80},{96,112},{128,144},{160,176},{192,208},{224... | collective-permute-start | bytes 294920 | tf_op jit(solution)/shard_map/ppermute | solution.py:525
  72.5 8.0 %collective-permute-start.10 = (bf16[3,384,128]{2,1,0:T(8,128)(2,1)S(1)}, bf16[3,384,128]{2,1,0:T(8,128)(2,1)S(1)}, u32[]{:S(2)}, u32[]{:S(2)}) collective-permute-start(bf16[3,384,128]{2,1,0:T(8,128)(2,1)S(1)} %pad_maximum_fusion.1.field_ref.near_grad_ref.grad_ref), channel_id=1, source_target_pairs={{0,1},{2,3},{4,5},{6,7},{8,9},{10,11},{12,13},{14,15},{1,0},{3,2},... | collective-permute-start | bytes 884744 | tf_op jit(solution)/shard_map/ppermute | solution.py:525
  74.2 9.0 %collective-permute-start.11 = (bf16[3,384,128]{2,1,0:T(8,128)(2,1)S(1)}, bf16[3,384,128]{2,1,0:T(8,128)(2,1)S(1)}, u32[]{:S(2)}, u32[]{:S(2)}) collective-permute-start(bf16[3,384,128]{2,1,0:T(8,128)(2,1)S(1)} %pad_maximum_fusion.1.field_ref.near_grad_ref.grad_ref), channel_id=1, source_target_pairs={{1,2},{3,4},{5,6},{7,8},{9,10},{11,12},{13,14},{15,0},{2,1},{4,3},... | collective-permute-start | bytes 884744 | tf_op jit(solution)/shard_map/ppermute | solution.py:525
  88.4 6.6 %collective-permute-start.13 = (bf16[64,384]{1,0:T(8,128)(2,1)S(1)}, bf16[64,384]{1,0:T(8,128)(2,1)S(1)}, u32[]{:S(2)}, u32[]{:S(2)}) collective-permute-start(bf16[64,384]{1,0:T(8,128)(2,1)S(1)} %first_outer.1), channel_id=1, source_target_pairs={{16,32},{48,64},{80,96},{112,128},{144,160},{176,192},{208,224},{2... | collective-permute-start | bytes 147464 | tf_op jit(solution)/shard_map/ppermute | solution.py:525
  90.6 4.4 %collective-permute-start.12 = (bf16[64,384]{1,0:T(8,128)(2,1)S(1)}, bf16[64,384]{1,0:T(8,128)(2,1)S(1)}, u32[]{:S(2)}, u32[]{:S(2)}) collective-permute-start(bf16[64,384]{1,0:T(8,128)(2,1)S(1)} %first_outer.1), channel_id=1, source_target_pairs={{0,16},{32,48},{64,80},{96,112},{128,144},{160,176},{192,208},{224... | collective-permute-start | bytes 147464 | tf_op jit(solution)/shard_map/ppermute | solution.py:525
  95.1 10.5 %collective-permute-start.15 = (bf16[3,64,384]{2,1,0:T(8,128)(2,1)S(1)}, bf16[3,64,384]{2,1,0:T(8,128)(2,1)S(1)}, u32[]{:S(2)}, u32[]{:S(2)}) collective-permute-start(bf16[3,64,384]{2,1,0:T(8,128)(2,1)S(1)} %pad_maximum_fusion.2.projected_ref.own_projected_ref), channel_id=1, source_target_pairs={{0,1},{2,3},{4,5},{6,7},{8,9},{10,11},{12,13},{14,15},{1,0},{3,2},... | collective-permute-start | bytes 442376 | tf_op jit(solution)/shard_map/ppermute | solution.py:525
  102.5 5.8 %copy-start.2 = (f32[9,1,128]{2,1,0:T(1,128)S(1)}, f32[9,1,128]{2,1,0:T(1,128)}, u32[]{:S(2)}) copy-start(f32[9,1,128]{2,1,0:T(1,128)} %get-tuple-element.47.mixed_ref) | copy-start | bytes 13828
  102.5 5.8 %copy-start.3 = (f32[3,1,128]{2,1,0:T(1,128)S(1)}, f32[3,1,128]{2,1,0:T(1,128)}, u32[]{:S(2)}) copy-start(f32[3,1,128]{2,1,0:T(1,128)} %get-tuple-element.48.mass_ref) | copy-start | bytes 4612
  102.5 5.8 %collective-permute-start.14 = (bf16[3,64,384]{2,1,0:T(8,128)(2,1)S(1)}, bf16[3,64,384]{2,1,0:T(8,128)(2,1)S(1)}, u32[]{:S(2)}, u32[]{:S(2)}) collective-permute-start(bf16[3,64,384]{2,1,0:T(8,128)(2,1)S(1)} %pad_maximum_fusion.2.projected_ref.own_projected_ref), channel_id=1, source_target_pairs={{1,2},{3,4},{5,6},{7,8},{9,10},{11,12},{13,14},{15,0},{2,1},{4,3},... | collective-permute-start | bytes 442376 | tf_op jit(solution)/shard_map/ppermute | solution.py:525

commit v5 on v4

--- a/solution.py
+++ b/solution.py
@@ -21,7 +21,7 @@
 ATOMS = COLUMN * SLOTS
 CHANNELS = 128
 PARTS = 9
-CHUNK = 32
+CHUNK = 16
 OUTER = -1
 LIMIT = 8 * 2**20
 

time: 113 us -> 113 us (level)
  no operation moved by 1% of the time
where the time goes in v5:
time: 113 us; the launch traced here: 112 us
  Pallas kernels  75 us (66%)
  starting transfers between devices  27.9 us (25%)
  waiting for transfers between devices  5.99 us (5%)
  other arithmetic  1.47 us (1%)
    ppermute x16, starting transfers between devices, swap(): lax.ppermute(cell, axis, pairs + [(right, left) for left, right in pairs])  27.9 us
    pallas_call x3, Pallas kernels, slope_of(): call(functools.partial(slope_kernel, group), f'slope_{group}', 3, (shape_...  21.5 us
    pallas_call x4, Pallas kernels, single(): pl.pallas_call(kernel, name=name, out_shape=out_shape, in_specs=[vmem] *...  15 us
    pallas_call x3, Pallas kernels, on_device(): call(functools.partial(pair_kernel, group), f'pair_{group}', 3, shape_of(...  11.8 us
    pallas_call x1, Pallas kernels, on_device(): call(functools.partial(basis_kernel, OUTER), 'basis_outer', 6, (shape_of(...  10.4 us
    ppermute x16, waiting for transfers between devices, swap(): lax.ppermute(cell, axis, pairs + [(right, left) for left, right in pairs])  5.99 us
    pallas_call x2, Pallas kernels, on_device(): call(functools.partial(kind_kernel, group), f'last_{group}', 3, shape_of(...  5.38 us
    pallas_call x1, Pallas kernels, on_device(): call(functools.partial(basis_kernel, 1), 'basis_row', 3, (shape_of(3, *pa...  5.05 us
  transfers between devices with their start and end apart: 16, of which 4 were waited for; matrix products, arithmetic and copies ran while one was open for 0% of the time, Pallas kernels for 43%

profile of v5, /device:TPU:1, one launch (start us, length us, event | category | flops | bytes accessed | tf_op | source)
XLA Modules:
  0.0 112.4 jit_solution(17194566405491802228)
XLA Ops:
  0.6 0.7 pad_add_fusion.parity_ref
  1.3 1.8 %prepare.1 = (f32[9,1,128]{2,1,0:T(1,128)}, f32[3,8,128]{2,1,0:T(8,128)}, f32[9,1,128]{2,1,0:T(1,128)}, f32[3,1,128]{2,1,0:T(1,128)}, f32[1152,128]{1,0:T(8,128)}) custom-call(s32[2]{0:T(128)} %pad_add_fusion.parity_ref, s32[1,1,3]{2,1,0:T(1,128)} %counts_ref.1, f32[6]{0:T(128)} %masses_ref.1, f32[9,1,128]{2,1,0:T(1,128)} %bitcast.42, ...), custom_call_target="tpu_custom_call" | custom-call | tf_op jit(solution)/shard_map/prepare/pallas_call | solution.py:604
  3.1 8.9 %collective-permute-start.1 = (f32[3,8,128]{2,1,0:T(8,128)}, f32[3,8,128]{2,1,0:T(8,128)S(1)}, u32[]{:S(2)}, u32[]{:S(2)}) collective-permute-start(f32[3,8,128]{2,1,0:T(8,128)} %get-tuple-element.28), channel_id=1, source_target_pairs={{16,32},{48,64},{80,96},{112,128},{144,160},{176,192},{208,224},{2... | collective-permute-start | bytes 36872 | tf_op jit(solution)/shard_map/ppermute | solution.py:525
  12.0 0.0 collective-permute-start
  12.0 1.3 %collective-permute-done.1 = f32[3,8,128]{2,1,0:T(8,128)S(1)} collective-permute-done((f32[3,8,128]{2,1,0:T(8,128)}, f32[3,8,128]{2,1,0:T(8,128)S(1)}, u32[]{:S(2)}, u32[]{:S(2)}) %collective-permute-start.1) | collective-permute-done | bytes 12320 | tf_op jit(solution)/shard_map/ppermute | solution.py:525
  13.3 1.5 %collective-permute-done = f32[3,8,128]{2,1,0:T(8,128)S(1)} collective-permute-done((f32[3,8,128]{2,1,0:T(8,128)}, f32[3,8,128]{2,1,0:T(8,128)S(1)}, u32[]{:S(2)}, u32[]{:S(2)}) %collective-permute-start) | collective-permute-done | bytes 12320 | tf_op jit(solution)/shard_map/ppermute | solution.py:525
  14.7 0.7 pad_maximum_fusion.3.own_ref.refs_0_.near_ref
  15.5 2.3 %collective-permute-start.2 = (f32[3,3,8,128]{3,2,1,0:T(8,128)S(1)}, f32[3,3,8,128]{3,2,1,0:T(8,128)S(1)}, u32[]{:S(2)}, u32[]{:S(2)}) collective-permute-start(f32[3,3,8,128]{3,2,1,0:T(8,128)S(1)} %pad_maximum_fusion.3.own_ref.refs_0_.near_ref), channel_id=1, source_target_pairs={{1,2},{3,4},{5,6},{7,8},{9,10},{11,12},{13,14},{15,0},{2,1},{4,3},... | collective-permute-start | bytes 110600 | tf_op jit(solution)/shard_map/ppermute | solution.py:525
  17.8 0.9 collective-permute-start.3
  18.6 1.1 copy-done
  19.7 5.0 %basis_row.1 = (bf16[3,8,384,384]{3,2,1,0:T(8,128)(2,1)S(1)}, f32[384,128]{1,0:T(8,128)S(1)}) custom-call(f32[3,3,8,128]{3,2,1,0:T(8,128)S(1)} %pad_maximum_fusion.3.own_ref.refs_0_.near_ref, f32[3,3,8,128]{3,2,1,0:T(8,128)S(1)} %pad_maximum_fusion.3.own_ref.refs_0_.near_ref, f32[1152,128]{1,0:T(8,128)S(1)} %copy-done, f32[1152,128]{1,0:T(8,128)S(1)} %copy-done), custom_call_target="tpu_custom_call" | custom-call | flops 905969664 | bytes 7077888 | tf_op jit(solution)/shard_map/basis_row/pallas_call | solution.py:641
  24.7 0.0 collective-permute-done.2.refs_1_.near_ref
  24.8 0.0 collective-permute-done.3.refs_0_.near_ref
  24.8 10.4 %basis_outer.1 = (bf16[6,8,384,384]{3,2,1,0:T(8,128)(2,1)S(1)}, bf16[384,128]{1,0:T(8,128)(2,1)S(1)}, f32[384,128]{1,0:T(8,128)S(1)}) custom-call(f32[3,3,8,128]{3,2,1,0:T(8,128)S(1)} %pad_maximum_fusion.3.own_ref.refs_0_.near_ref, f32[3,3,8,128]{3,2,1,0:T(8,128)S(1)} %collective-permute-done.3.refs_0_.near_ref, ...), custom_call_target="tpu_custom_call" | custom-call | flops 1811939328 | bytes 14155776 | tf_op jit(solution)/shard_map/basis_outer/pallas_call | solution.py:651
  35.1 4.3 %collective-permute-start.5 = (bf16[384,128]{1,0:T(8,128)(2,1)S(1)}, bf16[384,128]{1,0:T(8,128)(2,1)S(1)}, u32[]{:S(2)}, u32[]{:S(2)}) collective-permute-start(bf16[384,128]{1,0:T(8,128)(2,1)S(1)} %get-tuple-element.32), channel_id=1, source_target_pairs={{16,32},{48,64},{80,96},{112,128},{144,160},{176,192},{208,224},{2... | collective-permute-start | bytes 294920 | tf_op jit(solution)/shard_map/ppermute | solution.py:525
  39.4 0.0 collective-permute-start.4
  39.4 7.2 %slope_1.1 = (bf16[3,8,384,384]{3,2,1,0:T(8,128)(2,1)S(1)}, f32[8,384,128]{2,1,0:T(8,128)S(1)}) custom-call(f32[3,3,8,128]{3,2,1,0:T(8,128)S(1)} %pad_maximum_fusion.3.own_ref.refs_0_.near_ref, f32[3,3,8,128]{3,2,1,0:T(8,128)S(1)} %pad_maximum_fusion.3.own_ref.refs_0_.near_ref), custom_call_target="tpu_custom_call" | custom-call | flops 905969664 | bytes 7077888 | tf_op jit(solution)/shard_map/slope_1/pallas_call | solution.py:664
  46.6 0.0 collective-permute-done.5
  46.6 0.0 collective-permute-done.4
  46.7 0.4 collective-permute-start.6
  47.1 0.5 collective-permute-start.7
  47.6 7.2 %slope_0.1 = (bf16[3,8,384,384]{3,2,1,0:T(8,128)(2,1)S(1)}, f32[8,384,128]{2,1,0:T(8,128)S(1)}) custom-call(f32[3,3,8,128]{3,2,1,0:T(8,128)S(1)} %pad_maximum_fusion.3.own_ref.refs_0_.near_ref, f32[3,3,8,128]{3,2,1,0:T(8,128)S(1)} %collective-permute-done.3.refs_0_.near_ref, f32[8,384,128]{2,1,0:T(8,128)S(1)} %get-tuple-element.35.refs_0_), custom_call_target="tpu_custom_call" | custom-call | flops 905969664 | bytes 7077888 | tf_op jit(solution)/shard_map/slope_0/pallas_call | solution.py:664
  54.7 2.4 %second_row.1.before_ref = f32[384,128]{1,0:T(8,128)S(1)} custom-call(bf16[3,8,384,384]{3,2,1,0:T(8,128)(2,1)S(1)} %get-tuple-element.30.basis_ref, bf16[3,384,128]{2,1,0:T(8,128)(2,1)S(1)} %pad_maximum_fusion.field_ref.near_hidden_ref.hidden_ref, f32[1152,128]{1,0:T(8,128)S(1)} %copy-done.1), custom_call_target="tpu_custom_call" | custom-call | flops 1811939328 | bytes 14155776 | tf_op jit(solution)/shard_map/second_row/pallas_call | solution.py:676
  57.1 0.0 collective-permute-done.6.hidden_0.near_hidden_ref
  57.1 0.0 collective-permute-done.7.hidden_2.near_hidden_ref
  57.1 5.0 %second_outer.1 = bf16[384,128]{1,0:T(8,128)(2,1)S(1)} custom-call(bf16[6,8,384,384]{3,2,1,0:T(8,128)(2,1)S(1)} %get-tuple-element.39.basis_ref, bf16[3,384,128]{2,1,0:T(8,128)(2,1)S(1)} %collective-permute-done.6.hidden_0.near_hidden_ref, bf16[3,384,128]{2,1,0:T(8,128)(2,1)S(1)} %collective-permute-done.7.hidden_2.near_hidden_ref, ...), custom_call_target="tpu_custom_call" | custom-call | flops 1811939328 | bytes 14155776 | tf_op jit(solution)/shard_map/second_outer/pallas_call | solution.py:676
  62.2 3.0 %collective-permute-start.9 = (bf16[384,128]{1,0:T(8,128)(2,1)S(1)}, bf16[384,128]{1,0:T(8,128)(2,1)S(1)}, u32[]{:S(2)}, u32[]{:S(2)}) collective-permute-start(bf16[384,128]{1,0:T(8,128)(2,1)S(1)} %second_outer.1), channel_id=1, source_target_pairs={{16,32},{48,64},{80,96},{112,128},{144,160},{176,192},{208,224},{2... | collective-permute-start | bytes 294920 | tf_op jit(solution)/shard_map/ppermute | solution.py:525
  65.2 0.0 collective-permute-start.8
  65.2 7.2 %slope_2.1 = (bf16[3,8,384,384]{3,2,1,0:T(8,128)(2,1)S(1)}, f32[8,384,128]{2,1,0:T(8,128)S(1)}) custom-call(f32[3,3,8,128]{3,2,1,0:T(8,128)S(1)} %pad_maximum_fusion.3.own_ref.refs_0_.near_ref, f32[3,3,8,128]{3,2,1,0:T(8,128)S(1)} %collective-permute-done.2.refs_1_.near_ref, f32[8,384,128]{2,1,0:T(8,128)S(1)} %get-tuple-element.37.refs_0_), custom_call_target="tpu_custom_call" | custom-call | flops 905969664 | bytes 7077888 | tf_op jit(solution)/shard_map/slope_2/pallas_call | solution.py:664
  72.4 0.0 collective-permute-done.8
  72.5 1.7 %collective-permute-start.10 = (bf16[3,384,128]{2,1,0:T(8,128)(2,1)S(1)}, bf16[3,384,128]{2,1,0:T(8,128)(2,1)S(1)}, u32[]{:S(2)}, u32[]{:S(2)}) collective-permute-start(bf16[3,384,128]{2,1,0:T(8,128)(2,1)S(1)} %pad_maximum_fusion.1.field_ref.near_grad_ref.grad_ref), channel_id=1, source_target_pairs={{0,1},{2,3},{4,5},{6,7},{8,9},{10,11},{12,13},{14,15},{1,0},{3,2},... | collective-permute-start | bytes 884744 | tf_op jit(solution)/shard_map/ppermute | solution.py:525
  74.2 0.0 collective-permute-start.11
  74.2 2.4 %first_row.1.before_ref = f32[384,128]{1,0:T(8,128)S(1)} custom-call(bf16[3,8,384,384]{3,2,1,0:T(8,128)(2,1)S(1)} %get-tuple-element.30.basis_ref, bf16[3,384,128]{2,1,0:T(8,128)(2,1)S(1)} %pad_maximum_fusion.1.field_ref.near_grad_ref.grad_ref, f32[1152,128]{1,0:T(8,128)S(1)} %copy-done.1), custom_call_target="tpu_custom_call" | custom-call | flops 1811939328 | bytes 14155776 | tf_op jit(solution)/shard_map/first_row/pallas_call | solution.py:676
  76.5 3.9 %pair_1.1.refs_0_ = f32[3,384,128]{2,1,0:T(8,128)S(1)} custom-call(f32[3,3,8,128]{3,2,1,0:T(8,128)S(1)} %pad_maximum_fusion.3.own_ref.refs_0_.near_ref, f32[3,3,8,128]{3,2,1,0:T(8,128)S(1)} %pad_maximum_fusion.3.own_ref.refs_0_.near_ref, bf16[3,8,384,384]{3,2,1,0:T(8,128)(2,1)S(1)} %get-tuple-element.45.slope_ref, ...), custom_call_target="tpu_custom_call" | custom-call | flops 1811939328 | bytes 7077888 | tf_op jit(solution)/shard_map/pair_1/pallas_call | solution.py:718
  80.4 2.8 %collective-permute-done.11.grad_2.near_grad_ref = bf16[3,384,128]{2,1,0:T(8,128)(2,1)S(1)} collective-permute-done((bf16[3,384,128]{2,1,0:T(8,128)(2,1)S(1)}, bf16[3,384,128]{2,1,0:T(8,128)(2,1)S(1)}, u32[]{:S(2)}, u32[]{:S(2)}) %collective-permute-start.11) | collective-permute-done | bytes 294944 | tf_op jit(solution)/shard_map/ppermute | solution.py:525
  83.2 5.2 %first_outer.1 = bf16[64,384]{1,0:T(8,128)(2,1)S(1)} custom-call(bf16[6,8,384,384]{3,2,1,0:T(8,128)(2,1)S(1)} %get-tuple-element.39.basis_ref, bf16[3,384,128]{2,1,0:T(8,128)(2,1)S(1)} %collective-permute-done.10.grad_0.near_grad_ref, bf16[3,384,128]{2,1,0:T(8,128)(2,1)S(1)} %collective-permute-done.11.grad_2.near_grad_ref, f32[1152,128]{1,0:T(8,128)S(1)} %copy-done.1, ...), custom_call_target="tpu_custom_call" | custom-call | flops 1811939328 | bytes 14155776 | tf_op jit(solution)/shard_map/first_outer/pallas_call | solution.py:676
  88.4 2.2 %collective-permute-start.13 = (bf16[64,384]{1,0:T(8,128)(2,1)S(1)}, bf16[64,384]{1,0:T(8,128)(2,1)S(1)}, u32[]{:S(2)}, u32[]{:S(2)}) collective-permute-start(bf16[64,384]{1,0:T(8,128)(2,1)S(1)} %first_outer.1), channel_id=1, source_target_pairs={{16,32},{48,64},{80,96},{112,128},{144,160},{176,192},{208,224},{2... | collective-permute-start | bytes 147464 | tf_op jit(solution)/shard_map/ppermute | solution.py:525
  90.6 4.0 %pair_0.1.refs_0_ = f32[3,384,128]{2,1,0:T(8,128)S(1)} custom-call(f32[3,3,8,128]{3,2,1,0:T(8,128)S(1)} %pad_maximum_fusion.3.own_ref.refs_0_.near_ref, f32[3,3,8,128]{3,2,1,0:T(8,128)S(1)} %collective-permute-done.3.refs_0_.near_ref, bf16[3,8,384,384]{3,2,1,0:T(8,128)(2,1)S(1)} %get-tuple-element.44.slope_ref, ...), custom_call_target="tpu_custom_call" | custom-call | flops 1811939328 | bytes 7077888 | tf_op jit(solution)/shard_map/pair_0/pallas_call | solution.py:718
  94.6 0.4 collective-permute-done.13
  95.1 3.4 %collective-permute-start.15 = (bf16[3,64,384]{2,1,0:T(8,128)(2,1)S(1)}, bf16[3,64,384]{2,1,0:T(8,128)(2,1)S(1)}, u32[]{:S(2)}, u32[]{:S(2)}) collective-permute-start(bf16[3,64,384]{2,1,0:T(8,128)(2,1)S(1)} %pad_maximum_fusion.2.projected_ref.own_projected_ref), channel_id=1, source_target_pairs={{0,1},{2,3},{4,5},{6,7},{8,9},{10,11},{12,13},{14,15},{1,0},{3,2},... | collective-permute-start | bytes 442376 | tf_op jit(solution)/shard_map/ppermute | solution.py:525
  98.5 3.9 %pair_2.1.force_ref = f32[3,384,128]{2,1,0:T(8,128)S(1)} custom-call(f32[3,3,8,128]{3,2,1,0:T(8,128)S(1)} %pad_maximum_fusion.3.own_ref.refs_0_.near_ref, f32[3,3,8,128]{3,2,1,0:T(8,128)S(1)} %collective-permute-done.2.refs_1_.near_ref, bf16[3,8,384,384]{3,2,1,0:T(8,128)(2,1)S(1)} %get-tuple-element.38.slope_ref, ...), custom_call_target="tpu_custom_call" | custom-call | flops 1811939328 | bytes 7077888 | tf_op jit(solution)/shard_map/pair_2/pallas_call | solution.py:718
  102.5 0.0 copy-start.2
  102.5 0.0 copy-start.3
  102.5 0.4 collective-permute-start.14
  102.9 2.7 %last_1.1.refs_0_ = f32[384,128]{1,0:T(8,128)S(1)} custom-call(bf16[3,8,384,384]{3,2,1,0:T(8,128)(2,1)S(1)} %get-tuple-element.45.slope_ref, bf16[3,64,384]{2,1,0:T(8,128)(2,1)S(1)} %pad_maximum_fusion.2.projected_ref.own_projected_ref, f32[3,3,8,128]{3,2,1,0:T(8,128)S(1)} %pad_maximum_fusion.3.own_ref.refs_0_.near_ref), custom_call_target="tpu_custom_call" | custom-call | flops 905969664 | bytes 7077888 | tf_op jit(solution)/shard_map/last_1/pallas_call | solution.py:749
  105.6 0.0 collective-permute-done.15.projected_ref
  105.6 2.7 %last_0.1.before_ref = f32[384,128]{1,0:T(8,128)S(1)} custom-call(bf16[3,8,384,384]{3,2,1,0:T(8,128)(2,1)S(1)} %get-tuple-element.44.slope_ref, bf16[3,64,384]{2,1,0:T(8,128)(2,1)S(1)} %collective-permute-done.15.projected_ref, f32[3,3,8,128]{3,2,1,0:T(8,128)S(1)} %collective-permute-done.3.refs_0_.near_ref, f32[384,128]{1,0:T(8,128)S(1)} %last_1.1.refs_0_), custom_call_target="tpu_custom_call" | custom-call | flops 905969664 | bytes 7077888 | tf_op jit(solution)/shard_map/last_0/pallas_call | solution.py:749
  108.3 4.1 %last_2.1 = (f32[9,1,128]{2,1,0:T(1,128)}, f32[9,1,128]{2,1,0:T(1,128)}) custom-call(bf16[3,8,384,384]{3,2,1,0:T(8,128)(2,1)S(1)} %get-tuple-element.38.slope_ref, bf16[3,64,384]{2,1,0:T(8,128)(2,1)S(1)} %collective-permute-done.14.projected_ref, f32[3,3,8,128]{3,2,1,0:T(8,128)S(1)} %collective-permute-done.2.refs_1_.near_ref, ...), custom_call_target="tpu_custom_call" | custom-call | flops 905969664 | bytes 7077888 | tf_op jit(solution)/shard_map/last_2/pallas_call | solution.py:760
  (13 shorter events, 0.1 us)
Async XLA Ops:
  3.1 10.1 %collective-permute-start.1 = (f32[3,8,128]{2,1,0:T(8,128)}, f32[3,8,128]{2,1,0:T(8,128)S(1)}, u32[]{:S(2)}, u32[]{:S(2)}) collective-permute-start(f32[3,8,128]{2,1,0:T(8,128)} %get-tuple-element.28), channel_id=1, source_target_pairs={{16,32},{48,64},{80,96},{112,128},{144,160},{176,192},{208,224},{2... | collective-permute-start | bytes 36872 | tf_op jit(solution)/shard_map/ppermute | solution.py:525
  12.0 2.8 %collective-permute-start = (f32[3,8,128]{2,1,0:T(8,128)}, f32[3,8,128]{2,1,0:T(8,128)S(1)}, u32[]{:S(2)}, u32[]{:S(2)}) collective-permute-start(f32[3,8,128]{2,1,0:T(8,128)} %get-tuple-element.28), channel_id=1, source_target_pairs={{0,16},{32,48},{64,80},{96,112},{128,144},{160,176},{192,208},{224... | collective-permute-start | bytes 36872 | tf_op jit(solution)/shard_map/ppermute | solution.py:525
  15.5 9.3 %collective-permute-start.2 = (f32[3,3,8,128]{3,2,1,0:T(8,128)S(1)}, f32[3,3,8,128]{3,2,1,0:T(8,128)S(1)}, u32[]{:S(2)}, u32[]{:S(2)}) collective-permute-start(f32[3,3,8,128]{3,2,1,0:T(8,128)S(1)} %pad_maximum_fusion.3.own_ref.refs_0_.near_ref), channel_id=1, source_target_pairs={{1,2},{3,4},{5,6},{7,8},{9,10},{11,12},{13,14},{15,0},{2,1},{4,3},... | collective-permute-start | bytes 110600 | tf_op jit(solution)/shard_map/ppermute | solution.py:525
  17.8 7.0 %collective-permute-start.3 = (f32[3,3,8,128]{3,2,1,0:T(8,128)S(1)}, f32[3,3,8,128]{3,2,1,0:T(8,128)S(1)}, u32[]{:S(2)}, u32[]{:S(2)}) collective-permute-start(f32[3,3,8,128]{3,2,1,0:T(8,128)S(1)} %pad_maximum_fusion.3.own_ref.refs_0_.near_ref), channel_id=1, source_target_pairs={{0,1},{2,3},{4,5},{6,7},{8,9},{10,11},{12,13},{14,15},{1,0},{3,2},... | collective-permute-start | bytes 110600 | tf_op jit(solution)/shard_map/ppermute | solution.py:525
  18.6 1.1 copy-start
  24.7 30.0 %copy-start.1 = (f32[1152,128]{1,0:T(8,128)S(1)}, f32[1152,128]{1,0:T(8,128)}, u32[]{:S(2)}) copy-start(f32[1152,128]{1,0:T(8,128)} %get-tuple-element.29.refs_1_.refs_2_.refs_3_.refs_4_.weights_ref.radial_ref) | copy-start | bytes 1769476
  35.1 11.5 %collective-permute-start.5 = (bf16[384,128]{1,0:T(8,128)(2,1)S(1)}, bf16[384,128]{1,0:T(8,128)(2,1)S(1)}, u32[]{:S(2)}, u32[]{:S(2)}) collective-permute-start(bf16[384,128]{1,0:T(8,128)(2,1)S(1)} %get-tuple-element.32), channel_id=1, source_target_pairs={{16,32},{48,64},{80,96},{112,128},{144,160},{176,192},{208,224},{2... | collective-permute-start | bytes 294920 | tf_op jit(solution)/shard_map/ppermute | solution.py:525
  39.4 7.2 %collective-permute-start.4 = (bf16[384,128]{1,0:T(8,128)(2,1)S(1)}, bf16[384,128]{1,0:T(8,128)(2,1)S(1)}, u32[]{:S(2)}, u32[]{:S(2)}) collective-permute-start(bf16[384,128]{1,0:T(8,128)(2,1)S(1)} %get-tuple-element.32), channel_id=1, source_target_pairs={{0,16},{32,48},{64,80},{96,112},{128,144},{160,176},{192,208},{224... | collective-permute-start | bytes 294920 | tf_op jit(solution)/shard_map/ppermute | solution.py:525
  46.7 10.4 %collective-permute-start.6 = (bf16[3,384,128]{2,1,0:T(8,128)(2,1)S(1)}, bf16[3,384,128]{2,1,0:T(8,128)(2,1)S(1)}, u32[]{:S(2)}, u32[]{:S(2)}) collective-permute-start(bf16[3,384,128]{2,1,0:T(8,128)(2,1)S(1)} %pad_maximum_fusion.field_ref.near_hidden_ref.hidden_ref), channel_id=1, source_target_pairs={{0,1},{2,3},{4,5},{6,7},{8,9},{10,11},{12,13},{14,15},{1,0},{3,2},... | collective-permute-start | bytes 884744 | tf_op jit(solution)/shard_map/ppermute | solution.py:525
  47.1 10.1 %collective-permute-start.7 = (bf16[3,384,128]{2,1,0:T(8,128)(2,1)S(1)}, bf16[3,384,128]{2,1,0:T(8,128)(2,1)S(1)}, u32[]{:S(2)}, u32[]{:S(2)}) collective-permute-start(bf16[3,384,128]{2,1,0:T(8,128)(2,1)S(1)} %pad_maximum_fusion.field_ref.near_hidden_ref.hidden_ref), channel_id=1, source_target_pairs={{1,2},{3,4},{5,6},{7,8},{9,10},{11,12},{13,14},{15,0},{2,1},{4,3},... | collective-permute-start | bytes 884744 | tf_op jit(solution)/shard_map/ppermute | solution.py:525
  62.2 10.2 %collective-permute-start.9 = (bf16[384,128]{1,0:T(8,128)(2,1)S(1)}, bf16[384,128]{1,0:T(8,128)(2,1)S(1)}, u32[]{:S(2)}, u32[]{:S(2)}) collective-permute-start(bf16[384,128]{1,0:T(8,128)(2,1)S(1)} %second_outer.1), channel_id=1, source_target_pairs={{16,32},{48,64},{80,96},{112,128},{144,160},{176,192},{208,224},{2... | collective-permute-start | bytes 294920 | tf_op jit(solution)/shard_map/ppermute | solution.py:525
  65.2 7.2 %collective-permute-start.8 = (bf16[384,128]{1,0:T(8,128)(2,1)S(1)}, bf16[384,128]{1,0:T(8,128)(2,1)S(1)}, u32[]{:S(2)}, u32[]{:S(2)}) collective-permute-start(bf16[384,128]{1,0:T(8,128)(2,1)S(1)} %second_outer.1), channel_id=1, source_target_pairs={{0,16},{32,48},{64,80},{96,112},{128,144},{160,176},{192,208},{224... | collective-permute-start | bytes 294920 | tf_op jit(solution)/shard_map/ppermute | solution.py:525
  72.5 8.0 %collective-permute-start.10 = (bf16[3,384,128]{2,1,0:T(8,128)(2,1)S(1)}, bf16[3,384,128]{2,1,0:T(8,128)(2,1)S(1)}, u32[]{:S(2)}, u32[]{:S(2)}) collective-permute-start(bf16[3,384,128]{2,1,0:T(8,128)(2,1)S(1)} %pad_maximum_fusion.1.field_ref.near_grad_ref.grad_ref), channel_id=1, source_target_pairs={{0,1},{2,3},{4,5},{6,7},{8,9},{10,11},{12,13},{14,15},{1,0},{3,2},... | collective-permute-start | bytes 884744 | tf_op jit(solution)/shard_map/ppermute | solution.py:525
  74.2 9.0 %collective-permute-start.11 = (bf16[3,384,128]{2,1,0:T(8,128)(2,1)S(1)}, bf16[3,384,128]{2,1,0:T(8,128)(2,1)S(1)}, u32[]{:S(2)}, u32[]{:S(2)}) collective-permute-start(bf16[3,384,128]{2,1,0:T(8,128)(2,1)S(1)} %pad_maximum_fusion.1.field_ref.near_grad_ref.grad_ref), channel_id=1, source_target_pairs={{1,2},{3,4},{5,6},{7,8},{9,10},{11,12},{13,14},{15,0},{2,1},{4,3},... | collective-permute-start | bytes 884744 | tf_op jit(solution)/shard_map/ppermute | solution.py:525
  88.4 6.6 %collective-permute-start.13 = (bf16[64,384]{1,0:T(8,128)(2,1)S(1)}, bf16[64,384]{1,0:T(8,128)(2,1)S(1)}, u32[]{:S(2)}, u32[]{:S(2)}) collective-permute-start(bf16[64,384]{1,0:T(8,128)(2,1)S(1)} %first_outer.1), channel_id=1, source_target_pairs={{16,32},{48,64},{80,96},{112,128},{144,160},{176,192},{208,224},{2... | collective-permute-start | bytes 147464 | tf_op jit(solution)/shard_map/ppermute | solution.py:525
  90.6 4.4 %collective-permute-start.12 = (bf16[64,384]{1,0:T(8,128)(2,1)S(1)}, bf16[64,384]{1,0:T(8,128)(2,1)S(1)}, u32[]{:S(2)}, u32[]{:S(2)}) collective-permute-start(bf16[64,384]{1,0:T(8,128)(2,1)S(1)} %first_outer.1), channel_id=1, source_target_pairs={{0,16},{32,48},{64,80},{96,112},{128,144},{160,176},{192,208},{224... | collective-permute-start | bytes 147464 | tf_op jit(solution)/shard_map/ppermute | solution.py:525
  95.1 10.5 %collective-permute-start.15 = (bf16[3,64,384]{2,1,0:T(8,128)(2,1)S(1)}, bf16[3,64,384]{2,1,0:T(8,128)(2,1)S(1)}, u32[]{:S(2)}, u32[]{:S(2)}) collective-permute-start(bf16[3,64,384]{2,1,0:T(8,128)(2,1)S(1)} %pad_maximum_fusion.2.projected_ref.own_projected_ref), channel_id=1, source_target_pairs={{0,1},{2,3},{4,5},{6,7},{8,9},{10,11},{12,13},{14,15},{1,0},{3,2},... | collective-permute-start | bytes 442376 | tf_op jit(solution)/shard_map/ppermute | solution.py:525
  102.5 5.8 %copy-start.2 = (f32[9,1,128]{2,1,0:T(1,128)S(1)}, f32[9,1,128]{2,1,0:T(1,128)}, u32[]{:S(2)}) copy-start(f32[9,1,128]{2,1,0:T(1,128)} %get-tuple-element.47.mixed_ref) | copy-start | bytes 13828
  102.5 5.8 %copy-start.3 = (f32[3,1,128]{2,1,0:T(1,128)S(1)}, f32[3,1,128]{2,1,0:T(1,128)}, u32[]{:S(2)}) copy-start(f32[3,1,128]{2,1,0:T(1,128)} %get-tuple-element.48.mass_ref) | copy-start | bytes 4612
  102.5 5.8 %collective-permute-start.14 = (bf16[3,64,384]{2,1,0:T(8,128)(2,1)S(1)}, bf16[3,64,384]{2,1,0:T(8,128)(2,1)S(1)}, u32[]{:S(2)}, u32[]{:S(2)}) collective-permute-start(bf16[3,64,384]{2,1,0:T(8,128)(2,1)S(1)} %pad_maximum_fusion.2.projected_ref.own_projected_ref), channel_id=1, source_target_pairs={{1,2},{3,4},{5,6},{7,8},{9,10},{11,12},{13,14},{15,0},{2,1},{4,3},... | collective-permute-start | bytes 442376 | tf_op jit(solution)/shard_map/ppermute | solution.py:525
